TPU v7x, 32 devices: a whole 2x2x4 slice. The times are simulated.
32 devices in a mesh: rows: 8 (over z, y), cols: 4 (over x, core).
Axes of the slice: x: 2, y: 2, z: 4, core: 2. Of those that a mesh axis runs over, the one named last changes fastest.
Arguments:
- feats_t: bfloat16 [128, 16384], P('cols', 'rows'), may hold values from -6 to 6
- adj_index: int32 [128, 16], replicated, may hold values from 0 to 127, as said below
- adj_weight: bfloat16 [128, 16, 128, 128], P('rows'), as said below
- weight: bfloat16 [128, 256], replicated, may hold values from -0.5 to 0.5
- cotangent_t: bfloat16 [256, 16384], P('cols', 'rows'), may hold values from -6 to 6
Outputs:
- output_t: bfloat16 [256, 16384], P('cols', 'rows')
- weight_grad: float32 [128, 256], P('cols')
- feat_grad: float32 [128, 16384], P('cols', 'rows')
Inputs may be any that keep to these rules, and one draw needn't show every extreme that they name: `adj_index`: slot 0 of row block i names block i itself. Blocks are grouped 16 to a device in order. Slot 1 names a block of the next device (device index plus one, cyclically). The row blocks of one device name at most 4 distinct blocks of any other device, and exactly 4 of the next one. A block may stand in several slots of one row block. `adj_weight`: Nonnegative; about one entry in eight is nonzero.
All inputs are finite; a program needn't handle non-finite values.
Results may differ from a plain program's by a relative error of at most 0.0054.
Values may be sent and summed in bfloat16 or wider, within the bound.
No kernel may reach another device: no remote copies, remote signals or barrier semaphores. Data moves between devices by JAX's collectives and lax.ppermute only.
A program may use at most 128 MiB of HBM per device.

v0:
```python
import functools
import math

import jax
import jax.numpy as jnp
from jax import lax
from jax.experimental import pallas as pl
from jax.experimental.pallas import tpu as pltpu
from jax.sharding import PartitionSpec as P

CAP = 4
LANES = 128
F32, BF16, I32 = jnp.float32, jnp.bfloat16, jnp.int32
VMEM = pl.BlockSpec(memory_space=pltpu.VMEM)
SMEM = pl.BlockSpec(memory_space=pltpu.SMEM)
HBM = pl.BlockSpec(memory_space=pltpu.HBM)
MIB = 1 << 20


def masks_of(rows_n):
    return list(range(rows_n - 1, 0, -2)), list(range(rows_n - 2, -1, -2))


def call(kernel, in_specs, out_shape, args, scratch=(), flops=10**6, mib=8):
    outs = out_shape if isinstance(out_shape, list) else [out_shape]
    nbytes = sum(a.size * a.dtype.itemsize for a in args)
    return pl.pallas_call(
        kernel,
        out_shape=[pltpu.VMEM(s, d) for s, d in outs]
        if isinstance(out_shape, list)
        else pltpu.VMEM(*out_shape),
        in_specs=in_specs,
        out_specs=[VMEM] * len(outs) if isinstance(out_shape, list) else VMEM,
        scratch_shapes=list(scratch),
        compiler_params=pltpu.CompilerParams(vmem_limit_bytes=mib * MIB),
        cost_estimate=pl.CostEstimate(flops=flops, bytes_accessed=nbytes, transcendentals=0),
    )(*args)


def iota(shape, dim):
    return lax.broadcasted_iota(I32, shape, dim)


def position():
    col = lax.axis_index("cols")
    return lax.axis_index("rows"), lax.rem(col, 2), col // 2


def rows_at(start, size):
    return pl.ds(pl.multiple_of(start * size, size), size)


def choose_kernel(blk, adj_ref, feats, sel, copied, sem):
    copy = pltpu.make_async_copy(feats, copied, sem)
    copy.start()
    slots_n, ids_n = adj_ref.shape
    r, _, _ = position()
    adj = adj_ref[...]
    mine = r * blk + iota((blk, ids_n), 0)
    hits = jnp.zeros((blk, ids_n), F32)
    for k in range(slots_n):
        hits += (adj[k : k + 1, :] == mine).astype(F32)
    group = (iota((ids_n, LANES), 0) // blk == iota((ids_n, LANES), 1)).astype(BF16)
    wants = jnp.dot(hits.astype(BF16), group, preferred_element_type=F32) > 0.5
    below = (iota((blk, blk), 1) < iota((blk, blk), 0)).astype(BF16)
    order = jnp.dot(below, wants.astype(BF16), preferred_element_type=F32)
    number = iota((blk, LANES), 0).astype(F32)
    for o in range(CAP):
        pick = jnp.where(wants & (jnp.abs(order - o) < 0.5), number, 0.0)
        sel[o : o + 1, :] = jnp.sum(pick, axis=0, keepdims=True).astype(I32)
    copy.wait()


def slot_kernel(rows_n, blk, adj_ref, out_ref):
    slots_n, ids_n = adj_ref.shape
    r, c, _ = position()
    start = pl.multiple_of((r * blk) // LANES * LANES, LANES)
    near = adj_ref[:, pl.ds(start, LANES)]
    block = iota((ids_n, LANES), 0)
    seen = jnp.zeros((ids_n, LANES), F32)
    for k in range(slots_n):
        seen += (near[k : k + 1, :] == block).astype(F32)
    own = ((iota((LANES, LANES), 0) + start) // blk == r).astype(BF16)
    needed = jnp.dot(seen.astype(BF16), own, preferred_element_type=F32) > 0.5
    a, b = iota((ids_n, ids_n), 0), iota((ids_n, ids_n), 1)
    earlier = ((b < a) & (a // blk == b // blk)).astype(BF16)
    place = jnp.dot(earlier, needed.astype(BF16), preferred_element_type=F32).astype(I32)
    m = (block // blk) ^ r
    step = (rows_n - 1 - m) // 2
    other = jnp.where((m & 1) + c == 1, 0, rows_n // 2 * CAP)
    slot = jnp.where(m == 0, block % blk, blk + other + step * CAP + place).astype(F32)
    for k in range(slots_n):
        found = jnp.where(near[k : k + 1, :] == block, slot, 0.0)
        out_ref[k : k + 1, :] = jnp.sum(found, axis=0, keepdims=True).astype(I32)


def mask_at(masks, k, c):
    return jnp.where(c == 0, masks[0][k], masks[1][k])


def pack_kernel(masks, blk, sel, mine, mate, own, *sends):
    r, c, _ = position()
    f = mine.shape[0]
    tile = own.shape[2]
    top, low = rows_at(c, f), rows_at(1 - c, f)
    for k in range(len(masks[0])):
        d = r ^ mask_at(masks, k, c)
        for o in range(CAP):
            at = rows_at(sel[o, d], tile)
            sends[k][o, top, :] = mine[:, at]
            sends[k][o, low, :] = mate[:, at]
    for b in range(blk):
        own[b, top, :] = mine[:, b * tile : (b + 1) * tile]
        own[b, low, :] = mate[:, b * tile : (b + 1) * tile]


def fetch_kernel(a_hbm, cot, a_half, c0, c1, c2, c3, sems):
    _, c, x = position()
    n = a_half.shape[0]
    width = c0.shape[1]
    copies = []
    for q, piece in enumerate((c1, c2, c3, c0)):
        q = (q + 1) % 4
        at = rows_at((c ^ (q & 1)) * 2 + (x ^ (q >> 1)), width)
        copies.append(pltpu.make_async_copy(cot.at[:, at], piece, sems.at[q]))
    for i in range(n):
        copies.append(pltpu.make_async_copy(a_hbm.at[c * n + i], a_half.at[i], sems.at[4 + i]))
    for copy in copies:
        copy.start()
    for copy in copies:
        copy.wait()


def gather_kernel(side_of, blk, slot, a_half, own, *rest):
    recvs, out, table = rest[:-2], rest[-2], rest[-1]
    r, c, x = position()
    table[:blk] = own[...]
    for k, recv in enumerate(recvs):
        table[blk + k * CAP : blk + (k + 1) * CAP] = recv[...]
    n, slots_n, tile, _ = a_half.shape
    first = side_of(x) * (n // 2)
    lane = lax.rem(r * 2 * n, LANES) + c * n + first
    for t in range(n // 2):
        acc = None
        for k in range(0, slots_n, 2):
            left = [table[slot[k + h, lane + t]] for h in range(2)]
            right = [a_half[first + t, k + h] for h in range(2)]
            part = lax.dot_general(
                jnp.concatenate(left, axis=1),
                jnp.concatenate(right, axis=1),
                (((1,), (1,)), ((), ())),
                preferred_element_type=F32,
            )
            acc = part if acc is None else acc + part
        out[:, t * tile : (t + 1) * tile] = acc.astype(BF16)


def dense_kernel(keep, came, w_ref, c0, c1, c2, c3, *rest):
    outs, (g_send, g_keep), wgs = rest[:4], rest[4:6], rest[6:10]
    agg, cot, out_s, grad_s, wg_s = rest[10:]
    _, c, x = position()
    fx = keep.shape[0]
    u = c0.shape[0]
    col = 2 * x + c
    agg[rows_at(x, fx), :] = keep[...]
    agg[rows_at(1 - x, fx), :] = came[...]
    for q, piece in enumerate((c0, c1, c2, c3)):
        cot[rows_at(col ^ q, u), :] = piece[...]
    w = w_ref[...]
    act = agg[...]
    pre_act = lax.dot_general(w, act, (((0,), (0,)), ((), ())), preferred_element_type=F32)
    sigm = jax.nn.sigmoid(pre_act)
    out_s[...] = (pre_act * sigm).astype(BF16)
    pre = (cot[...].astype(F32) * sigm * (1.0 + pre_act * (1.0 - sigm))).astype(BF16)
    grad_s[...] = jnp.dot(w, pre, preferred_element_type=F32).astype(BF16)
    wg_s[...] = lax.dot_general(act, pre, (((1,), (1,)), ((), ())), preferred_element_type=F32)
    g_keep[...] = grad_s[rows_at(x, fx), :]
    g_send[...] = grad_s[rows_at(1 - x, fx), :]
    f = wgs[0].shape[0]
    for q in range(4):
        outs[q][...] = out_s[rows_at(col ^ q, u), :]
        wgs[q][...] = wg_s[rows_at(col ^ q, f), :]


def spread(side_of, slot, a_half, g_ref, acc):
    r, c, x = position()
    n, slots_n, tile, _ = a_half.shape
    first = side_of(x) * (n // 2)
    lane = lax.rem(r * 2 * n, LANES) + c * n + first
    for t in range(n // 2):
        g = g_ref[:, t * tile : (t + 1) * tile]
        for k in range(0, slots_n, 2):
            right = jnp.concatenate([a_half[first + t, k], a_half[first + t, k + 1]], axis=1)
            part = jnp.dot(g, right, preferred_element_type=F32)
            acc[slot[k, lane + t]] += part[:, :tile]
            acc[slot[k + 1, lane + t]] += part[:, tile:]


def spread_first_kernel(side_of, slot, a_half, g_ref, acc):
    acc[...] = jnp.zeros_like(acc)
    spread(side_of, slot, a_half, g_ref, acc)


def spread_last_kernel(side_of, steps, blk, slot, a_half, g_ref, before, own, stay, *rest):
    sends, acc = rest[:steps], rest[steps]
    acc[...] = before[...]
    spread(side_of, slot, a_half, g_ref, acc)
    tile = g_ref.shape[1] // (a_half.shape[0] // 2)
    for k in range(steps):
        at = blk + (steps + k) * CAP
        sends[k][...] = acc[at : at + CAP].astype(BF16)
    for b in range(blk):
        own[:, b * tile : (b + 1) * tile] = acc[b]
    stay[...] = acc[blk : blk + steps * CAP]


def collect_kernel(masks, sel, own, *rest):
    steps = len(masks[0])
    recvs, keep, send, acc = rest[:steps], rest[steps], rest[steps + 1], rest[steps + 2]
    r, c, _ = position()
    tile = recvs[0].shape[2]
    f = keep.shape[0]
    acc[...] = own[...]

    def add(k):
        d = r ^ mask_at(masks, k, c)
        for o in range(CAP):
            acc[:, rows_at(sel[o, d], tile)] += recvs[k][o].astype(F32)

    for k in range(steps - 1):
        add(k)

    @pl.when(c == 0)
    def _():
        add(steps - 1)

    keep[...] = acc[rows_at(c, f), :]
    send[...] = acc[rows_at(1 - c, f), :]


def place_kernel(p0, p1, p2, p3, out):
    _, c, x = position()
    width = p0.shape[1]
    for q, piece in enumerate((p0, p1, p2, p3)):
        out[:, rows_at((c ^ (q & 1)) * 2 + (x ^ (q >> 1)), width)] = piece[...]


def layer(feats_t, adj_index, adj_weight, weight, cotangent_t):
    f, nodes = feats_t.shape
    blk, slots_n, tile, _ = adj_weight.shape
    units_loc = cotangent_t.shape[0]
    f_in, units = weight.shape
    rows_n, cols_n = lax.axis_size("rows"), lax.axis_size("cols")
    assert cols_n == 4 and rows_n & (rows_n - 1) == 0 and blk % 4 == 0
    masks = masks_of(rows_n)
    steps = len(masks[0])
    table_n = blk + 2 * steps * CAP
    fx = 2 * f
    quarter = nodes // 4
    half = blk // 2
    big = min(48, 8 + rows_n)

    def mate(v, q):
        return lax.ppermute(v, "cols", [(i, i ^ q) for i in range(cols_n)])

    def over_rows(v, k):
        pairs = []
        for i in range(rows_n):
            for j in range(cols_n):
                m = masks[j % 2][k]
                if m:
                    pairs.append((i * cols_n + j, (i ^ m) * cols_n + j))
        return lax.ppermute(v, ("rows", "cols"), pairs)

    adj_t = adj_index.T
    in_hbm = functools.partial(pltpu.with_memory_space_constraint, memory_space=pltpu.HBM)
    feats_mate = mate(feats_t, 1)
    sel, feats = call(
        functools.partial(choose_kernel, blk), [VMEM, HBM],
        [((8, LANES), I32), ((f, nodes), BF16)], [adj_t, in_hbm(feats_t)],
        [pltpu.SemaphoreType.DMA], mib=big,
    )
    part = ((CAP, fx, tile), BF16)
    piece = ((units_loc, quarter), BF16)
    own_t, *sends = call(
        functools.partial(pack_kernel, masks, blk), [SMEM, VMEM, VMEM],
        [((blk, fx, tile), BF16)] + [part] * steps, [sel, feats, feats_mate], mib=big,
    )
    got = [over_rows(s, k) for k, s in enumerate(sends)]
    a_half, *cots = call(
        fetch_kernel, [HBM, HBM],
        [((half, slots_n, tile, tile), BF16)] + [piece] * 4,
        [in_hbm(adj_weight), in_hbm(cotangent_t)],
        [pltpu.SemaphoreType.DMA((4 + half,))],
    )
    slot = call(
        functools.partial(slot_kernel, rows_n, blk), [VMEM],
        ((slots_n, LANES), I32), [adj_t], mib=big,
    )
    cots = [cots[0]] + [mate(cots[q], q) for q in (1, 2, 3)]
    got_mate = [mate(g, 1) for g in got]

    def far(x):
        return 1 - x

    def near(x):
        return x

    a_flops = half * slots_n * fx * tile * tile

    def gather(side_of):
        args = [slot, a_half, own_t, *got, *got_mate]
        return call(
            functools.partial(gather_kernel, side_of, blk), [SMEM] + [VMEM] * (len(args) - 1),
            ((fx, quarter), BF16), args, [pltpu.VMEM((table_n, fx, tile), BF16)], a_flops,
            big,
        )

    agg_far = gather(far)
    agg_came = mate(agg_far, 2)
    agg_near = gather(near)

    half_g = ((fx, quarter), BF16)
    wg_part = ((f, units), F32)
    args = [agg_near, agg_came, weight, *cots]
    *outs, g_send, g_keep, w0, w1, w2, w3 = call(
        dense_kernel, [VMEM] * len(args),
        [piece] * 4 + [half_g] * 2 + [wg_part] * 4, args,
        [
            pltpu.VMEM((f_in, quarter), BF16),
            pltpu.VMEM((units, quarter), BF16),
            pltpu.VMEM((units, quarter), BF16),
            pltpu.VMEM((f_in, quarter), BF16),
            pltpu.VMEM((f_in, units), F32),
        ],
        6 * f_in * units * quarter, 12,
    )
    g_came = mate(g_send, 2)
    wg = w0 + mate(w1, 1) + mate(w2, 2) + mate(w3, 3)
    bit = 0
    while 1 << bit < rows_n:
        wg = wg + lax.ppermute(wg, "rows", [(i, i ^ (1 << bit)) for i in range(rows_n)])
        bit += 1
    weight_grad = wg * (1.0 / math.sqrt(nodes * rows_n))

    acc = call(
        functools.partial(spread_first_kernel, near), [SMEM, VMEM, VMEM],
        ((table_n, fx, tile), F32), [slot, a_half, g_keep], [], a_flops, big,
    )
    own_acc, stay, *grads = call(
        functools.partial(spread_last_kernel, far, steps, blk),
        [SMEM, VMEM, VMEM, VMEM],
        [((fx, nodes), F32), ((steps * CAP, fx, tile), F32)] + [part] * steps,
        [slot, a_half, g_came, acc], [pltpu.VMEM((table_n, fx, tile), F32)], a_flops, big + 8,
    )
    back = []
    for k in range(steps):
        came = mate(grads[k], 1)
        total = stay[k * CAP : (k + 1) * CAP] + came.astype(F32)
        back.append(over_rows(total.astype(BF16), k))
    keep, send = call(
        functools.partial(collect_kernel, masks), [SMEM, VMEM] + [VMEM] * steps,
        [((f, nodes), F32)] * 2, [sel, own_acc, *back], [pltpu.VMEM((fx, nodes), F32)], mib=big,
    )
    feat_grad = keep + mate(send, 1)

    outs = [outs[0]] + [mate(outs[q], q) for q in (1, 2, 3)]
    output_t = pl.pallas_call(
        place_kernel,
        out_shape=jax.ShapeDtypeStruct((units_loc, nodes), BF16),
        in_specs=[VMEM] * 4,
        out_specs=VMEM,
        compiler_params=pltpu.CompilerParams(vmem_limit_bytes=4 * MIB),
        name="place",
    )(*outs)
    return output_t, weight_grad, feat_grad


def solution(mesh):
    return jax.shard_map(
        layer,
        mesh=mesh,
        in_specs=(P("cols", "rows"), P(), P("rows", None, None, None), P(), P("cols", "rows")),
        out_specs=(P("cols", "rows"), P("cols", None), P("cols", "rows")),
        check_vma=False,
    )
```

profile of v0, /device:TPU:0, one launch (start us, length us, event | category | flops | bytes accessed | tf_op | source)
XLA Modules:
  0.0 62.7 jit_solution(9311889078337179584)
XLA Ops:
  0.6 0.6 collective-permute-start
  1.2 0.7 %copy-done.1 = s32[128,16]{0,1:T(8,128)S(1)} copy-done((s32[128,16]{0,1:T(8,128)S(1)}, s32[128,16]{0,1:T(8,128)}, u32[]{:S(2)}) %copy-start.1) | copy-done | bytes 8216
  1.9 0.9 %shard_map.78 = (s32[8,128]{1,0:T(8,128)S(1)}, bf16[32,2048]{1,0:T(8,128)(2,1)S(1)}) custom-call(s32[16,128]{1,0:T(8,128)S(1)} %bitcast.1, bf16[32,2048]{1,0:T(8,128)(2,1)} %feats.1), custom_call_target="tpu_custom_call" | custom-call | flops 1000000 | bytes 139264 | tf_op jit(solution)/shard_map/pallas_call | solution.py:27
  2.8 0.0 collective-permute-done.mate
  2.8 0.7 %shard_map.79 = (bf16[16,64,128]{2,1,0:T(8,128)(2,1)S(1)}, bf16[4,64,128]{2,1,0:T(8,128)(2,1)S(1)}, bf16[4,64,128]{2,1,0:T(8,128)(2,1)S(1)}, bf16[4,64,128]{2,1,0:T(8,128)(2,1)S(1)}, bf16[4,64,128]{2,1,0:T(8,128)(2,1)S(1)}) custom-call(s32[8,128]{1,0:T(8,128)S(1)} %get-tuple-element.34.sel, bf16[32,2048]{1,0:T(8,128)(2,1)S(1)} %get-tuple-element.35.mine, ...), custom_call_target="tpu_custom_call" | custom-call | flops 1000000 | bytes 266240 | tf_op jit(solution)/shard_map/pallas_call | solution.py:27
  3.5 5.6 %collective-permute-start.1 = (bf16[4,64,128]{2,1,0:T(8,128)(2,1)S(1)}, bf16[4,64,128]{2,1,0:T(8,128)(2,1)S(1)}, u32[]{:S(2)}, u32[]{:S(2)}) collective-permute-start(bf16[4,64,128]{2,1,0:T(8,128)(2,1)S(1)} %get-tuple-element.37), channel_id=1, source_target_pairs={{0,28},{1,25},{2,30},{3,27},{4,24},{5,29},{6,26},{7,31},{8,20},{9,... | collective-permute-start | bytes 196616 | tf_op jit(solution)/shard_map/ppermute | solution.py:273
  9.2 0.0 collective-permute-start.2
  9.2 1.7 %collective-permute-start.3 = (bf16[4,64,128]{2,1,0:T(8,128)(2,1)S(1)}, bf16[4,64,128]{2,1,0:T(8,128)(2,1)S(1)}, u32[]{:S(2)}, u32[]{:S(2)}) collective-permute-start(bf16[4,64,128]{2,1,0:T(8,128)(2,1)S(1)} %get-tuple-element.39), channel_id=1, source_target_pairs={{0,12},{1,9},{2,14},{3,11},{4,8},{5,13},{6,10},{7,15},{8,4},{9,1},... | collective-permute-start | bytes 196616 | tf_op jit(solution)/shard_map/ppermute | solution.py:273
  10.9 2.4 %collective-permute-start.4 = (bf16[4,64,128]{2,1,0:T(8,128)(2,1)S(1)}, bf16[4,64,128]{2,1,0:T(8,128)(2,1)S(1)}, u32[]{:S(2)}, u32[]{:S(2)}) collective-permute-start(bf16[4,64,128]{2,1,0:T(8,128)(2,1)S(1)} %get-tuple-element.40), channel_id=1, source_target_pairs={{0,4},{2,6},{4,0},{6,2},{8,12},{10,14},{12,8},{14,10},{16,20},{18,... | collective-permute-start | bytes 196616 | tf_op jit(solution)/shard_map/ppermute | solution.py:273
  13.3 0.0 collective-permute-done.1.rest_0_
  13.3 0.1 collective-permute-start.5
  13.4 1.9 %collective-permute-done.2.rest_1_ = bf16[4,64,128]{2,1,0:T(8,128)(2,1)S(1)} collective-permute-done((bf16[4,64,128]{2,1,0:T(8,128)(2,1)S(1)}, bf16[4,64,128]{2,1,0:T(8,128)(2,1)S(1)}, u32[]{:S(2)}, u32[]{:S(2)}) %collective-permute-start.2) | collective-permute-done | bytes 65568 | tf_op jit(solution)/shard_map/ppermute | solution.py:273
  15.3 0.0 collective-permute-start.6
  15.3 0.0 collective-permute-done.3.rest_2_
  15.3 0.5 collective-permute-start.7
  15.8 1.3 %collective-permute-done.4.rest_3_ = bf16[4,64,128]{2,1,0:T(8,128)(2,1)S(1)} collective-permute-done((bf16[4,64,128]{2,1,0:T(8,128)(2,1)S(1)}, bf16[4,64,128]{2,1,0:T(8,128)(2,1)S(1)}, u32[]{:S(2)}, u32[]{:S(2)}) %collective-permute-start.4) | collective-permute-done | bytes 65568 | tf_op jit(solution)/shard_map/ppermute | solution.py:273
  17.1 0.0 collective-permute-start.8
  17.1 2.4 %shard_map.77 = (bf16[8,16,128,128]{3,2,1,0:T(8,128)(2,1)S(1)}, bf16[64,512]{1,0:T(8,128)(2,1)S(1)}, bf16[64,512]{1,0:T(8,128)(2,1)S(1)}, bf16[64,512]{1,0:T(8,128)(2,1)S(1)}, bf16[64,512]{1,0:T(8,128)(2,1)S(1)}) custom-call(bf16[16,16,128,128]{3,2,1,0:T(8,128)(2,1)} %a_hbm.1, bf16[64,2048]{1,0:T(8,128)(2,1)} %cot.1), custom_call_target="tpu_custom_call" | custom-call | flops 1000000 | bytes 8650752 | tf_op jit(solution)/shard_map/pallas_call | solution.py:27
  19.5 0.6 collective-permute-start.10
  20.1 0.6 shard_map.76.slot
  20.7 1.6 %collective-permute-start.11 = (bf16[64,512]{1,0:T(8,128)(2,1)S(1)}, bf16[64,512]{1,0:T(8,128)(2,1)S(1)}, u32[]{:S(2)}, u32[]{:S(2)}) collective-permute-start(bf16[64,512]{1,0:T(8,128)(2,1)S(1)} %get-tuple-element.43), channel_id=1, source_target_pairs={{0,2},{1,3},{2,0},{3,1},{4,6},{5,7},{6,4},{7,5},{8,10},{9,11},{10,... | collective-permute-start | bytes 196616 | tf_op jit(solution)/shard_map/ppermute | solution.py:264
  22.3 0.0 collective-permute-done.6.rest_5_
  22.3 0.0 collective-permute-start.12
  22.3 0.0 collective-permute-done.7.rest_6_
  22.3 0.0 copy-start
  22.3 1.5 %shard_map.81 = bf16[64,512]{1,0:T(8,128)(2,1)S(1)} custom-call(s32[16,128]{1,0:T(8,128)S(1)} %shard_map.76.slot, bf16[8,16,128,128]{3,2,1,0:T(8,128)(2,1)S(1)} %get-tuple-element.33.a_half, bf16[16,64,128]{2,1,0:T(8,128)(2,1)S(1)} %get-tuple-element.36.own, bf16[4,64,128]{2,1,0:T(8,128)(2,1)S(1)} %collective-permute-done.1.rest_0_, ...), custom_call_target="tpu_custom_call" | custom-call | flops 134217728 | bytes 4988928 | tf_op jit(solution)/shard_map/pallas_call | solution.py:27
  23.8 1.4 %collective-permute-start.9 = (bf16[64,512]{1,0:T(8,128)(2,1)S(1)}, bf16[64,512]{1,0:T(8,128)(2,1)S(1)}, u32[]{:S(2)}, u32[]{:S(2)}) collective-permute-start(bf16[64,512]{1,0:T(8,128)(2,1)S(1)} %shard_map.81), channel_id=1, source_target_pairs={{0,2},{1,3},{2,0},{3,1},{4,6},{5,7},{6,4},{7,5},{8,10},{9,11},{10,... | collective-permute-start | bytes 196616 | tf_op jit(solution)/shard_map/ppermute | solution.py:264
  25.3 1.5 %shard_map.80.keep = bf16[64,512]{1,0:T(8,128)(2,1)S(1)} custom-call(s32[16,128]{1,0:T(8,128)S(1)} %shard_map.76.slot, bf16[8,16,128,128]{3,2,1,0:T(8,128)(2,1)S(1)} %get-tuple-element.33.a_half, bf16[16,64,128]{2,1,0:T(8,128)(2,1)S(1)} %get-tuple-element.36.own, bf16[4,64,128]{2,1,0:T(8,128)(2,1)S(1)} %collective-permute-done.1.rest_0_, ...), custom_call_target="tpu_custom_call" | custom-call | flops 134217728 | bytes 4988928 | tf_op jit(solution)/shard_map/pallas_call | solution.py:27
  26.8 0.0 collective-permute-done.10.c1
  26.8 0.0 collective-permute-done.12.c3
  26.8 1.7 %collective-permute-done.9.came = bf16[64,512]{1,0:T(8,128)(2,1)S(1)} collective-permute-done((bf16[64,512]{1,0:T(8,128)(2,1)S(1)}, bf16[64,512]{1,0:T(8,128)(2,1)S(1)}, u32[]{:S(2)}, u32[]{:S(2)}) %collective-permute-start.9) | collective-permute-done | bytes 65568 | tf_op jit(solution)/shard_map/ppermute | solution.py:264
  28.5 0.6 shard_map.82
  29.2 1.6 %collective-permute-start.22 = (bf16[64,512]{1,0:T(8,128)(2,1)S(1)}, bf16[64,512]{1,0:T(8,128)(2,1)S(1)}, u32[]{:S(2)}, u32[]{:S(2)}) collective-permute-start(bf16[64,512]{1,0:T(8,128)(2,1)S(1)} %get-tuple-element.53), channel_id=1, source_target_pairs={{0,2},{1,3},{2,0},{3,1},{4,6},{5,7},{6,4},{7,5},{8,10},{9,11},{10,... | collective-permute-start | bytes 196616 | tf_op jit(solution)/shard_map/ppermute | solution.py:264
  30.7 1.3 %shard_map.83.before = f32[48,64,128]{2,1,0:T(8,128)S(1)} custom-call(s32[16,128]{1,0:T(8,128)S(1)} %shard_map.76.slot, bf16[8,16,128,128]{3,2,1,0:T(8,128)(2,1)S(1)} %get-tuple-element.33.a_half, bf16[64,512]{1,0:T(8,128)(2,1)S(1)} %get-tuple-element.54.g_ref), custom_call_target="tpu_custom_call" | custom-call | flops 134217728 | bytes 4268032 | tf_op jit(solution)/shard_map/pallas_call | solution.py:27
  32.0 1.5 %collective-permute-done.22.g_ref = bf16[64,512]{1,0:T(8,128)(2,1)S(1)} collective-permute-done((bf16[64,512]{1,0:T(8,128)(2,1)S(1)}, bf16[64,512]{1,0:T(8,128)(2,1)S(1)}, u32[]{:S(2)}, u32[]{:S(2)}) %collective-permute-start.22) | collective-permute-done | bytes 65568 | tf_op jit(solution)/shard_map/ppermute | solution.py:264
  33.5 1.4 %shard_map.84 = (f32[64,2048]{1,0:T(8,128)S(1)}, f32[16,64,128]{2,1,0:T(8,128)S(1)}, bf16[4,64,128]{2,1,0:T(8,128)(2,1)S(1)}, bf16[4,64,128]{2,1,0:T(8,128)(2,1)...) custom-call(s32[16,128]{1,0:T(8,128)S(1)} %shard_map.76.slot, ...), custom_call_target="tpu_custom_call" | custom-call | flops 134217728 | bytes 5840896 | tf_op jit(solution)/shard_map/pallas_call | solution.py:27
  34.9 0.1 collective-permute-start.23
  35.0 0.5 collective-permute-start.25
  35.5 0.1 collective-permute-start.27
  35.6 0.4 collective-permute-start.29
  36.0 0.1 collective-permute-start.16
  36.1 0.2 collective-permute-done.23
  36.2 1.5 %collective-permute-start.17 = (f32[32,256]{1,0:T(8,128)S(1)}, f32[32,256]{1,0:T(8,128)S(1)}, u32[]{:S(2)}, u32[]{:S(2)}) collective-permute-start(f32[32,256]{1,0:T(8,128)S(1)} %get-tuple-element.51), channel_id=1, source_target_pairs={{0,2},{1,3},{2,0},{3,1},{4,6},{5,7},{6,4},{7,5},{8,10},{9,11},{10,... | collective-permute-start | bytes 98312 | tf_op jit(solution)/shard_map/ppermute | solution.py:264
  37.7 0.0 collective-permute-done.25
  37.7 0.1 collective-permute-start.18
  37.9 0.0 collective-permute-done.27
  37.9 0.1 add_convert_fusion
  37.9 2.4 %collective-permute-start.30 = (bf16[4,64,128]{2,1,0:T(8,128)(2,1)S(1)}, bf16[4,64,128]{2,1,0:T(8,128)(2,1)S(1)}, u32[]{:S(2)}, u32[]{:S(2)}) collective-permute-start(bf16[4,64,128]{2,1,0:T(8,128)(2,1)S(1)} %get-tuple-element.63), channel_id=1, source_target_pairs={{0,4},{2,6},{4,0},{6,2},{8,12},{10,14},{12,8},{14,10},{16,20},{18,... | collective-permute-start | bytes 196616 | tf_op jit(solution)/shard_map/ppermute | solution.py:273
  40.3 1.7 %collective-permute-start.28 = (bf16[4,64,128]{2,1,0:T(8,128)(2,1)S(1)}, bf16[4,64,128]{2,1,0:T(8,128)(2,1)S(1)}, u32[]{:S(2)}, u32[]{:S(2)}) collective-permute-start(bf16[4,64,128]{2,1,0:T(8,128)(2,1)S(1)} %get-tuple-element.64), channel_id=1, source_target_pairs={{0,12},{1,9},{2,14},{3,11},{4,8},{5,13},{6,10},{7,15},{8,4},{9,1},... | collective-permute-start | bytes 196616 | tf_op jit(solution)/shard_map/ppermute | solution.py:273
  42.1 3.4 %collective-permute-start.26 = (bf16[4,64,128]{2,1,0:T(8,128)(2,1)S(1)}, bf16[4,64,128]{2,1,0:T(8,128)(2,1)S(1)}, u32[]{:S(2)}, u32[]{:S(2)}) collective-permute-start(bf16[4,64,128]{2,1,0:T(8,128)(2,1)S(1)} %get-tuple-element.65), channel_id=1, source_target_pairs={{0,20},{1,17},{2,22},{3,19},{4,16},{5,21},{6,18},{7,23},{8,28},{9,... | collective-permute-start | bytes 196616 | tf_op jit(solution)/shard_map/ppermute | solution.py:273
  45.5 1.2 %collective-permute-start.24 = (bf16[4,64,128]{2,1,0:T(8,128)(2,1)S(1)}, bf16[4,64,128]{2,1,0:T(8,128)(2,1)S(1)}, u32[]{:S(2)}, u32[]{:S(2)}) collective-permute-start(bf16[4,64,128]{2,1,0:T(8,128)(2,1)S(1)} %get-tuple-element.66), channel_id=1, source_target_pairs={{0,28},{1,25},{2,30},{3,27},{4,24},{5,29},{6,26},{7,31},{8,20},{9,... | collective-permute-start | bytes 196616 | tf_op jit(solution)/shard_map/ppermute | solution.py:273
  46.7 0.5 collective-permute-start.19
  47.2 3.4 %collective-permute-done.19 = f32[32,256]{1,0:T(8,128)S(1)} collective-permute-done((f32[32,256]{1,0:T(8,128)S(1)}, f32[32,256]{1,0:T(8,128)S(1)}, u32[]{:S(2)}, u32[]{:S(2)}) %collective-permute-start.19) | collective-permute-done | bytes 32800 | tf_op jit(solution)/shard_map/ppermute | solution.py:342
  50.7 1.6 %collective-permute-start.14 = (bf16[64,512]{1,0:T(8,128)(2,1)S(1)}, bf16[64,512]{1,0:T(8,128)(2,1)S(1)}, u32[]{:S(2)}, u32[]{:S(2)}) collective-permute-start(bf16[64,512]{1,0:T(8,128)(2,1)S(1)} %get-tuple-element.47), channel_id=1, source_target_pairs={{0,2},{1,3},{2,0},{3,1},{4,6},{5,7},{6,4},{7,5},{8,10},{9,11},{10,... | collective-permute-start | bytes 196616 | tf_op jit(solution)/shard_map/ppermute | solution.py:264
  52.3 0.4 collective-permute-start.15
  52.6 0.5 collective-permute-start.20
  53.1 0.8 %shard_map.85 = (f32[32,2048]{1,0:T(8,128)S(1)}, f32[32,2048]{1,0:T(8,128)S(1)}) custom-call(s32[8,128]{1,0:T(8,128)S(1)} %get-tuple-element.34.sel, f32[64,2048]{1,0:T(8,128)S(1)} %get-tuple-element.55.own, bf16[4,64,128]{2,1,0:T(8,128)(2,1)S(1)} %collective-permute-done.24.rest_0_, bf16[4,64,128]{2,1,0:T(8,128)(2,1)S(1)} %collective-permute-done.26.rest_1_, ...), custom_call_target="tpu_custom_call" | custom-call | flops 1000000 | bytes 790528 | tf_op jit(solution)/shard_map/pallas_call | solution.py:27
  53.9 0.1 collective-permute-start.31
  54.0 2.5 %collective-permute-done.20 = f32[32,256]{1,0:T(8,128)S(1)} collective-permute-done((f32[32,256]{1,0:T(8,128)S(1)}, f32[32,256]{1,0:T(8,128)S(1)}, u32[]{:S(2)}, u32[]{:S(2)}) %collective-permute-start.20) | collective-permute-done | bytes 32800 | tf_op jit(solution)/shard_map/ppermute | solution.py:342
  56.6 2.1 %collective-permute-start.21 = (f32[32,256]{1,0:T(8,128)S(1)}, f32[32,256]{1,0:T(8,128)S(1)}, u32[]{:S(2)}, u32[]{:S(2)}) collective-permute-start(f32[32,256]{1,0:T(8,128)S(1)} %add.37), channel_id=1, source_target_pairs={{0,16},{4,20},{8,24},{12,28},{16,0},{20,4},{24,8},{28,12},{1,17},{... | collective-permute-start | bytes 98312 | tf_op jit(solution)/shard_map/ppermute | solution.py:342
  58.7 0.7 %place.1 = bf16[64,2048]{1,0:T(8,128)(2,1)} custom-call(bf16[64,512]{1,0:T(8,128)(2,1)S(1)} %get-tuple-element.45.p0, bf16[64,512]{1,0:T(8,128)(2,1)S(1)} %collective-permute-done.13.p1, bf16[64,512]{1,0:T(8,128)(2,1)S(1)} %collective-permute-done.14.p2, bf16[64,512]{1,0:T(8,128)(2,1)S(1)} %collective-permute-done.15.p3), custom_call_target="tpu_custom_call" | custom-call | tf_op jit(solution)/shard_map/place/pallas_call | solution.py:368
  59.4 1.9 %collective-permute-done.21 = f32[32,256]{1,0:T(8,128)S(1)} collective-permute-done((f32[32,256]{1,0:T(8,128)S(1)}, f32[32,256]{1,0:T(8,128)S(1)}, u32[]{:S(2)}, u32[]{:S(2)}) %collective-permute-start.21) | collective-permute-done | bytes 32800 | tf_op jit(solution)/shard_map/ppermute | solution.py:342
  61.4 0.6 add_multiply_fusion
  62.0 0.7 %add.43 = f32[32,2048]{1,0:T(8,128)} add(f32[32,2048]{1,0:T(8,128)S(1)} %get-tuple-element.61, f32[32,2048]{1,0:T(8,128)S(1)} %collective-permute-done.31) | non-fusion elementwise | flops 65536 | bytes 786432 | tf_op jit(solution)/shard_map/add | solution.py:365
  (23 shorter events, 0.1 us)
Async XLA Ops:
  0.6 2.2 %collective-permute-start = (bf16[32,2048]{1,0:T(8,128)(2,1)}, bf16[32,2048]{1,0:T(8,128)(2,1)S(1)}, u32[]{:S(2)}, u32[]{:S(2)}) collective-permute-start(bf16[32,2048]{1,0:T(8,128)(2,1)} %feats.1), channel_id=1, source_target_pairs={{0,1},{1,0},{2,3},{3,2},{4,5},{5,4},{6,7},{7,6},{8,9},{9,8},{10,11... | collective-permute-start | bytes 393224 | tf_op jit(solution)/shard_map/ppermute | solution.py:264
  1.2 0.7 %copy-start.1 = (s32[128,16]{0,1:T(8,128)S(1)}, s32[128,16]{0,1:T(8,128)}, u32[]{:S(2)}) copy-start(s32[128,16]{0,1:T(8,128)} %param.6) | copy-start | bytes 24580
  3.5 9.8 %collective-permute-start.1 = (bf16[4,64,128]{2,1,0:T(8,128)(2,1)S(1)}, bf16[4,64,128]{2,1,0:T(8,128)(2,1)S(1)}, u32[]{:S(2)}, u32[]{:S(2)}) collective-permute-start(bf16[4,64,128]{2,1,0:T(8,128)(2,1)S(1)} %get-tuple-element.37), channel_id=1, source_target_pairs={{0,28},{1,25},{2,30},{3,27},{4,24},{5,29},{6,26},{7,31},{8,20},{9,... | collective-permute-start | bytes 196616 | tf_op jit(solution)/shard_map/ppermute | solution.py:273
  9.2 6.1 %collective-permute-start.2 = (bf16[4,64,128]{2,1,0:T(8,128)(2,1)S(1)}, bf16[4,64,128]{2,1,0:T(8,128)(2,1)S(1)}, u32[]{:S(2)}, u32[]{:S(2)}) collective-permute-start(bf16[4,64,128]{2,1,0:T(8,128)(2,1)S(1)} %get-tuple-element.38), channel_id=1, source_target_pairs={{0,20},{1,17},{2,22},{3,19},{4,16},{5,21},{6,18},{7,23},{8,28},{9,... | collective-permute-start | bytes 196616 | tf_op jit(solution)/shard_map/ppermute | solution.py:273
  9.2 6.1 %collective-permute-start.3 = (bf16[4,64,128]{2,1,0:T(8,128)(2,1)S(1)}, bf16[4,64,128]{2,1,0:T(8,128)(2,1)S(1)}, u32[]{:S(2)}, u32[]{:S(2)}) collective-permute-start(bf16[4,64,128]{2,1,0:T(8,128)(2,1)S(1)} %get-tuple-element.39), channel_id=1, source_target_pairs={{0,12},{1,9},{2,14},{3,11},{4,8},{5,13},{6,10},{7,15},{8,4},{9,1},... | collective-permute-start | bytes 196616 | tf_op jit(solution)/shard_map/ppermute | solution.py:273
  10.8 9.3 %copy-start.2 = (s32[128,16]{0,1:T(8,128)S(1)}, s32[128,16]{0,1:T(8,128)}, u32[]{:S(2)}) copy-start(s32[128,16]{0,1:T(8,128)} %param.6) | copy-start | bytes 24580
  10.9 6.3 %collective-permute-start.4 = (bf16[4,64,128]{2,1,0:T(8,128)(2,1)S(1)}, bf16[4,64,128]{2,1,0:T(8,128)(2,1)S(1)}, u32[]{:S(2)}, u32[]{:S(2)}) collective-permute-start(bf16[4,64,128]{2,1,0:T(8,128)(2,1)S(1)} %get-tuple-element.40), channel_id=1, source_target_pairs={{0,4},{2,6},{4,0},{6,2},{8,12},{10,14},{12,8},{14,10},{16,20},{18,... | collective-permute-start | bytes 196616 | tf_op jit(solution)/shard_map/ppermute | solution.py:273
  13.3 7.4 %collective-permute-start.5 = (bf16[4,64,128]{2,1,0:T(8,128)(2,1)S(1)}, bf16[4,64,128]{2,1,0:T(8,128)(2,1)S(1)}, u32[]{:S(2)}, u32[]{:S(2)}) collective-permute-start(bf16[4,64,128]{2,1,0:T(8,128)(2,1)S(1)} %collective-permute-done.1.rest_0_), channel_id=1, source_target_pairs={{0,1},{1,0},{2,3},{3,2},{4,5},{5,4},{6,7},{7,6},{8,9},{9,8},{10,11... | collective-permute-start | bytes 196616 | tf_op jit(solution)/shard_map/ppermute | solution.py:264
  15.3 7.0 %collective-permute-start.6 = (bf16[4,64,128]{2,1,0:T(8,128)(2,1)S(1)}, bf16[4,64,128]{2,1,0:T(8,128)(2,1)S(1)}, u32[]{:S(2)}, u32[]{:S(2)}) collective-permute-start(bf16[4,64,128]{2,1,0:T(8,128)(2,1)S(1)} %collective-permute-done.2.rest_1_), channel_id=1, source_target_pairs={{0,1},{1,0},{2,3},{3,2},{4,5},{5,4},{6,7},{7,6},{8,9},{9,8},{10,11... | collective-permute-start | bytes 196616 | tf_op jit(solution)/shard_map/ppermute | solution.py:264
  15.3 7.0 %collective-permute-start.7 = (bf16[4,64,128]{2,1,0:T(8,128)(2,1)S(1)}, bf16[4,64,128]{2,1,0:T(8,128)(2,1)S(1)}, u32[]{:S(2)}, u32[]{:S(2)}) collective-permute-start(bf16[4,64,128]{2,1,0:T(8,128)(2,1)S(1)} %collective-permute-done.3.rest_2_), channel_id=1, source_target_pairs={{0,1},{1,0},{2,3},{3,2},{4,5},{5,4},{6,7},{7,6},{8,9},{9,8},{10,11... | collective-permute-start | bytes 196616 | tf_op jit(solution)/shard_map/ppermute | solution.py:264
  17.1 5.2 %collective-permute-start.8 = (bf16[4,64,128]{2,1,0:T(8,128)(2,1)S(1)}, bf16[4,64,128]{2,1,0:T(8,128)(2,1)S(1)}, u32[]{:S(2)}, u32[]{:S(2)}) collective-permute-start(bf16[4,64,128]{2,1,0:T(8,128)(2,1)S(1)} %collective-permute-done.4.rest_3_), channel_id=1, source_target_pairs={{0,1},{1,0},{2,3},{3,2},{4,5},{5,4},{6,7},{7,6},{8,9},{9,8},{10,11... | collective-permute-start | bytes 196616 | tf_op jit(solution)/shard_map/ppermute | solution.py:264
  19.5 7.3 %collective-permute-start.10 = (bf16[64,512]{1,0:T(8,128)(2,1)S(1)}, bf16[64,512]{1,0:T(8,128)(2,1)S(1)}, u32[]{:S(2)}, u32[]{:S(2)}) collective-permute-start(bf16[64,512]{1,0:T(8,128)(2,1)S(1)} %get-tuple-element.42), channel_id=1, source_target_pairs={{0,1},{1,0},{2,3},{3,2},{4,5},{5,4},{6,7},{7,6},{8,9},{9,8},{10,11... | collective-permute-start | bytes 196616 | tf_op jit(solution)/shard_map/ppermute | solution.py:264
  20.7 6.1 %collective-permute-start.11 = (bf16[64,512]{1,0:T(8,128)(2,1)S(1)}, bf16[64,512]{1,0:T(8,128)(2,1)S(1)}, u32[]{:S(2)}, u32[]{:S(2)}) collective-permute-start(bf16[64,512]{1,0:T(8,128)(2,1)S(1)} %get-tuple-element.43), channel_id=1, source_target_pairs={{0,2},{1,3},{2,0},{3,1},{4,6},{5,7},{6,4},{7,5},{8,10},{9,11},{10,... | collective-permute-start | bytes 196616 | tf_op jit(solution)/shard_map/ppermute | solution.py:264
  22.3 4.5 %collective-permute-start.12 = (bf16[64,512]{1,0:T(8,128)(2,1)S(1)}, bf16[64,512]{1,0:T(8,128)(2,1)S(1)}, u32[]{:S(2)}, u32[]{:S(2)}) collective-permute-start(bf16[64,512]{1,0:T(8,128)(2,1)S(1)} %get-tuple-element.44), channel_id=1, source_target_pairs={{0,3},{1,2},{2,1},{3,0},{4,7},{5,6},{6,5},{7,4},{8,11},{9,10},{10,... | collective-permute-start | bytes 196616 | tf_op jit(solution)/shard_map/ppermute | solution.py:264
  22.3 6.2 %copy-start = (bf16[128,256]{1,0:T(8,128)(2,1)S(1)}, bf16[128,256]{1,0:T(8,128)(2,1)}, u32[]{:S(2)}) copy-start(bf16[128,256]{1,0:T(8,128)(2,1)} %w_ref.1) | copy-start | bytes 196612
  23.8 4.7 %collective-permute-start.9 = (bf16[64,512]{1,0:T(8,128)(2,1)S(1)}, bf16[64,512]{1,0:T(8,128)(2,1)S(1)}, u32[]{:S(2)}, u32[]{:S(2)}) collective-permute-start(bf16[64,512]{1,0:T(8,128)(2,1)S(1)} %shard_map.81), channel_id=1, source_target_pairs={{0,2},{1,3},{2,0},{3,1},{4,6},{5,7},{6,4},{7,5},{8,10},{9,11},{10,... | collective-permute-start | bytes 196616 | tf_op jit(solution)/shard_map/ppermute | solution.py:264
  29.2 4.3 %collective-permute-start.22 = (bf16[64,512]{1,0:T(8,128)(2,1)S(1)}, bf16[64,512]{1,0:T(8,128)(2,1)S(1)}, u32[]{:S(2)}, u32[]{:S(2)}) collective-permute-start(bf16[64,512]{1,0:T(8,128)(2,1)S(1)} %get-tuple-element.53), channel_id=1, source_target_pairs={{0,2},{1,3},{2,0},{3,1},{4,6},{5,7},{6,4},{7,5},{8,10},{9,11},{10,... | collective-permute-start | bytes 196616 | tf_op jit(solution)/shard_map/ppermute | solution.py:264
  34.9 1.3 %collective-permute-start.23 = (bf16[4,64,128]{2,1,0:T(8,128)(2,1)S(1)}, bf16[4,64,128]{2,1,0:T(8,128)(2,1)S(1)}, u32[]{:S(2)}, u32[]{:S(2)}) collective-permute-start(bf16[4,64,128]{2,1,0:T(8,128)(2,1)S(1)} %get-tuple-element.57), channel_id=1, source_target_pairs={{0,1},{1,0},{2,3},{3,2},{4,5},{5,4},{6,7},{7,6},{8,9},{9,8},{10,11... | collective-permute-start | bytes 196616 | tf_op jit(solution)/shard_map/ppermute | solution.py:264
  35.0 2.7 %collective-permute-start.25 = (bf16[4,64,128]{2,1,0:T(8,128)(2,1)S(1)}, bf16[4,64,128]{2,1,0:T(8,128)(2,1)S(1)}, u32[]{:S(2)}, u32[]{:S(2)}) collective-permute-start(bf16[4,64,128]{2,1,0:T(8,128)(2,1)S(1)} %get-tuple-element.58), channel_id=1, source_target_pairs={{0,1},{1,0},{2,3},{3,2},{4,5},{5,4},{6,7},{7,6},{8,9},{9,8},{10,11... | collective-permute-start | bytes 196616 | tf_op jit(solution)/shard_map/ppermute | solution.py:264
  35.5 2.4 %collective-permute-start.27 = (bf16[4,64,128]{2,1,0:T(8,128)(2,1)S(1)}, bf16[4,64,128]{2,1,0:T(8,128)(2,1)S(1)}, u32[]{:S(2)}, u32[]{:S(2)}) collective-permute-start(bf16[4,64,128]{2,1,0:T(8,128)(2,1)S(1)} %get-tuple-element.59), channel_id=1, source_target_pairs={{0,1},{1,0},{2,3},{3,2},{4,5},{5,4},{6,7},{7,6},{8,9},{9,8},{10,11... | collective-permute-start | bytes 196616 | tf_op jit(solution)/shard_map/ppermute | solution.py:264
  35.6 2.3 %collective-permute-start.29 = (bf16[4,64,128]{2,1,0:T(8,128)(2,1)S(1)}, bf16[4,64,128]{2,1,0:T(8,128)(2,1)S(1)}, u32[]{:S(2)}, u32[]{:S(2)}) collective-permute-start(bf16[4,64,128]{2,1,0:T(8,128)(2,1)S(1)} %get-tuple-element.60), channel_id=1, source_target_pairs={{0,1},{1,0},{2,3},{3,2},{4,5},{5,4},{6,7},{7,6},{8,9},{9,8},{10,11... | collective-permute-start | bytes 196616 | tf_op jit(solution)/shard_map/ppermute | solution.py:264
  36.0 6.1 %collective-permute-start.16 = (f32[32,256]{1,0:T(8,128)S(1)}, f32[32,256]{1,0:T(8,128)S(1)}, u32[]{:S(2)}, u32[]{:S(2)}) collective-permute-start(f32[32,256]{1,0:T(8,128)S(1)} %get-tuple-element.50), channel_id=1, source_target_pairs={{0,1},{1,0},{2,3},{3,2},{4,5},{5,4},{6,7},{7,6},{8,9},{9,8},{10,11... | collective-permute-start | bytes 98312 | tf_op jit(solution)/shard_map/ppermute | solution.py:264
  36.2 9.3 %collective-permute-start.17 = (f32[32,256]{1,0:T(8,128)S(1)}, f32[32,256]{1,0:T(8,128)S(1)}, u32[]{:S(2)}, u32[]{:S(2)}) collective-permute-start(f32[32,256]{1,0:T(8,128)S(1)} %get-tuple-element.51), channel_id=1, source_target_pairs={{0,2},{1,3},{2,0},{3,1},{4,6},{5,7},{6,4},{7,5},{8,10},{9,11},{10,... | collective-permute-start | bytes 98312 | tf_op jit(solution)/shard_map/ppermute | solution.py:264
  37.7 9.0 %collective-permute-start.18 = (f32[32,256]{1,0:T(8,128)S(1)}, f32[32,256]{1,0:T(8,128)S(1)}, u32[]{:S(2)}, u32[]{:S(2)}) collective-permute-start(f32[32,256]{1,0:T(8,128)S(1)} %get-tuple-element.52), channel_id=1, source_target_pairs={{0,3},{1,2},{2,1},{3,0},{4,7},{5,6},{6,5},{7,4},{8,11},{9,10},{10,... | collective-permute-start | bytes 98312 | tf_op jit(solution)/shard_map/ppermute | solution.py:264
  37.9 12.8 %collective-permute-start.30 = (bf16[4,64,128]{2,1,0:T(8,128)(2,1)S(1)}, bf16[4,64,128]{2,1,0:T(8,128)(2,1)S(1)}, u32[]{:S(2)}, u32[]{:S(2)}) collective-permute-start(bf16[4,64,128]{2,1,0:T(8,128)(2,1)S(1)} %get-tuple-element.63), channel_id=1, source_target_pairs={{0,4},{2,6},{4,0},{6,2},{8,12},{10,14},{12,8},{14,10},{16,20},{18,... | collective-permute-start | bytes 196616 | tf_op jit(solution)/shard_map/ppermute | solution.py:273
  40.3 11.9 %collective-permute-start.28 = (bf16[4,64,128]{2,1,0:T(8,128)(2,1)S(1)}, bf16[4,64,128]{2,1,0:T(8,128)(2,1)S(1)}, u32[]{:S(2)}, u32[]{:S(2)}) collective-permute-start(bf16[4,64,128]{2,1,0:T(8,128)(2,1)S(1)} %get-tuple-element.64), channel_id=1, source_target_pairs={{0,12},{1,9},{2,14},{3,11},{4,8},{5,13},{6,10},{7,15},{8,4},{9,1},... | collective-permute-start | bytes 196616 | tf_op jit(solution)/shard_map/ppermute | solution.py:273
  42.1 10.5 %collective-permute-start.26 = (bf16[4,64,128]{2,1,0:T(8,128)(2,1)S(1)}, bf16[4,64,128]{2,1,0:T(8,128)(2,1)S(1)}, u32[]{:S(2)}, u32[]{:S(2)}) collective-permute-start(bf16[4,64,128]{2,1,0:T(8,128)(2,1)S(1)} %get-tuple-element.65), channel_id=1, source_target_pairs={{0,20},{1,17},{2,22},{3,19},{4,16},{5,21},{6,18},{7,23},{8,28},{9,... | collective-permute-start | bytes 196616 | tf_op jit(solution)/shard_map/ppermute | solution.py:273
  45.5 7.6 %collective-permute-start.24 = (bf16[4,64,128]{2,1,0:T(8,128)(2,1)S(1)}, bf16[4,64,128]{2,1,0:T(8,128)(2,1)S(1)}, u32[]{:S(2)}, u32[]{:S(2)}) collective-permute-start(bf16[4,64,128]{2,1,0:T(8,128)(2,1)S(1)} %get-tuple-element.66), channel_id=1, source_target_pairs={{0,28},{1,25},{2,30},{3,27},{4,24},{5,29},{6,26},{7,31},{8,20},{9,... | collective-permute-start | bytes 196616 | tf_op jit(solution)/shard_map/ppermute | solution.py:273
  46.7 4.0 %collective-permute-start.19 = (f32[32,256]{1,0:T(8,128)S(1)}, f32[32,256]{1,0:T(8,128)S(1)}, u32[]{:S(2)}, u32[]{:S(2)}) collective-permute-start(f32[32,256]{1,0:T(8,128)S(1)} %add_add_fusion), channel_id=1, source_target_pairs={{0,4},{4,0},{8,12},{12,8},{16,20},{20,16},{24,28},{28,24},{1,5},{5... | collective-permute-start | bytes 98312 | tf_op jit(solution)/shard_map/ppermute | solution.py:342
  50.7 8.0 %collective-permute-start.13 = (bf16[64,512]{1,0:T(8,128)(2,1)S(1)}, bf16[64,512]{1,0:T(8,128)(2,1)S(1)}, u32[]{:S(2)}, u32[]{:S(2)}) collective-permute-start(bf16[64,512]{1,0:T(8,128)(2,1)S(1)} %get-tuple-element.46), channel_id=1, source_target_pairs={{0,1},{1,0},{2,3},{3,2},{4,5},{5,4},{6,7},{7,6},{8,9},{9,8},{10,11... | collective-permute-start | bytes 196616 | tf_op jit(solution)/shard_map/ppermute | solution.py:264
  50.7 8.0 %collective-permute-start.14 = (bf16[64,512]{1,0:T(8,128)(2,1)S(1)}, bf16[64,512]{1,0:T(8,128)(2,1)S(1)}, u32[]{:S(2)}, u32[]{:S(2)}) collective-permute-start(bf16[64,512]{1,0:T(8,128)(2,1)S(1)} %get-tuple-element.47), channel_id=1, source_target_pairs={{0,2},{1,3},{2,0},{3,1},{4,6},{5,7},{6,4},{7,5},{8,10},{9,11},{10,... | collective-permute-start | bytes 196616 | tf_op jit(solution)/shard_map/ppermute | solution.py:264
  52.3 6.4 %collective-permute-start.15 = (bf16[64,512]{1,0:T(8,128)(2,1)S(1)}, bf16[64,512]{1,0:T(8,128)(2,1)S(1)}, u32[]{:S(2)}, u32[]{:S(2)}) collective-permute-start(bf16[64,512]{1,0:T(8,128)(2,1)S(1)} %get-tuple-element.48), channel_id=1, source_target_pairs={{0,3},{1,2},{2,1},{3,0},{4,7},{5,6},{6,5},{7,4},{8,11},{9,10},{10,... | collective-permute-start | bytes 196616 | tf_op jit(solution)/shard_map/ppermute | solution.py:264
  52.6 3.9 %collective-permute-start.20 = (f32[32,256]{1,0:T(8,128)S(1)}, f32[32,256]{1,0:T(8,128)S(1)}, u32[]{:S(2)}, u32[]{:S(2)}) collective-permute-start(f32[32,256]{1,0:T(8,128)S(1)} %add.36), channel_id=1, source_target_pairs={{0,8},{4,12},{8,0},{12,4},{16,24},{20,28},{24,16},{28,20},{1,9},{5... | collective-permute-start | bytes 98312 | tf_op jit(solution)/shard_map/ppermute | solution.py:342
  53.9 8.1 %collective-permute-start.31 = (f32[32,2048]{1,0:T(8,128)S(1)}, f32[32,2048]{1,0:T(8,128)S(1)}, u32[]{:S(2)}, u32[]{:S(2)}) collective-permute-start(f32[32,2048]{1,0:T(8,128)S(1)} %get-tuple-element.62), channel_id=1, source_target_pairs={{0,1},{1,0},{2,3},{3,2},{4,5},{5,4},{6,7},{7,6},{8,9},{9,8},{10,11... | collective-permute-start | bytes 786440 | tf_op jit(solution)/shard_map/ppermute | solution.py:264
  56.6 4.8 %collective-permute-start.21 = (f32[32,256]{1,0:T(8,128)S(1)}, f32[32,256]{1,0:T(8,128)S(1)}, u32[]{:S(2)}, u32[]{:S(2)}) collective-permute-start(f32[32,256]{1,0:T(8,128)S(1)} %add.37), channel_id=1, source_target_pairs={{0,16},{4,20},{8,24},{12,28},{16,0},{20,4},{24,8},{28,12},{1,17},{... | collective-permute-start | bytes 98312 | tf_op jit(solution)/shard_map/ppermute | solution.py:342
where the time goes:
time: 63 us; the launch traced here: 62.7 us
  starting transfers between devices  32.7 us (52%)
  waiting for transfers between devices  14.5 us (23%)
  Pallas kernels  12.5 us (20%)
  other arithmetic  1.45 us (2%)
  between operations  0.86 us (1%)
  local copies, waits for them, and re-layouts  0.71 us (1%)
    ppermute x8, starting transfers between devices, over_rows(): return lax.ppermute(v, ('rows', 'cols'), pairs)  18.5 us
    pallas_call x10, Pallas kernels, call(): pl.pallas_call(kernel, out_shape=[pltpu.VMEM(s, d) for s, d in outs] if i...  11.7 us
    ppermute x21, starting transfers between devices, mate(): return lax.ppermute(v, 'cols', [(i, i ^ q) for i in range(cols_n)])  11 us
    ppermute x3, waiting for transfers between devices, layer(): lax.ppermute(wg, 'rows', [(i, i ^ 1 << bit) for i in range(rows_n)])  7.9 us
    ppermute x21, waiting for transfers between devices, mate(): return lax.ppermute(v, 'cols', [(i, i ^ q) for i in range(cols_n)])  3.4 us
    ppermute x8, waiting for transfers between devices, over_rows(): return lax.ppermute(v, ('rows', 'cols'), pairs)  3.23 us
    ppermute x3, starting transfers between devices, layer(): lax.ppermute(wg, 'rows', [(i, i ^ 1 << bit) for i in range(rows_n)])  3.18 us
  transfers between devices with their start and end apart: 32, of which 8 were waited for; matrix products, arithmetic and copies ran while one was open for 1% of the time, Pallas kernels for 16%

commit v1 on v0

v1 whole, which is shorter than its diff:
```python
import functools
import math

import jax
import jax.numpy as jnp
from jax import lax
from jax.experimental import pallas as pl
from jax.experimental.pallas import tpu as pltpu
from jax.sharding import PartitionSpec as P

CAP = 4
LANES = 128
F32, BF16, I32 = jnp.float32, jnp.bfloat16, jnp.int32
VMEM = pl.BlockSpec(memory_space=pltpu.VMEM)
SMEM = pl.BlockSpec(memory_space=pltpu.SMEM)
HBM = pl.BlockSpec(memory_space=pltpu.HBM)
MIB = 1 << 20


def call(kernel, in_specs, out_shape, args, scratch=(), flops=10**6, mib=8, out=False):
    place = jax.ShapeDtypeStruct if out else pltpu.VMEM
    outs = out_shape if isinstance(out_shape, list) else [out_shape]
    nbytes = sum(a.size * a.dtype.itemsize for a in args)
    return pl.pallas_call(
        kernel,
        out_shape=[place(s, d) for s, d in outs]
        if isinstance(out_shape, list)
        else place(*out_shape),
        in_specs=in_specs,
        out_specs=[VMEM] * len(outs) if isinstance(out_shape, list) else VMEM,
        scratch_shapes=list(scratch),
        compiler_params=pltpu.CompilerParams(vmem_limit_bytes=mib * MIB),
        cost_estimate=pl.CostEstimate(flops=flops, bytes_accessed=nbytes, transcendentals=0),
    )(*args)


def iota(shape, dim):
    return lax.broadcasted_iota(I32, shape, dim)


def position():
    col = lax.axis_index("cols")
    return lax.axis_index("rows"), lax.rem(col, 2), col // 2


def rows_at(start, size):
    return pl.ds(pl.multiple_of(start * size, size), size)


def choose_kernel(adj_ref, feats, sel, copied, sends, sel_s, sems):
    copy = pltpu.make_async_copy(feats, copied, sems.at[0])
    copy.start()
    slots_n, ids_n = adj_ref.shape
    tile = sends.shape[3]
    blk = feats.shape[1] // tile
    r, _, _ = position()
    adj = adj_ref[...]
    mine = r * blk + iota((blk, ids_n), 0)
    hits = jnp.zeros((blk, ids_n), F32)
    for k in range(slots_n):
        hits += (adj[k : k + 1, :] == mine).astype(F32)
    group = (iota((ids_n, LANES), 0) // blk == iota((ids_n, LANES), 1)).astype(BF16)
    wants = jnp.dot(hits.astype(BF16), group, preferred_element_type=F32) > 0.5
    below = (iota((blk, blk), 1) < iota((blk, blk), 0)).astype(BF16)
    order = jnp.dot(below, wants.astype(BF16), preferred_element_type=F32)
    number = iota((blk, LANES), 0).astype(F32)
    for o in range(CAP):
        pick = jnp.where(wants & (jnp.abs(order - o) < 0.5), number, 0.0)
        sel[o : o + 1, :] = jnp.sum(pick, axis=0, keepdims=True).astype(I32)
    scalars = pltpu.make_async_copy(sel, sel_s, sems.at[1])
    scalars.start()
    copy.wait()
    scalars.wait()
    for d in range(sends.shape[0]):
        for o in range(CAP):
            sends[d, o] = copied[:, rows_at(sel_s[o, d], tile)]


def slot_kernel(blk, adj_ref, out_ref):
    slots_n, ids_n = adj_ref.shape
    r, _, _ = position()
    start = pl.multiple_of((r * blk) // LANES * LANES, LANES)
    near = adj_ref[:, pl.ds(start, LANES)]
    block = iota((ids_n, LANES), 0)
    seen = jnp.zeros((ids_n, LANES), F32)
    for k in range(slots_n):
        seen += (near[k : k + 1, :] == block).astype(F32)
    own = ((iota((LANES, LANES), 0) + start) // blk == r).astype(BF16)
    needed = jnp.dot(seen.astype(BF16), own, preferred_element_type=F32) > 0.5
    a, b = iota((ids_n, ids_n), 0), iota((ids_n, ids_n), 1)
    earlier = ((b < a) & (a // blk == b // blk)).astype(BF16)
    place = jnp.dot(earlier, needed.astype(BF16), preferred_element_type=F32).astype(I32)
    source = block // blk
    slot = jnp.where(source == r, block % blk, blk + source * CAP + place).astype(F32)
    for k in range(slots_n):
        found = jnp.where(near[k : k + 1, :] == block, slot, 0.0)
        out_ref[k : k + 1, :] = jnp.sum(found, axis=0, keepdims=True).astype(I32)


def fetch_kernel(side_of, a_hbm, *rest):
    _, c, x = position()
    copies = []
    if len(rest) > 2:
        cot, a_side, *pieces, sems = rest
        width = pieces[0].shape[1]
        for q in (1, 2, 3, 0):
            at = rows_at((c ^ (q & 1)) * 2 + (x ^ (q >> 1)), width)
            copies.append(pltpu.make_async_copy(cot.at[:, at], pieces[q], sems.at[q]))
    else:
        a_side, sems = rest
    n = a_side.shape[0]
    first = (2 * c + side_of(x)) * n
    for i in range(n):
        copies.append(pltpu.make_async_copy(a_hbm.at[first + i], a_side.at[i], sems.at[4 + i]))
    for copy in copies:
        copy.start()
    for copy in copies:
        copy.wait()


def gather_kernel(side_of, slot, a_side, mine, mate, got, got_mate, out, table):
    r, c, x = position()
    f = mine.shape[0]
    top, low = rows_at(c, f), rows_at(1 - c, f)
    tile = a_side.shape[3]
    blk = mine.shape[1] // tile
    for b in range(blk):
        table[b, top, :] = mine[:, b * tile : (b + 1) * tile]
        table[b, low, :] = mate[:, b * tile : (b + 1) * tile]
    for d in range(got.shape[0]):
        for o in range(CAP):
            table[blk + d * CAP + o, top, :] = got[d, o]
            table[blk + d * CAP + o, low, :] = got_mate[d, o]
    n, slots_n, tile, _ = a_side.shape
    lane = lax.rem(r * 4 * n, LANES) + (2 * c + side_of(x)) * n
    for t in range(n):
        acc = None
        for k in range(0, slots_n, 2):
            left = [table[slot[k + h, lane + t]] for h in range(2)]
            right = [a_side[t, k + h] for h in range(2)]
            part = lax.dot_general(
                jnp.concatenate(left, axis=1),
                jnp.concatenate(right, axis=1),
                (((1,), (1,)), ((), ())),
                preferred_element_type=F32,
            )
            acc = part if acc is None else acc + part
        out[:, t * tile : (t + 1) * tile] = acc.astype(BF16)


def dense_kernel(keep, came, w_ref, c0, c1, c2, c3, *rest):
    outs, (g_send, g_keep), wgs = rest[:4], rest[4:6], rest[6:10]
    agg, cot, out_s, grad_s, wg_s = rest[10:]
    _, c, x = position()
    fx = keep.shape[0]
    u = c0.shape[0]
    col = 2 * x + c
    agg[rows_at(x, fx), :] = keep[...]
    agg[rows_at(1 - x, fx), :] = came[...]
    for q, piece in enumerate((c0, c1, c2, c3)):
        cot[rows_at(col ^ q, u), :] = piece[...]
    w = w_ref[...]
    act = agg[...]
    pre_act = lax.dot_general(w, act, (((0,), (0,)), ((), ())), preferred_element_type=F32)
    sigm = jax.nn.sigmoid(pre_act)
    out_s[...] = (pre_act * sigm).astype(BF16)
    pre = (cot[...].astype(F32) * sigm * (1.0 + pre_act * (1.0 - sigm))).astype(BF16)
    grad_s[...] = jnp.dot(w, pre, preferred_element_type=F32).astype(BF16)
    wg_s[...] = lax.dot_general(act, pre, (((1,), (1,)), ((), ())), preferred_element_type=F32)
    g_keep[...] = grad_s[rows_at(x, fx), :]
    g_send[...] = grad_s[rows_at(1 - x, fx), :]
    f = wgs[0].shape[0]
    for q in range(4):
        outs[q][...] = out_s[rows_at(col ^ q, u), :]
        wgs[q][...] = wg_s[rows_at(col ^ q, f), :]


def spread(side_of, slot, a_side, g_ref, acc):
    r, c, x = position()
    n, slots_n, tile, _ = a_side.shape
    lane = lax.rem(r * 4 * n, LANES) + (2 * c + side_of(x)) * n
    for t in range(n):
        g = g_ref[:, t * tile : (t + 1) * tile]
        for k in range(0, slots_n, 2):
            right = jnp.concatenate([a_side[t, k], a_side[t, k + 1]], axis=1)
            part = jnp.dot(g, right, preferred_element_type=F32)
            acc[slot[k, lane + t]] += part[:, :tile]
            acc[slot[k + 1, lane + t]] += part[:, tile:]


def spread_first_kernel(side_of, slot, a_side, g_ref, acc):
    acc[...] = jnp.zeros_like(acc)
    spread(side_of, slot, a_side, g_ref, acc)


def spread_last_kernel(side_of, slot, a_side, g_ref, before, own, own_send, stay, send, acc):
    acc[...] = before[...]
    spread(side_of, slot, a_side, g_ref, acc)
    _, c, _ = position()
    f = own.shape[0]
    top, low = rows_at(c, f), rows_at(1 - c, f)
    tile = a_side.shape[3]
    blk = own.shape[1] // tile
    for d in range(send.shape[0]):
        for o in range(CAP):
            stay[d, o] = acc[blk + d * CAP + o, top, :]
            send[d, o] = acc[blk + d * CAP + o, low, :].astype(BF16)
    for b in range(blk):
        own[:, b * tile : (b + 1) * tile] = acc[b, top, :]
        own_send[:, b * tile : (b + 1) * tile] = acc[b, low, :]


def collect_kernel(sel, own, came, back, out):
    tile = back.shape[3]
    out[...] = own[...] + came[...]
    for d in range(back.shape[0]):
        for o in range(CAP):
            out[:, rows_at(sel[o, d], tile)] += back[d, o].astype(F32)


def place_kernel(p0, p1, p2, p3, out):
    _, c, x = position()
    width = p0.shape[1]
    for q, piece in enumerate((p0, p1, p2, p3)):
        out[:, rows_at((c ^ (q & 1)) * 2 + (x ^ (q >> 1)), width)] = piece[...]


def layer(feats_t, adj_index, adj_weight, weight, cotangent_t):
    f, nodes = feats_t.shape
    blk, slots_n, tile, _ = adj_weight.shape
    units_loc = cotangent_t.shape[0]
    f_in, units = weight.shape
    rows_n, cols_n = lax.axis_size("rows"), lax.axis_size("cols")
    assert cols_n == 4 and rows_n & (rows_n - 1) == 0 and blk % 4 == 0
    table_n = blk + rows_n * CAP
    fx = 2 * f
    quarter = nodes // 4
    big = min(48, 8 + rows_n)

    def mate(v, q):
        return lax.ppermute(v, "cols", [(i, i ^ q) for i in range(cols_n)])

    def over_rows(v):
        return lax.all_to_all(v, "rows", 0, 0, tiled=True)

    adj_t = adj_index.T
    in_hbm = functools.partial(pltpu.with_memory_space_constraint, memory_space=pltpu.HBM)
    part = (rows_n, CAP, f, tile)
    piece = ((units_loc, quarter), BF16)
    sel, feats, sends = call(
        choose_kernel, [VMEM, HBM],
        [((8, LANES), I32), ((f, nodes), BF16), (part, BF16)], [adj_t, in_hbm(feats_t)],
        [pltpu.SMEM((8, LANES), I32), pltpu.SemaphoreType.DMA((2,))], mib=big,
    )
    feats_mate = mate(feats, 1)
    got = over_rows(sends)

    def far(x):
        return 1 - x

    def near(x):
        return x

    a_side = ((blk // 4, slots_n, tile, tile), BF16)
    sems = [pltpu.SemaphoreType.DMA((4 + blk // 4,))]
    a_far, *cots = call(
        functools.partial(fetch_kernel, far), [HBM, HBM], [a_side] + [piece] * 4,
        [in_hbm(adj_weight), in_hbm(cotangent_t)], sems,
    )
    a_near = call(
        functools.partial(fetch_kernel, near), [HBM], a_side,
        [in_hbm(adj_weight)], sems,
    )
    slot = call(
        functools.partial(slot_kernel, blk), [VMEM],
        ((slots_n, LANES), I32), [adj_t], mib=big,
    )
    cots = [cots[0]] + [mate(cots[q], q) for q in (1, 2, 3)]
    got_mate = mate(got, 1)

    a_flops = blk // 2 * slots_n * fx * tile * tile

    def gather(side_of, a_side):
        args = [slot, a_side, feats, feats_mate, got, got_mate]
        return call(
            functools.partial(gather_kernel, side_of), [SMEM] + [VMEM] * (len(args) - 1),
            ((fx, quarter), BF16), args, [pltpu.VMEM((table_n, fx, tile), BF16)], a_flops,
            big,
        )

    agg_far = gather(far, a_far)
    agg_came = mate(agg_far, 2)
    agg_near = gather(near, a_near)

    half_g = ((fx, quarter), BF16)
    wg_part = ((f, units), F32)
    args = [agg_near, agg_came, weight, *cots]
    *outs, g_send, g_keep, w0, w1, w2, w3 = call(
        dense_kernel, [VMEM] * len(args),
        [piece] * 4 + [half_g] * 2 + [wg_part] * 4, args,
        [
            pltpu.VMEM((f_in, quarter), BF16),
            pltpu.VMEM((units, quarter), BF16),
            pltpu.VMEM((units, quarter), BF16),
            pltpu.VMEM((f_in, quarter), BF16),
            pltpu.VMEM((f_in, units), F32),
        ],
        6 * f_in * units * quarter, 12,
    )
    g_came = mate(g_send, 2)
    wg = w0 + mate(w1, 1) + mate(w2, 2) + mate(w3, 3)
    bit = 0
    while 1 << bit < rows_n:
        wg = wg + lax.ppermute(wg, "rows", [(i, i ^ (1 << bit)) for i in range(rows_n)])
        bit += 1
    weight_grad = wg * (1.0 / math.sqrt(nodes * rows_n))

    acc = call(
        functools.partial(spread_first_kernel, near), [SMEM, VMEM, VMEM],
        ((table_n, fx, tile), F32), [slot, a_near, g_keep], [], a_flops, big,
    )
    own, own_send, stay, send = call(
        functools.partial(spread_last_kernel, far), [SMEM, VMEM, VMEM, VMEM],
        [((f, nodes), F32)] * 2 + [(part, F32), (part, BF16)],
        [slot, a_far, g_came, acc], [pltpu.VMEM((table_n, fx, tile), F32)], a_flops, big + 8,
    )
    total = (stay + mate(send, 1).astype(F32)).astype(BF16)
    own_came = mate(own_send, 1)
    back = over_rows(total)
    feat_grad = call(
        collect_kernel, [SMEM, VMEM, VMEM, VMEM], ((f, nodes), F32),
        [sel, own, own_came, back], mib=big, out=True,
    )

    outs = [outs[0]] + [mate(outs[q], q) for q in (1, 2, 3)]
    output_t = call(place_kernel, [VMEM] * 4, ((units_loc, nodes), BF16), outs, out=True)
    return output_t, weight_grad, feat_grad


def solution(mesh):
    return jax.shard_map(
        layer,
        mesh=mesh,
        in_specs=(P("cols", "rows"), P(), P("rows", None, None, None), P(), P("cols", "rows")),
        out_specs=(P("cols", "rows"), P("cols", None), P("cols", "rows")),
        check_vma=False,
    )
```

time: 63 us -> 59.1 us (0.938)
  blocking collectives: 0 us -> 16 us
  starting transfers between devices: 32.7 us -> 19.6 us
  waiting for transfers between devices: 14.5 us -> 6.55 us
  Pallas kernels: 12.5 us -> 13.6 us
    ppermute x8 -> x0, starting transfers between devices: 18.5 us -> none  [over_rows(): return lax.ppermute(v, ('rows', 'cols'), pairs)]
    all_to_all x0 -> x1, blocking collectives: none -> 16 us  [over_rows(): return lax.all_to_all(v, 'rows', 0, 0, tiled=True)]
    ppermute x3, starting transfers between devices: 3.18 us -> 6.78 us  [layer(): lax.ppermute(wg, 'rows', [(i, i ^ 1 << bit) for i in range(rows_n)])]
    all_to_all x0 -> x1, starting transfers between devices: none -> 3.59 us  [over_rows(): return lax.all_to_all(v, 'rows', 0, 0, tiled=True)]
    ppermute x3, waiting for transfers between devices: 7.9 us -> 4.66 us  [layer(): lax.ppermute(wg, 'rows', [(i, i ^ 1 << bit) for i in range(rows_n)])]
    ppermute x8 -> x0, waiting for transfers between devices: 3.23 us -> none  [over_rows(): return lax.ppermute(v, ('rows', 'cols'), pairs)]
    ppermute x21 -> x15, starting transfers between devices: 11 us -> 9.26 us  [mate(): return lax.ppermute(v, 'cols', [(i, i ^ q) for i in range(cols_n)])]
    ppermute x21 -> x15, waiting for transfers between devices: 3.4 us -> 1.88 us  [mate(): return lax.ppermute(v, 'cols', [(i, i ^ q) for i in range(cols_n)])]
  transfers between devices with their start and end apart: 32 -> 19, of which waited for: 8 -> 4; matrix products, arithmetic and copies ran while one was open for 1% -> 2% of each run, Pallas kernels for 16% -> 15%
where the time goes in v1:
time: 59.1 us; the launch traced here: 58.7 us
  starting transfers between devices  19.6 us (33%)
  blocking collectives  16 us (27%)
  Pallas kernels  13.6 us (23%)
  waiting for transfers between devices  6.55 us (11%)
  other arithmetic  1.42 us (2%)
  between operations  0.82 us (1%)
  local copies, waits for them, and re-layouts  0.7 us (1%)
    all_to_all x1, blocking collectives, over_rows(): return lax.all_to_all(v, 'rows', 0, 0, tiled=True)  16 us
    pallas_call x11, Pallas kernels, call(): pl.pallas_call(kernel, out_shape=[place(s, d) for s, d in outs] if isinst...  13.6 us
    ppermute x15, starting transfers between devices, mate(): return lax.ppermute(v, 'cols', [(i, i ^ q) for i in range(cols_n)])  9.26 us
    ppermute x3, starting transfers between devices, layer(): lax.ppermute(wg, 'rows', [(i, i ^ 1 << bit) for i in range(rows_n)])  6.78 us
    ppermute x3, waiting for transfers between devices, layer(): lax.ppermute(wg, 'rows', [(i, i ^ 1 << bit) for i in range(rows_n)])  4.66 us
    all_to_all x1, starting transfers between devices, over_rows(): return lax.all_to_all(v, 'rows', 0, 0, tiled=True)  3.59 us
    ppermute x15, waiting for transfers between devices, mate(): return lax.ppermute(v, 'cols', [(i, i ^ q) for i in range(cols_n)])  1.88 us
  transfers between devices with their start and end apart: 19, of which 4 were waited for; matrix products, arithmetic and copies ran while one was open for 2% of the time, Pallas kernels for 15%

profile of v1, /device:TPU:0, one launch (start us, length us, event | category | flops | bytes accessed | tf_op | source)
XLA Modules:
  0.0 58.7 jit_solution(3282595358873265138)
XLA Ops:
  0.6 0.0 copy-start.1
  0.6 0.7 %copy-done.1 = s32[128,16]{0,1:T(8,128)S(1)} copy-done((s32[128,16]{0,1:T(8,128)S(1)}, s32[128,16]{0,1:T(8,128)}, u32[]{:S(2)}) %copy-start.1) | copy-done | bytes 8216
  1.3 1.0 %shard_map.78 = (s32[8,128]{1,0:T(8,128)S(1)}, bf16[32,2048]{1,0:T(8,128)(2,1)S(1)}, bf16[8,4,32,128]{3,2,1,0:T(8,128)(2,1)S(1)}) custom-call(s32[16,128]{1,0:T(8,128)S(1)} %bitcast.1, bf16[32,2048]{1,0:T(8,128)(2,1)} %feats.1), custom_call_target="tpu_custom_call" | custom-call | flops 1000000 | bytes 139264 | tf_op jit(solution)/shard_map/pallas_call | solution.py:24
  2.3 16.0 %all_to_all.10.got = bf16[8,4,32,128]{3,2,1,0:T(8,128)(2,1)S(1)} all-to-all(bf16[8,4,32,128]{3,2,1,0:T(8,128)(2,1)S(1)} %get-tuple-element.26), channel_id=1, replica_groups=mesh['rows'=8,'cols'=4] {'rows'}, dimensions={0} | all-to-all | bytes 524288 | tf_op jit(solution)/shard_map/all_to_all | solution.py:244
  18.4 0.0 collective-permute-start.1
  18.4 0.5 collective-permute-start
  18.9 1.7 %shard_map.80 = (bf16[4,16,128,128]{3,2,1,0:T(8,128)(2,1)S(1)}, bf16[64,512]{1,0:T(8,128)(2,1)S(1)}, bf16[64,512]{1,0:T(8,128)(2,1)S(1)}, bf16[64,512]{1,0:T(8,128)(2,1)S(1)}, bf16[64,512]{1,0:T(8,128)(2,1)S(1)}) custom-call(bf16[16,16,128,128]{3,2,1,0:T(8,128)(2,1)} %a_hbm.3, bf16[64,2048]{1,0:T(8,128)(2,1)} %rest_0_.1), custom_call_target="tpu_custom_call" | custom-call | flops 1000000 | bytes 8650752 | tf_op jit(solution)/shard_map/pallas_call | solution.py:24
  20.6 0.1 collective-permute-start.3
  20.7 1.6 %collective-permute-start.4 = (bf16[64,512]{1,0:T(8,128)(2,1)S(1)}, bf16[64,512]{1,0:T(8,128)(2,1)S(1)}, u32[]{:S(2)}, u32[]{:S(2)}) collective-permute-start(bf16[64,512]{1,0:T(8,128)(2,1)S(1)} %get-tuple-element.30), channel_id=1, source_target_pairs={{0,2},{1,3},{2,0},{3,1},{4,6},{5,7},{6,4},{7,5},{8,10},{9,11},{10,... | collective-permute-start | bytes 196616 | tf_op jit(solution)/shard_map/ppermute | solution.py:241
  22.2 0.3 collective-permute-start.5
  22.5 0.6 %shard_map.76.slot = s32[16,128]{1,0:T(8,128)S(1)} custom-call(s32[16,128]{1,0:T(8,128)S(1)} %bitcast.2), custom_call_target="tpu_custom_call" | custom-call | flops 1000000 | bytes 8192 | tf_op jit(solution)/shard_map/pallas_call | solution.py:24
  23.1 0.0 collective-permute-done.mate
  23.2 0.0 collective-permute-done.1.got_mate
  23.2 1.6 %shard_map.81 = bf16[64,512]{1,0:T(8,128)(2,1)S(1)} custom-call(s32[16,128]{1,0:T(8,128)S(1)} %shard_map.76.slot, bf16[4,16,128,128]{3,2,1,0:T(8,128)(2,1)S(1)} %get-tuple-element.27.a_side, bf16[32,2048]{1,0:T(8,128)(2,1)S(1)} %get-tuple-element.25.mine, bf16[32,2048]{1,0:T(8,128)(2,1)S(1)} %collective-permute-done.mate, ...), custom_call_target="tpu_custom_call" | custom-call | flops 134217728 | bytes 2891776 | tf_op jit(solution)/shard_map/pallas_call | solution.py:24
  24.7 1.6 %collective-permute-start.2 = (bf16[64,512]{1,0:T(8,128)(2,1)S(1)}, bf16[64,512]{1,0:T(8,128)(2,1)S(1)}, u32[]{:S(2)}, u32[]{:S(2)}) collective-permute-start(bf16[64,512]{1,0:T(8,128)(2,1)S(1)} %shard_map.81), channel_id=1, source_target_pairs={{0,2},{1,3},{2,0},{3,1},{4,6},{5,7},{6,4},{7,5},{8,10},{9,11},{10,... | collective-permute-start | bytes 196616 | tf_op jit(solution)/shard_map/ppermute | solution.py:241
  26.3 1.6 %shard_map.77.a_side = bf16[4,16,128,128]{3,2,1,0:T(8,128)(2,1)S(1)} custom-call(bf16[16,16,128,128]{3,2,1,0:T(8,128)(2,1)} %a_hbm.3), custom_call_target="tpu_custom_call" | custom-call | flops 1000000 | bytes 8388608 | tf_op jit(solution)/shard_map/pallas_call | solution.py:24
  27.9 0.0 copy-start
  27.9 1.6 %shard_map.79.keep = bf16[64,512]{1,0:T(8,128)(2,1)S(1)} custom-call(s32[16,128]{1,0:T(8,128)S(1)} %shard_map.76.slot, bf16[4,16,128,128]{3,2,1,0:T(8,128)(2,1)S(1)} %shard_map.77.a_side, bf16[32,2048]{1,0:T(8,128)(2,1)S(1)} %get-tuple-element.25.mine, bf16[32,2048]{1,0:T(8,128)(2,1)S(1)} %collective-permute-done.mate, ...), custom_call_target="tpu_custom_call" | custom-call | flops 134217728 | bytes 2891776 | tf_op jit(solution)/shard_map/pallas_call | solution.py:24
  29.5 0.0 collective-permute-done.3.c1
  29.5 0.0 collective-permute-done.4.c2
  29.5 0.0 collective-permute-done.5.c3
  29.5 0.0 collective-permute-done.2.came
  29.5 0.0 copy-done
  29.5 0.6 %shard_map.82 = (bf16[64,512]{1,0:T(8,128)(2,1)S(1)}, bf16[64,512]{1,0:T(8,128)(2,1)S(1)}, bf16[64,512]{1,0:T(8,128)(2,1)S(1)}, bf16[64,512]{1,0:T(8,128)(2,1)S(...) custom-call(bf16[64,512]{1,0:T(8,128)(2,1)S(1)} %shard_map.79.keep, ...), custom_call_target="tpu_custom_call" | custom-call | flops 100663296 | bytes 458752 | tf_op jit(solution)/shard_map/pallas_call | solution.py:24
  30.1 1.2 %collective-permute-start.15 = (bf16[64,512]{1,0:T(8,128)(2,1)S(1)}, bf16[64,512]{1,0:T(8,128)(2,1)S(1)}, u32[]{:S(2)}, u32[]{:S(2)}) collective-permute-start(bf16[64,512]{1,0:T(8,128)(2,1)S(1)} %get-tuple-element.41), channel_id=1, source_target_pairs={{0,2},{1,3},{2,0},{3,1},{4,6},{5,7},{6,4},{7,5},{8,10},{9,11},{10,... | collective-permute-start | bytes 196616 | tf_op jit(solution)/shard_map/ppermute | solution.py:241
  31.3 1.3 %shard_map.84.before = f32[48,64,128]{2,1,0:T(8,128)S(1)} custom-call(s32[16,128]{1,0:T(8,128)S(1)} %shard_map.76.slot, bf16[4,16,128,128]{3,2,1,0:T(8,128)(2,1)S(1)} %shard_map.77.a_side, bf16[64,512]{1,0:T(8,128)(2,1)S(1)} %get-tuple-element.42.g_ref), custom_call_target="tpu_custom_call" | custom-call | flops 134217728 | bytes 2170880 | tf_op jit(solution)/shard_map/pallas_call | solution.py:24
  32.6 1.8 %collective-permute-done.15.g_ref = bf16[64,512]{1,0:T(8,128)(2,1)S(1)} collective-permute-done((bf16[64,512]{1,0:T(8,128)(2,1)S(1)}, bf16[64,512]{1,0:T(8,128)(2,1)S(1)}, u32[]{:S(2)}, u32[]{:S(2)}) %collective-permute-start.15) | collective-permute-done | bytes 65568 | tf_op jit(solution)/shard_map/ppermute | solution.py:241
  34.4 1.4 %shard_map.85 = (f32[32,2048]{1,0:T(8,128)S(1)}, f32[32,2048]{1,0:T(8,128)S(1)}, f32[8,4,32,128]{3,2,1,0:T(8,128)S(1)}, bf16[8,4,32,128]{3,2,1,0:T(8,128)(2,1)S(1)}) custom-call(s32[16,128]{1,0:T(8,128)S(1)} %shard_map.76.slot, bf16[4,16,128,128]{3,2,1,0:T(8,128)(2,1)S(1)} %get-tuple-element.27.a_side, bf16[64,512]{1,0:T(8,128)(2,1)S(1)} %collective-permute-done.15.g_ref, ...), custom_call_target="tpu_custom_call" | custom-call | flops 134217728 | bytes 3743744 | tf_op jit(solution)/shard_map/pallas_call | solution.py:24
  35.9 0.1 collective-permute-start.17
  35.9 1.2 %collective-permute-start.11 = (f32[32,256]{1,0:T(8,128)S(1)}, f32[32,256]{1,0:T(8,128)S(1)}, u32[]{:S(2)}, u32[]{:S(2)}) collective-permute-start(f32[32,256]{1,0:T(8,128)S(1)} %get-tuple-element.39), channel_id=1, source_target_pairs={{0,3},{1,2},{2,1},{3,0},{4,7},{5,6},{6,5},{7,4},{8,11},{9,10},{10,... | collective-permute-start | bytes 98312 | tf_op jit(solution)/shard_map/ppermute | solution.py:241
  37.2 0.9 %collective-permute-start.10 = (f32[32,256]{1,0:T(8,128)S(1)}, f32[32,256]{1,0:T(8,128)S(1)}, u32[]{:S(2)}, u32[]{:S(2)}) collective-permute-start(f32[32,256]{1,0:T(8,128)S(1)} %get-tuple-element.38), channel_id=1, source_target_pairs={{0,2},{1,3},{2,0},{3,1},{4,6},{5,7},{6,4},{7,5},{8,10},{9,11},{10,... | collective-permute-start | bytes 98312 | tf_op jit(solution)/shard_map/ppermute | solution.py:241
  38.1 0.0 collective-permute-start.9
  38.1 0.0 collective-permute-done.17
  38.1 0.8 %add_convert_fusion = bf16[8,4,32,128]{3,2,1,0:T(8,128)(2,1)} fusion(f32[8,4,32,128]{3,2,1,0:T(8,128)S(1)} %get-tuple-element.45, bf16[8,4,32,128]{3,2,1,0:T(8,128)(2,1)S(1)} %collective-permute-done.17), kind=kLoop, calls=%fused_computation | loop fusion | flops 393216 | bytes 1048576 | tf_op jit(solution)/shard_map/convert_element_type | solution.py:327
  38.8 3.6 %all-to-all-start.1 = ((bf16[8,4,32,128]{3,2,1,0:T(8,128)(2,1)}), bf16[8,4,32,128]{3,2,1,0:T(8,128)(2,1)S(1)}, u32[]{:S(2)}, u32[]{:S(2)}) async-start(bf16[8,4,32,128]{3,2,1,0:T(8,128)(2,1)} %add_convert_fusion), calls=%async_computation.1 | async-start | bytes 524288 | tf_op jit(solution)/shard_map/all_to_all | solution.py:244
  42.4 0.0 collective-permute-done.11
  42.4 0.0 collective-permute-done.10
  42.5 0.0 collective-permute-done.9
  42.5 2.1 %collective-permute-start.12 = (f32[32,256]{1,0:T(8,128)S(1)}, f32[32,256]{1,0:T(8,128)S(1)}, u32[]{:S(2)}, u32[]{:S(2)}) collective-permute-start(f32[32,256]{1,0:T(8,128)S(1)} %add_add_fusion), channel_id=1, source_target_pairs={{0,4},{4,0},{8,12},{12,8},{16,20},{20,16},{24,28},{28,24},{1,5},{5... | collective-permute-start | bytes 98312 | tf_op jit(solution)/shard_map/ppermute | solution.py:314
  44.6 0.0 collective-permute-start.6
  44.6 1.1 %collective-permute-start.7 = (bf16[64,512]{1,0:T(8,128)(2,1)S(1)}, bf16[64,512]{1,0:T(8,128)(2,1)S(1)}, u32[]{:S(2)}, u32[]{:S(2)}) collective-permute-start(bf16[64,512]{1,0:T(8,128)(2,1)S(1)} %get-tuple-element.34), channel_id=1, source_target_pairs={{0,2},{1,3},{2,0},{3,1},{4,6},{5,7},{6,4},{7,5},{8,10},{9,11},{10,... | collective-permute-start | bytes 196616 | tf_op jit(solution)/shard_map/ppermute | solution.py:241
  45.7 0.7 %collective-permute-start.8 = (bf16[64,512]{1,0:T(8,128)(2,1)S(1)}, bf16[64,512]{1,0:T(8,128)(2,1)S(1)}, u32[]{:S(2)}, u32[]{:S(2)}) collective-permute-start(bf16[64,512]{1,0:T(8,128)(2,1)S(1)} %get-tuple-element.35), channel_id=1, source_target_pairs={{0,3},{1,2},{2,1},{3,0},{4,7},{5,6},{6,5},{7,4},{8,11},{9,10},{10,... | collective-permute-start | bytes 196616 | tf_op jit(solution)/shard_map/ppermute | solution.py:241
  46.4 0.8 %collective-permute-done.12 = f32[32,256]{1,0:T(8,128)S(1)} collective-permute-done((f32[32,256]{1,0:T(8,128)S(1)}, f32[32,256]{1,0:T(8,128)S(1)}, u32[]{:S(2)}, u32[]{:S(2)}) %collective-permute-start.12) | collective-permute-done | bytes 32800 | tf_op jit(solution)/shard_map/ppermute | solution.py:314
  47.3 1.2 %collective-permute-start.13 = (f32[32,256]{1,0:T(8,128)S(1)}, f32[32,256]{1,0:T(8,128)S(1)}, u32[]{:S(2)}, u32[]{:S(2)}) collective-permute-start(f32[32,256]{1,0:T(8,128)S(1)} %add.24), channel_id=1, source_target_pairs={{0,8},{4,12},{8,0},{12,4},{16,24},{20,28},{24,16},{28,20},{1,9},{5... | collective-permute-start | bytes 98312 | tf_op jit(solution)/shard_map/ppermute | solution.py:314
  48.5 0.0 collective-permute-start.16
  48.5 2.7 %collective-permute-done.13 = f32[32,256]{1,0:T(8,128)S(1)} collective-permute-done((f32[32,256]{1,0:T(8,128)S(1)}, f32[32,256]{1,0:T(8,128)S(1)}, u32[]{:S(2)}, u32[]{:S(2)}) %collective-permute-start.13) | collective-permute-done | bytes 32800 | tf_op jit(solution)/shard_map/ppermute | solution.py:314
  51.2 3.5 %collective-permute-start.14 = (f32[32,256]{1,0:T(8,128)S(1)}, f32[32,256]{1,0:T(8,128)S(1)}, u32[]{:S(2)}, u32[]{:S(2)}) collective-permute-start(f32[32,256]{1,0:T(8,128)S(1)} %add.25), channel_id=1, source_target_pairs={{0,16},{4,20},{8,24},{12,28},{16,0},{20,4},{24,8},{28,12},{1,17},{... | collective-permute-start | bytes 98312 | tf_op jit(solution)/shard_map/ppermute | solution.py:314
  54.7 0.0 collective-permute-done.6.p1
  54.7 0.0 collective-permute-done.7.p2
  54.7 0.0 collective-permute-done.8.p3
  54.7 0.7 %shard_map.83 = bf16[64,2048]{1,0:T(8,128)(2,1)} custom-call(bf16[64,512]{1,0:T(8,128)(2,1)S(1)} %get-tuple-element.32.p0, bf16[64,512]{1,0:T(8,128)(2,1)S(1)} %collective-permute-done.6.p1, bf16[64,512]{1,0:T(8,128)(2,1)S(1)} %collective-permute-done.7.p2, bf16[64,512]{1,0:T(8,128)(2,1)S(1)} %collective-permute-done.8.p3), custom_call_target="tpu_custom_call" | custom-call | flops 1000000 | bytes 262144 | tf_op jit(solution)/shard_map/pallas_call | solution.py:24
  55.4 1.1 %collective-permute-done.14 = f32[32,256]{1,0:T(8,128)S(1)} collective-permute-done((f32[32,256]{1,0:T(8,128)S(1)}, f32[32,256]{1,0:T(8,128)S(1)}, u32[]{:S(2)}, u32[]{:S(2)}) %collective-permute-start.14) | collective-permute-done | bytes 32800 | tf_op jit(solution)/shard_map/ppermute | solution.py:314
  56.6 0.6 %add_multiply_fusion = f32[32,256]{1,0:T(8,128)} fusion(f32[32,256]{1,0:T(8,128)S(1)} %add.25, f32[32,256]{1,0:T(8,128)S(1)} %collective-permute-done.14), kind=kLoop, calls=%fused_computation.1 | loop fusion | flops 16384 | bytes 98304 | tf_op jit(solution)/shard_map/mul | solution.py:316
  57.2 0.0 collective-permute-done.16.came
  57.2 0.0 all-to-all-done.1.back
  57.2 1.5 %shard_map.86 = f32[32,2048]{1,0:T(8,128)} custom-call(s32[8,128]{1,0:T(8,128)S(1)} %get-tuple-element.40.sel, f32[32,2048]{1,0:T(8,128)S(1)} %get-tuple-element.43.own, f32[32,2048]{1,0:T(8,128)S(1)} %collective-permute-done.16.came, bf16[8,4,32,128]{3,2,1,0:T(8,128)(2,1)S(1)} %all-to-all-done.1.back), custom_call_target="tpu_custom_call" | custom-call | flops 1000000 | bytes 790528 | tf_op jit(solution)/shard_map/pallas_call | solution.py:24
  (3 shorter events, 0.0 us)
Async XLA Ops:
  0.6 0.7 %copy-start.1 = (s32[128,16]{0,1:T(8,128)S(1)}, s32[128,16]{0,1:T(8,128)}, u32[]{:S(2)}) copy-start(s32[128,16]{0,1:T(8,128)} %param.6) | copy-start | bytes 24580
  18.4 4.8 %collective-permute-start.1 = (bf16[8,4,32,128]{3,2,1,0:T(8,128)(2,1)S(1)}, bf16[8,4,32,128]{3,2,1,0:T(8,128)(2,1)S(1)}, u32[]{:S(2)}, u32[]{:S(2)}) collective-permute-start(bf16[8,4,32,128]{3,2,1,0:T(8,128)(2,1)S(1)} %all_to_all.10.got), channel_id=1, source_target_pairs={{0,1},{1,0},{2,3},{3,2},{4,5},{5,4},{6,7},{7,6},{8,9},{9,8},{10,11... | collective-permute-start | bytes 786440 | tf_op jit(solution)/shard_map/ppermute | solution.py:241
  18.4 4.8 %collective-permute-start = (bf16[32,2048]{1,0:T(8,128)(2,1)S(1)}, bf16[32,2048]{1,0:T(8,128)(2,1)S(1)}, u32[]{:S(2)}, u32[]{:S(2)}) collective-permute-start(bf16[32,2048]{1,0:T(8,128)(2,1)S(1)} %get-tuple-element.25.mine), channel_id=1, source_target_pairs={{0,1},{1,0},{2,3},{3,2},{4,5},{5,4},{6,7},{7,6},{8,9},{9,8},{10,11... | collective-permute-start | bytes 393224 | tf_op jit(solution)/shard_map/ppermute | solution.py:241
  20.6 8.8 %collective-permute-start.3 = (bf16[64,512]{1,0:T(8,128)(2,1)S(1)}, bf16[64,512]{1,0:T(8,128)(2,1)S(1)}, u32[]{:S(2)}, u32[]{:S(2)}) collective-permute-start(bf16[64,512]{1,0:T(8,128)(2,1)S(1)} %get-tuple-element.29), channel_id=1, source_target_pairs={{0,1},{1,0},{2,3},{3,2},{4,5},{5,4},{6,7},{7,6},{8,9},{9,8},{10,11... | collective-permute-start | bytes 196616 | tf_op jit(solution)/shard_map/ppermute | solution.py:241
  20.7 8.8 %collective-permute-start.4 = (bf16[64,512]{1,0:T(8,128)(2,1)S(1)}, bf16[64,512]{1,0:T(8,128)(2,1)S(1)}, u32[]{:S(2)}, u32[]{:S(2)}) collective-permute-start(bf16[64,512]{1,0:T(8,128)(2,1)S(1)} %get-tuple-element.30), channel_id=1, source_target_pairs={{0,2},{1,3},{2,0},{3,1},{4,6},{5,7},{6,4},{7,5},{8,10},{9,11},{10,... | collective-permute-start | bytes 196616 | tf_op jit(solution)/shard_map/ppermute | solution.py:241
  22.2 7.2 %collective-permute-start.5 = (bf16[64,512]{1,0:T(8,128)(2,1)S(1)}, bf16[64,512]{1,0:T(8,128)(2,1)S(1)}, u32[]{:S(2)}, u32[]{:S(2)}) collective-permute-start(bf16[64,512]{1,0:T(8,128)(2,1)S(1)} %get-tuple-element.31), channel_id=1, source_target_pairs={{0,3},{1,2},{2,1},{3,0},{4,7},{5,6},{6,5},{7,4},{8,11},{9,10},{10,... | collective-permute-start | bytes 196616 | tf_op jit(solution)/shard_map/ppermute | solution.py:241
  24.7 4.8 %collective-permute-start.2 = (bf16[64,512]{1,0:T(8,128)(2,1)S(1)}, bf16[64,512]{1,0:T(8,128)(2,1)S(1)}, u32[]{:S(2)}, u32[]{:S(2)}) collective-permute-start(bf16[64,512]{1,0:T(8,128)(2,1)S(1)} %shard_map.81), channel_id=1, source_target_pairs={{0,2},{1,3},{2,0},{3,1},{4,6},{5,7},{6,4},{7,5},{8,10},{9,11},{10,... | collective-permute-start | bytes 196616 | tf_op jit(solution)/shard_map/ppermute | solution.py:241
  27.9 1.6 %copy-start = (bf16[128,256]{1,0:T(8,128)(2,1)S(1)}, bf16[128,256]{1,0:T(8,128)(2,1)}, u32[]{:S(2)}) copy-start(bf16[128,256]{1,0:T(8,128)(2,1)} %w_ref.1) | copy-start | bytes 196612
  30.1 4.3 %collective-permute-start.15 = (bf16[64,512]{1,0:T(8,128)(2,1)S(1)}, bf16[64,512]{1,0:T(8,128)(2,1)S(1)}, u32[]{:S(2)}, u32[]{:S(2)}) collective-permute-start(bf16[64,512]{1,0:T(8,128)(2,1)S(1)} %get-tuple-element.41), channel_id=1, source_target_pairs={{0,2},{1,3},{2,0},{3,1},{4,6},{5,7},{6,4},{7,5},{8,10},{9,11},{10,... | collective-permute-start | bytes 196616 | tf_op jit(solution)/shard_map/ppermute | solution.py:241
  35.9 2.2 %collective-permute-start.17 = (bf16[8,4,32,128]{3,2,1,0:T(8,128)(2,1)S(1)}, bf16[8,4,32,128]{3,2,1,0:T(8,128)(2,1)S(1)}, u32[]{:S(2)}, u32[]{:S(2)}) collective-permute-start(bf16[8,4,32,128]{3,2,1,0:T(8,128)(2,1)S(1)} %get-tuple-element.46), channel_id=1, source_target_pairs={{0,1},{1,0},{2,3},{3,2},{4,5},{5,4},{6,7},{7,6},{8,9},{9,8},{10,11... | collective-permute-start | bytes 786440 | tf_op jit(solution)/shard_map/ppermute | solution.py:241
  35.9 6.5 %collective-permute-start.11 = (f32[32,256]{1,0:T(8,128)S(1)}, f32[32,256]{1,0:T(8,128)S(1)}, u32[]{:S(2)}, u32[]{:S(2)}) collective-permute-start(f32[32,256]{1,0:T(8,128)S(1)} %get-tuple-element.39), channel_id=1, source_target_pairs={{0,3},{1,2},{2,1},{3,0},{4,7},{5,6},{6,5},{7,4},{8,11},{9,10},{10,... | collective-permute-start | bytes 98312 | tf_op jit(solution)/shard_map/ppermute | solution.py:241
  37.2 5.3 %collective-permute-start.10 = (f32[32,256]{1,0:T(8,128)S(1)}, f32[32,256]{1,0:T(8,128)S(1)}, u32[]{:S(2)}, u32[]{:S(2)}) collective-permute-start(f32[32,256]{1,0:T(8,128)S(1)} %get-tuple-element.38), channel_id=1, source_target_pairs={{0,2},{1,3},{2,0},{3,1},{4,6},{5,7},{6,4},{7,5},{8,10},{9,11},{10,... | collective-permute-start | bytes 98312 | tf_op jit(solution)/shard_map/ppermute | solution.py:241
  38.1 4.4 %collective-permute-start.9 = (f32[32,256]{1,0:T(8,128)S(1)}, f32[32,256]{1,0:T(8,128)S(1)}, u32[]{:S(2)}, u32[]{:S(2)}) collective-permute-start(f32[32,256]{1,0:T(8,128)S(1)} %get-tuple-element.37), channel_id=1, source_target_pairs={{0,1},{1,0},{2,3},{3,2},{4,5},{5,4},{6,7},{7,6},{8,9},{9,8},{10,11... | collective-permute-start | bytes 98312 | tf_op jit(solution)/shard_map/ppermute | solution.py:241
  38.8 18.3 %all-to-all-start.1 = ((bf16[8,4,32,128]{3,2,1,0:T(8,128)(2,1)}), bf16[8,4,32,128]{3,2,1,0:T(8,128)(2,1)S(1)}, u32[]{:S(2)}, u32[]{:S(2)}) async-start(bf16[8,4,32,128]{3,2,1,0:T(8,128)(2,1)} %add_convert_fusion), calls=%async_computation.1 | async-start | bytes 524288 | tf_op jit(solution)/shard_map/all_to_all | solution.py:244
  42.5 4.8 %collective-permute-start.12 = (f32[32,256]{1,0:T(8,128)S(1)}, f32[32,256]{1,0:T(8,128)S(1)}, u32[]{:S(2)}, u32[]{:S(2)}) collective-permute-start(f32[32,256]{1,0:T(8,128)S(1)} %add_add_fusion), channel_id=1, source_target_pairs={{0,4},{4,0},{8,12},{12,8},{16,20},{20,16},{24,28},{28,24},{1,5},{5... | collective-permute-start | bytes 98312 | tf_op jit(solution)/shard_map/ppermute | solution.py:314
  44.6 10.1 %collective-permute-start.6 = (bf16[64,512]{1,0:T(8,128)(2,1)S(1)}, bf16[64,512]{1,0:T(8,128)(2,1)S(1)}, u32[]{:S(2)}, u32[]{:S(2)}) collective-permute-start(bf16[64,512]{1,0:T(8,128)(2,1)S(1)} %get-tuple-element.33), channel_id=1, source_target_pairs={{0,1},{1,0},{2,3},{3,2},{4,5},{5,4},{6,7},{7,6},{8,9},{9,8},{10,11... | collective-permute-start | bytes 196616 | tf_op jit(solution)/shard_map/ppermute | solution.py:241
  44.6 10.1 %collective-permute-start.7 = (bf16[64,512]{1,0:T(8,128)(2,1)S(1)}, bf16[64,512]{1,0:T(8,128)(2,1)S(1)}, u32[]{:S(2)}, u32[]{:S(2)}) collective-permute-start(bf16[64,512]{1,0:T(8,128)(2,1)S(1)} %get-tuple-element.34), channel_id=1, source_target_pairs={{0,2},{1,3},{2,0},{3,1},{4,6},{5,7},{6,4},{7,5},{8,10},{9,11},{10,... | collective-permute-start | bytes 196616 | tf_op jit(solution)/shard_map/ppermute | solution.py:241
  45.7 9.0 %collective-permute-start.8 = (bf16[64,512]{1,0:T(8,128)(2,1)S(1)}, bf16[64,512]{1,0:T(8,128)(2,1)S(1)}, u32[]{:S(2)}, u32[]{:S(2)}) collective-permute-start(bf16[64,512]{1,0:T(8,128)(2,1)S(1)} %get-tuple-element.35), channel_id=1, source_target_pairs={{0,3},{1,2},{2,1},{3,0},{4,7},{5,6},{6,5},{7,4},{8,11},{9,10},{10,... | collective-permute-start | bytes 196616 | tf_op jit(solution)/shard_map/ppermute | solution.py:241
  47.3 3.9 %collective-permute-start.13 = (f32[32,256]{1,0:T(8,128)S(1)}, f32[32,256]{1,0:T(8,128)S(1)}, u32[]{:S(2)}, u32[]{:S(2)}) collective-permute-start(f32[32,256]{1,0:T(8,128)S(1)} %add.24), channel_id=1, source_target_pairs={{0,8},{4,12},{8,0},{12,4},{16,24},{20,28},{24,16},{28,20},{1,9},{5... | collective-permute-start | bytes 98312 | tf_op jit(solution)/shard_map/ppermute | solution.py:314
  48.5 8.7 %collective-permute-start.16 = (f32[32,2048]{1,0:T(8,128)S(1)}, f32[32,2048]{1,0:T(8,128)S(1)}, u32[]{:S(2)}, u32[]{:S(2)}) collective-permute-start(f32[32,2048]{1,0:T(8,128)S(1)} %get-tuple-element.44), channel_id=1, source_target_pairs={{0,1},{1,0},{2,3},{3,2},{4,5},{5,4},{6,7},{7,6},{8,9},{9,8},{10,11... | collective-permute-start | bytes 786440 | tf_op jit(solution)/shard_map/ppermute | solution.py:241
  51.2 5.4 %collective-permute-start.14 = (f32[32,256]{1,0:T(8,128)S(1)}, f32[32,256]{1,0:T(8,128)S(1)}, u32[]{:S(2)}, u32[]{:S(2)}) collective-permute-start(f32[32,256]{1,0:T(8,128)S(1)} %add.25), channel_id=1, source_target_pairs={{0,16},{4,20},{8,24},{12,28},{16,0},{20,4},{24,8},{28,12},{1,17},{... | collective-permute-start | bytes 98312 | tf_op jit(solution)/shard_map/ppermute | solution.py:314

commit v2 on v1

--- a/solution.py
+++ b/solution.py
@@ -47,13 +47,16 @@
     return pl.ds(pl.multiple_of(start * size, size), size)
 
 
-def choose_kernel(adj_ref, feats, sel, copied, sends, sel_s, sems):
+def choose_kernel(adj_hbm, feats, sel, copied, adj_ref, sends, sel_s, sems):
+    names = pltpu.make_async_copy(adj_hbm, adj_ref, sems.at[2])
+    names.start()
     copy = pltpu.make_async_copy(feats, copied, sems.at[0])
     copy.start()
     slots_n, ids_n = adj_ref.shape
     tile = sends.shape[3]
     blk = feats.shape[1] // tile
     r, _, _ = position()
+    names.wait()
     adj = adj_ref[...]
     mine = r * blk + iota((blk, ids_n), 0)
     hits = jnp.zeros((blk, ids_n), F32)
@@ -210,12 +213,31 @@
         own_send[:, b * tile : (b + 1) * tile] = acc[b, low, :]
 
 
-def collect_kernel(sel, own, came, back, out):
-    tile = back.shape[3]
+def total_kernel(stay, came, w0, w1, w2, w3, out):
+    f, tile = stay.shape[2], stay.shape[3]
+    part = ((w0[...] + w1[...]) + (w2[...] + w3[...])).astype(BF16)
+    for d in range(stay.shape[0]):
+        for o in range(CAP):
+            out[d, o * f : (o + 1) * f, :] = (stay[d, o] + came[d, o].astype(F32)).astype(BF16)
+        for h in range(part.shape[1] // tile):
+            at = (CAP + h) * f
+            out[d, at : at + f, :] = part[:, h * tile : (h + 1) * tile]
+
+
+def collect_kernel(scale, sel, own, came, back, out, wg):
+    tile = back.shape[2]
+    f = own.shape[0]
     out[...] = own[...] + came[...]
     for d in range(back.shape[0]):
         for o in range(CAP):
-            out[:, rows_at(sel[o, d], tile)] += back[d, o].astype(F32)
+            term = back[d, o * f : (o + 1) * f, :].astype(F32)
+            out[:, rows_at(sel[o, d], tile)] += term
+    for h in range(wg.shape[1] // tile):
+        at = (CAP + h) * f
+        total = back[0, at : at + f, :].astype(F32)
+        for d in range(1, back.shape[0]):
+            total = total + back[d, at : at + f, :].astype(F32)
+        wg[:, h * tile : (h + 1) * tile] = total * scale
 
 
 def place_kernel(p0, p1, p2, p3, out):
@@ -247,10 +269,11 @@
     in_hbm = functools.partial(pltpu.with_memory_space_constraint, memory_space=pltpu.HBM)
     part = (rows_n, CAP, f, tile)
     piece = ((units_loc, quarter), BF16)
-    sel, feats, sends = call(
-        choose_kernel, [VMEM, HBM],
-        [((8, LANES), I32), ((f, nodes), BF16), (part, BF16)], [adj_t, in_hbm(feats_t)],
-        [pltpu.SMEM((8, LANES), I32), pltpu.SemaphoreType.DMA((2,))], mib=big,
+    sel, feats, adj, sends = call(
+        choose_kernel, [HBM, HBM],
+        [((8, LANES), I32), ((f, nodes), BF16), (adj_t.shape, I32), (part, BF16)],
+        [in_hbm(adj_t), in_hbm(feats_t)],
+        [pltpu.SMEM((8, LANES), I32), pltpu.SemaphoreType.DMA((3,))], mib=big,
     )
     feats_mate = mate(feats, 1)
     got = over_rows(sends)
@@ -273,7 +296,7 @@
     )
     slot = call(
         functools.partial(slot_kernel, blk), [VMEM],
-        ((slots_n, LANES), I32), [adj_t], mib=big,
+        ((slots_n, LANES), I32), [adj], mib=big,
     )
     cots = [cots[0]] + [mate(cots[q], q) for q in (1, 2, 3)]
     got_mate = mate(got, 1)
@@ -308,12 +331,7 @@
         6 * f_in * units * quarter, 12,
     )
     g_came = mate(g_send, 2)
-    wg = w0 + mate(w1, 1) + mate(w2, 2) + mate(w3, 3)
-    bit = 0
-    while 1 << bit < rows_n:
-        wg = wg + lax.ppermute(wg, "rows", [(i, i ^ (1 << bit)) for i in range(rows_n)])
-        bit += 1
-    weight_grad = wg * (1.0 / math.sqrt(nodes * rows_n))
+    wgs = [w0, mate(w1, 1), mate(w2, 2), mate(w3, 3)]
 
     acc = call(
         functools.partial(spread_first_kernel, near), [SMEM, VMEM, VMEM],
@@ -324,12 +342,15 @@
         [((f, nodes), F32)] * 2 + [(part, F32), (part, BF16)],
         [slot, a_far, g_came, acc], [pltpu.VMEM((table_n, fx, tile), F32)], a_flops, big + 8,
     )
-    total = (stay + mate(send, 1).astype(F32)).astype(BF16)
     own_came = mate(own_send, 1)
-    back = over_rows(total)
-    feat_grad = call(
-        collect_kernel, [SMEM, VMEM, VMEM, VMEM], ((f, nodes), F32),
-        [sel, own, own_came, back], mib=big, out=True,
+    total = call(
+        total_kernel, [VMEM] * 6, ((rows_n, CAP * f + f * units // tile, tile), BF16),
+        [stay, mate(send, 1), *wgs], mib=big,
+    )
+    feat_grad, weight_grad = call(
+        functools.partial(collect_kernel, 1.0 / math.sqrt(nodes * rows_n)),
+        [SMEM, VMEM, VMEM, VMEM], [((f, nodes), F32), wg_part],
+        [sel, own, own_came, over_rows(total)], mib=big, out=True,
     )
 
     outs = [outs[0]] + [mate(outs[q], q) for q in (1, 2, 3)]

time: 59.1 us -> 59.5 us (level)
  waiting for transfers between devices: 6.55 us -> 14.6 us
  starting transfers between devices: 19.6 us -> 12.7 us
  other arithmetic: 1.42 us -> 0 us
  Pallas kernels: 13.6 us -> 15 us
  local copies, waits for them, and re-layouts: 0.7 us -> 0.01 us
    ppermute x15, waiting for transfers between devices: 1.88 us -> 9.12 us  [mate(): return lax.ppermute(v, 'cols', [(i, i ^ q) for i in range(cols_n)])]
    ppermute x3 -> x0, starting transfers between devices: 6.78 us -> none  [layer(): lax.ppermute(wg, 'rows', [(i, i ^ 1 << bit) for i in range(rows_n)])]
    all_to_all x1, waiting for transfers between devices: 0.01 us -> 5.47 us  [over_rows(): return lax.all_to_all(v, 'rows', 0, 0, tiled=True)]
    ppermute x3 -> x0, waiting for transfers between devices: 4.66 us -> none  [layer(): lax.ppermute(wg, 'rows', [(i, i ^ 1 << bit) for i in range(rows_n)])]
    pallas_call x11 -> x12, Pallas kernels: 13.6 us -> 15 us  [call(): pl.pallas_call(kernel, out_shape=[place(s, d) for s, d in outs] if isinst...]
    convert_element_type x1 -> x0, other arithmetic: 0.78 us -> none  [layer(): total = (stay + mate(send, 1).astype(F32)).astype(BF16)]
    unnamed x4 -> x2, local copies, waits for them, and re-layouts: 0.7 us -> 0.01 us
    mul x1 -> x0, other arithmetic: 0.62 us -> none  [layer(): weight_grad = wg * (1.0 / math.sqrt(nodes * rows_n))]
  transfers between devices with their start and end apart: 19 -> 16, of which waited for: 4 -> 6; matrix products, arithmetic and copies ran while one was open for 2% -> 0% of each run, Pallas kernels for 15% -> 15%
where the time goes in v2:
time: 59.5 us; the launch traced here: 59.2 us
  blocking collectives  16 us (27%)
  Pallas kernels  15 us (25%)
  waiting for transfers between devices  14.6 us (25%)
  starting transfers between devices  12.7 us (21%)
  between operations  0.78 us (1%)
    all_to_all x1, blocking collectives, over_rows(): return lax.all_to_all(v, 'rows', 0, 0, tiled=True)  16 us
    pallas_call x12, Pallas kernels, call(): pl.pallas_call(kernel, out_shape=[place(s, d) for s, d in outs] if isinst...  15 us
    ppermute x15, starting transfers between devices, mate(): return lax.ppermute(v, 'cols', [(i, i ^ q) for i in range(cols_n)])  9.12 us
    ppermute x15, waiting for transfers between devices, mate(): return lax.ppermute(v, 'cols', [(i, i ^ q) for i in range(cols_n)])  9.12 us
    all_to_all x1, waiting for transfers between devices, over_rows(): return lax.all_to_all(v, 'rows', 0, 0, tiled=True)  5.47 us
    all_to_all x1, starting transfers between devices, over_rows(): return lax.all_to_all(v, 'rows', 0, 0, tiled=True)  3.59 us
  transfers between devices with their start and end apart: 16, of which 6 were waited for; matrix products, arithmetic and copies ran while one was open for 0% of the time, Pallas kernels for 15%

profile of v2, /device:TPU:0, one launch (start us, length us, event | category | flops | bytes accessed | tf_op | source)
XLA Modules:
  0.0 59.2 jit_solution(1918903635248351028)
XLA Ops:
  0.6 1.7 %shard_map.76 = (s32[8,128]{1,0:T(8,128)S(1)}, bf16[32,2048]{1,0:T(8,128)(2,1)S(1)}, s32[16,128]{1,0:T(8,128)S(1)}, bf16[8,4,32,128]{3,2,1,0:T(8,128)(2,1)S(1)}) custom-call(s32[16,128]{1,0:T(8,128)} %bitcast.1, bf16[32,2048]{1,0:T(8,128)(2,1)} %feats.1), custom_call_target="tpu_custom_call" | custom-call | flops 1000000 | bytes 139264 | tf_op jit(solution)/shard_map/pallas_call | solution.py:24
  2.3 16.0 %all_to_all.10.got = bf16[8,4,32,128]{3,2,1,0:T(8,128)(2,1)S(1)} all-to-all(bf16[8,4,32,128]{3,2,1,0:T(8,128)(2,1)S(1)} %get-tuple-element.30), channel_id=1, replica_groups=mesh['rows'=8,'cols'=4] {'rows'}, dimensions={0} | all-to-all | bytes 524288 | tf_op jit(solution)/shard_map/all_to_all | solution.py:266
  18.3 0.0 collective-permute-start.1
  18.3 0.5 collective-permute-start
  18.8 1.7 %shard_map.80 = (bf16[4,16,128,128]{3,2,1,0:T(8,128)(2,1)S(1)}, bf16[64,512]{1,0:T(8,128)(2,1)S(1)}, bf16[64,512]{1,0:T(8,128)(2,1)S(1)}, bf16[64,512]{1,0:T(8,128)(2,1)S(1)}, bf16[64,512]{1,0:T(8,128)(2,1)S(1)}) custom-call(bf16[16,16,128,128]{3,2,1,0:T(8,128)(2,1)} %a_hbm.3, bf16[64,2048]{1,0:T(8,128)(2,1)} %rest_0_.1), custom_call_target="tpu_custom_call" | custom-call | flops 1000000 | bytes 8650752 | tf_op jit(solution)/shard_map/pallas_call | solution.py:24
  20.6 0.1 collective-permute-start.3
  20.7 1.6 %collective-permute-start.4 = (bf16[64,512]{1,0:T(8,128)(2,1)S(1)}, bf16[64,512]{1,0:T(8,128)(2,1)S(1)}, u32[]{:S(2)}, u32[]{:S(2)}) collective-permute-start(bf16[64,512]{1,0:T(8,128)(2,1)S(1)} %get-tuple-element.34), channel_id=1, source_target_pairs={{0,2},{1,3},{2,0},{3,1},{4,6},{5,7},{6,4},{7,5},{8,10},{9,11},{10,... | collective-permute-start | bytes 196616 | tf_op jit(solution)/shard_map/ppermute | solution.py:263
  22.2 0.3 collective-permute-start.5
  22.5 0.6 %shard_map.77.slot = s32[16,128]{1,0:T(8,128)S(1)} custom-call(s32[16,128]{1,0:T(8,128)S(1)} %get-tuple-element.28.adj_ref), custom_call_target="tpu_custom_call" | custom-call | flops 1000000 | bytes 8192 | tf_op jit(solution)/shard_map/pallas_call | solution.py:24
  23.1 0.0 collective-permute-done.mate
  23.1 0.0 collective-permute-done.1.got_mate
  23.1 1.6 %shard_map.81 = bf16[64,512]{1,0:T(8,128)(2,1)S(1)} custom-call(s32[16,128]{1,0:T(8,128)S(1)} %shard_map.77.slot, bf16[4,16,128,128]{3,2,1,0:T(8,128)(2,1)S(1)} %get-tuple-element.31.a_side, bf16[32,2048]{1,0:T(8,128)(2,1)S(1)} %get-tuple-element.29.mine, bf16[32,2048]{1,0:T(8,128)(2,1)S(1)} %collective-permute-done.mate, ...), custom_call_target="tpu_custom_call" | custom-call | flops 134217728 | bytes 2891776 | tf_op jit(solution)/shard_map/pallas_call | solution.py:24
  24.7 1.6 %collective-permute-start.2 = (bf16[64,512]{1,0:T(8,128)(2,1)S(1)}, bf16[64,512]{1,0:T(8,128)(2,1)S(1)}, u32[]{:S(2)}, u32[]{:S(2)}) collective-permute-start(bf16[64,512]{1,0:T(8,128)(2,1)S(1)} %shard_map.81), channel_id=1, source_target_pairs={{0,2},{1,3},{2,0},{3,1},{4,6},{5,7},{6,4},{7,5},{8,10},{9,11},{10,... | collective-permute-start | bytes 196616 | tf_op jit(solution)/shard_map/ppermute | solution.py:263
  26.2 1.6 %shard_map.78.a_side = bf16[4,16,128,128]{3,2,1,0:T(8,128)(2,1)S(1)} custom-call(bf16[16,16,128,128]{3,2,1,0:T(8,128)(2,1)} %a_hbm.3), custom_call_target="tpu_custom_call" | custom-call | flops 1000000 | bytes 8388608 | tf_op jit(solution)/shard_map/pallas_call | solution.py:24
  27.8 0.0 copy-start
  27.9 1.6 %shard_map.79.keep = bf16[64,512]{1,0:T(8,128)(2,1)S(1)} custom-call(s32[16,128]{1,0:T(8,128)S(1)} %shard_map.77.slot, bf16[4,16,128,128]{3,2,1,0:T(8,128)(2,1)S(1)} %shard_map.78.a_side, bf16[32,2048]{1,0:T(8,128)(2,1)S(1)} %get-tuple-element.29.mine, bf16[32,2048]{1,0:T(8,128)(2,1)S(1)} %collective-permute-done.mate, ...), custom_call_target="tpu_custom_call" | custom-call | flops 134217728 | bytes 2891776 | tf_op jit(solution)/shard_map/pallas_call | solution.py:24
  29.4 0.0 collective-permute-done.3.c1
  29.4 0.0 collective-permute-done.4.c2
  29.4 0.0 collective-permute-done.5.c3
  29.4 0.0 collective-permute-done.2.came
  29.5 0.0 copy-done
  29.5 0.6 %shard_map.82 = (bf16[64,512]{1,0:T(8,128)(2,1)S(1)}, bf16[64,512]{1,0:T(8,128)(2,1)S(1)}, bf16[64,512]{1,0:T(8,128)(2,1)S(1)}, bf16[64,512]{1,0:T(8,128)(2,1)S(...) custom-call(bf16[64,512]{1,0:T(8,128)(2,1)S(1)} %shard_map.79.keep, ...), custom_call_target="tpu_custom_call" | custom-call | flops 100663296 | bytes 458752 | tf_op jit(solution)/shard_map/pallas_call | solution.py:24
  30.1 1.2 %collective-permute-start.9 = (bf16[64,512]{1,0:T(8,128)(2,1)S(1)}, bf16[64,512]{1,0:T(8,128)(2,1)S(1)}, u32[]{:S(2)}, u32[]{:S(2)}) collective-permute-start(bf16[64,512]{1,0:T(8,128)(2,1)S(1)} %get-tuple-element.41), channel_id=1, source_target_pairs={{0,2},{1,3},{2,0},{3,1},{4,6},{5,7},{6,4},{7,5},{8,10},{9,11},{10,... | collective-permute-start | bytes 196616 | tf_op jit(solution)/shard_map/ppermute | solution.py:263
  31.3 1.3 %shard_map.84.before = f32[48,64,128]{2,1,0:T(8,128)S(1)} custom-call(s32[16,128]{1,0:T(8,128)S(1)} %shard_map.77.slot, bf16[4,16,128,128]{3,2,1,0:T(8,128)(2,1)S(1)} %shard_map.78.a_side, bf16[64,512]{1,0:T(8,128)(2,1)S(1)} %get-tuple-element.42.g_ref), custom_call_target="tpu_custom_call" | custom-call | flops 134217728 | bytes 2170880 | tf_op jit(solution)/shard_map/pallas_call | solution.py:24
  32.6 1.8 %collective-permute-done.9.g_ref = bf16[64,512]{1,0:T(8,128)(2,1)S(1)} collective-permute-done((bf16[64,512]{1,0:T(8,128)(2,1)S(1)}, bf16[64,512]{1,0:T(8,128)(2,1)S(1)}, u32[]{:S(2)}, u32[]{:S(2)}) %collective-permute-start.9) | collective-permute-done | bytes 65568 | tf_op jit(solution)/shard_map/ppermute | solution.py:263
  34.4 1.4 %shard_map.85 = (f32[32,2048]{1,0:T(8,128)S(1)}, f32[32,2048]{1,0:T(8,128)S(1)}, f32[8,4,32,128]{3,2,1,0:T(8,128)S(1)}, bf16[8,4,32,128]{3,2,1,0:T(8,128)(2,1)S(1)}) custom-call(s32[16,128]{1,0:T(8,128)S(1)} %shard_map.77.slot, bf16[4,16,128,128]{3,2,1,0:T(8,128)(2,1)S(1)} %get-tuple-element.31.a_side, bf16[64,512]{1,0:T(8,128)(2,1)S(1)} %collective-permute-done.9.g_ref, ...), custom_call_target="tpu_custom_call" | custom-call | flops 134217728 | bytes 3743744 | tf_op jit(solution)/shard_map/pallas_call | solution.py:24
  35.8 0.1 collective-permute-start.11
  35.9 0.5 collective-permute-start.12
  36.4 1.1 %collective-permute-start.13 = (f32[32,256]{1,0:T(8,128)S(1)}, f32[32,256]{1,0:T(8,128)S(1)}, u32[]{:S(2)}, u32[]{:S(2)}) collective-permute-start(f32[32,256]{1,0:T(8,128)S(1)} %get-tuple-element.49), channel_id=1, source_target_pairs={{0,2},{1,3},{2,0},{3,1},{4,6},{5,7},{6,4},{7,5},{8,10},{9,11},{10,... | collective-permute-start | bytes 98312 | tf_op jit(solution)/shard_map/ppermute | solution.py:263
  37.5 0.3 collective-permute-start.14
  37.8 0.0 collective-permute-done.12.w1
  37.8 2.5 %collective-permute-done.13.w2 = f32[32,256]{1,0:T(8,128)S(1)} collective-permute-done((f32[32,256]{1,0:T(8,128)S(1)}, f32[32,256]{1,0:T(8,128)S(1)}, u32[]{:S(2)}, u32[]{:S(2)}) %collective-permute-start.13) | collective-permute-done | bytes 32800 | tf_op jit(solution)/shard_map/ppermute | solution.py:263
  40.3 0.9 %collective-permute-done.14.w3 = f32[32,256]{1,0:T(8,128)S(1)} collective-permute-done((f32[32,256]{1,0:T(8,128)S(1)}, f32[32,256]{1,0:T(8,128)S(1)}, u32[]{:S(2)}, u32[]{:S(2)}) %collective-permute-start.14) | collective-permute-done | bytes 32800 | tf_op jit(solution)/shard_map/ppermute | solution.py:263
  41.2 0.0 collective-permute-done.11.came
  41.2 0.8 %shard_map.86 = bf16[8,192,128]{2,1,0:T(8,128)(2,1)} custom-call(f32[8,4,32,128]{3,2,1,0:T(8,128)S(1)} %get-tuple-element.45.stay, bf16[8,4,32,128]{3,2,1,0:T(8,128)(2,1)S(1)} %collective-permute-done.11.came, f32[32,256]{1,0:T(8,128)S(1)} %get-tuple-element.47.w0, f32[32,256]{1,0:T(8,128)S(1)} %collective-permute-done.12.w1, ...), custom_call_target="tpu_custom_call" | custom-call | flops 1000000 | bytes 917504 | tf_op jit(solution)/shard_map/pallas_call | solution.py:24
  42.0 3.6 %all-to-all-start.1 = ((bf16[8,192,128]{2,1,0:T(8,128)(2,1)}), bf16[8,192,128]{2,1,0:T(8,128)(2,1)S(1)}, u32[]{:S(2)}, u32[]{:S(2)}) async-start(bf16[8,192,128]{2,1,0:T(8,128)(2,1)} %shard_map.86), calls=%async_computation.1 | async-start | bytes 786432 | tf_op jit(solution)/shard_map/all_to_all | solution.py:266
  45.6 0.0 collective-permute-start.10
  45.7 0.5 collective-permute-start.6
  46.1 0.9 %collective-permute-start.7 = (bf16[64,512]{1,0:T(8,128)(2,1)S(1)}, bf16[64,512]{1,0:T(8,128)(2,1)S(1)}, u32[]{:S(2)}, u32[]{:S(2)}) collective-permute-start(bf16[64,512]{1,0:T(8,128)(2,1)S(1)} %get-tuple-element.38), channel_id=1, source_target_pairs={{0,2},{1,3},{2,0},{3,1},{4,6},{5,7},{6,4},{7,5},{8,10},{9,11},{10,... | collective-permute-start | bytes 196616 | tf_op jit(solution)/shard_map/ppermute | solution.py:263
  47.0 0.5 collective-permute-start.8
  47.6 0.0 collective-permute-done.6.p1
  47.6 3.2 %collective-permute-done.7.p2 = bf16[64,512]{1,0:T(8,128)(2,1)S(1)} collective-permute-done((bf16[64,512]{1,0:T(8,128)(2,1)S(1)}, bf16[64,512]{1,0:T(8,128)(2,1)S(1)}, u32[]{:S(2)}, u32[]{:S(2)}) %collective-permute-start.7) | collective-permute-done | bytes 65568 | tf_op jit(solution)/shard_map/ppermute | solution.py:263
  50.8 0.7 %collective-permute-done.8.p3 = bf16[64,512]{1,0:T(8,128)(2,1)S(1)} collective-permute-done((bf16[64,512]{1,0:T(8,128)(2,1)S(1)}, bf16[64,512]{1,0:T(8,128)(2,1)S(1)}, u32[]{:S(2)}, u32[]{:S(2)}) %collective-permute-start.8) | collective-permute-done | bytes 65568 | tf_op jit(solution)/shard_map/ppermute | solution.py:263
  51.4 0.7 %shard_map.83 = bf16[64,2048]{1,0:T(8,128)(2,1)} custom-call(bf16[64,512]{1,0:T(8,128)(2,1)S(1)} %get-tuple-element.36.p0, bf16[64,512]{1,0:T(8,128)(2,1)S(1)} %collective-permute-done.6.p1, bf16[64,512]{1,0:T(8,128)(2,1)S(1)} %collective-permute-done.7.p2, bf16[64,512]{1,0:T(8,128)(2,1)S(1)} %collective-permute-done.8.p3), custom_call_target="tpu_custom_call" | custom-call | flops 1000000 | bytes 262144 | tf_op jit(solution)/shard_map/pallas_call | solution.py:24
  52.2 0.0 collective-permute-done.10.came
  52.2 5.5 %all-to-all-done.1.back = bf16[8,192,128]{2,1,0:T(8,128)(2,1)S(1)} async-done(((bf16[8,192,128]{2,1,0:T(8,128)(2,1)}), bf16[8,192,128]{2,1,0:T(8,128)(2,1)S(1)}, u32[]{:S(2)}, u32[]{:S(2)}) %all-to-all-start.1) | async-done | bytes 393248 | tf_op jit(solution)/shard_map/all_to_all | solution.py:266
  57.6 1.5 %shard_map.87 = (f32[32,2048]{1,0:T(8,128)}, f32[32,256]{1,0:T(8,128)}) custom-call(s32[8,128]{1,0:T(8,128)S(1)} %get-tuple-element.40.sel, f32[32,2048]{1,0:T(8,128)S(1)} %get-tuple-element.43.own, f32[32,2048]{1,0:T(8,128)S(1)} %collective-permute-done.10.came, bf16[8,192,128]{2,1,0:T(8,128)(2,1)S(1)} %all-to-all-done.1.back), custom_call_target="tpu_custom_call" | custom-call | flops 1000000 | bytes 921600 | tf_op jit(solution)/shard_map/pallas_call | solution.py:24
Async XLA Ops:
  18.3 4.8 %collective-permute-start.1 = (bf16[8,4,32,128]{3,2,1,0:T(8,128)(2,1)S(1)}, bf16[8,4,32,128]{3,2,1,0:T(8,128)(2,1)S(1)}, u32[]{:S(2)}, u32[]{:S(2)}) collective-permute-start(bf16[8,4,32,128]{3,2,1,0:T(8,128)(2,1)S(1)} %all_to_all.10.got), channel_id=1, source_target_pairs={{0,1},{1,0},{2,3},{3,2},{4,5},{5,4},{6,7},{7,6},{8,9},{9,8},{10,11... | collective-permute-start | bytes 786440 | tf_op jit(solution)/shard_map/ppermute | solution.py:263
  18.3 4.8 %collective-permute-start = (bf16[32,2048]{1,0:T(8,128)(2,1)S(1)}, bf16[32,2048]{1,0:T(8,128)(2,1)S(1)}, u32[]{:S(2)}, u32[]{:S(2)}) collective-permute-start(bf16[32,2048]{1,0:T(8,128)(2,1)S(1)} %get-tuple-element.29.mine), channel_id=1, source_target_pairs={{0,1},{1,0},{2,3},{3,2},{4,5},{5,4},{6,7},{7,6},{8,9},{9,8},{10,11... | collective-permute-start | bytes 393224 | tf_op jit(solution)/shard_map/ppermute | solution.py:263
  20.6 8.8 %collective-permute-start.3 = (bf16[64,512]{1,0:T(8,128)(2,1)S(1)}, bf16[64,512]{1,0:T(8,128)(2,1)S(1)}, u32[]{:S(2)}, u32[]{:S(2)}) collective-permute-start(bf16[64,512]{1,0:T(8,128)(2,1)S(1)} %get-tuple-element.33), channel_id=1, source_target_pairs={{0,1},{1,0},{2,3},{3,2},{4,5},{5,4},{6,7},{7,6},{8,9},{9,8},{10,11... | collective-permute-start | bytes 196616 | tf_op jit(solution)/shard_map/ppermute | solution.py:263
  20.7 8.8 %collective-permute-start.4 = (bf16[64,512]{1,0:T(8,128)(2,1)S(1)}, bf16[64,512]{1,0:T(8,128)(2,1)S(1)}, u32[]{:S(2)}, u32[]{:S(2)}) collective-permute-start(bf16[64,512]{1,0:T(8,128)(2,1)S(1)} %get-tuple-element.34), channel_id=1, source_target_pairs={{0,2},{1,3},{2,0},{3,1},{4,6},{5,7},{6,4},{7,5},{8,10},{9,11},{10,... | collective-permute-start | bytes 196616 | tf_op jit(solution)/shard_map/ppermute | solution.py:263
  22.2 7.2 %collective-permute-start.5 = (bf16[64,512]{1,0:T(8,128)(2,1)S(1)}, bf16[64,512]{1,0:T(8,128)(2,1)S(1)}, u32[]{:S(2)}, u32[]{:S(2)}) collective-permute-start(bf16[64,512]{1,0:T(8,128)(2,1)S(1)} %get-tuple-element.35), channel_id=1, source_target_pairs={{0,3},{1,2},{2,1},{3,0},{4,7},{5,6},{6,5},{7,4},{8,11},{9,10},{10,... | collective-permute-start | bytes 196616 | tf_op jit(solution)/shard_map/ppermute | solution.py:263
  24.7 4.8 %collective-permute-start.2 = (bf16[64,512]{1,0:T(8,128)(2,1)S(1)}, bf16[64,512]{1,0:T(8,128)(2,1)S(1)}, u32[]{:S(2)}, u32[]{:S(2)}) collective-permute-start(bf16[64,512]{1,0:T(8,128)(2,1)S(1)} %shard_map.81), channel_id=1, source_target_pairs={{0,2},{1,3},{2,0},{3,1},{4,6},{5,7},{6,4},{7,5},{8,10},{9,11},{10,... | collective-permute-start | bytes 196616 | tf_op jit(solution)/shard_map/ppermute | solution.py:263
  27.8 1.6 %copy-start = (bf16[128,256]{1,0:T(8,128)(2,1)S(1)}, bf16[128,256]{1,0:T(8,128)(2,1)}, u32[]{:S(2)}) copy-start(bf16[128,256]{1,0:T(8,128)(2,1)} %w_ref.1) | copy-start | bytes 196612
  30.1 4.3 %collective-permute-start.9 = (bf16[64,512]{1,0:T(8,128)(2,1)S(1)}, bf16[64,512]{1,0:T(8,128)(2,1)S(1)}, u32[]{:S(2)}, u32[]{:S(2)}) collective-permute-start(bf16[64,512]{1,0:T(8,128)(2,1)S(1)} %get-tuple-element.41), channel_id=1, source_target_pairs={{0,2},{1,3},{2,0},{3,1},{4,6},{5,7},{6,4},{7,5},{8,10},{9,11},{10,... | collective-permute-start | bytes 196616 | tf_op jit(solution)/shard_map/ppermute | solution.py:263
  35.8 5.4 %collective-permute-start.11 = (bf16[8,4,32,128]{3,2,1,0:T(8,128)(2,1)S(1)}, bf16[8,4,32,128]{3,2,1,0:T(8,128)(2,1)S(1)}, u32[]{:S(2)}, u32[]{:S(2)}) collective-permute-start(bf16[8,4,32,128]{3,2,1,0:T(8,128)(2,1)S(1)} %get-tuple-element.46), channel_id=1, source_target_pairs={{0,1},{1,0},{2,3},{3,2},{4,5},{5,4},{6,7},{7,6},{8,9},{9,8},{10,11... | collective-permute-start | bytes 786440 | tf_op jit(solution)/shard_map/ppermute | solution.py:263
  35.9 1.9 %collective-permute-start.12 = (f32[32,256]{1,0:T(8,128)S(1)}, f32[32,256]{1,0:T(8,128)S(1)}, u32[]{:S(2)}, u32[]{:S(2)}) collective-permute-start(f32[32,256]{1,0:T(8,128)S(1)} %get-tuple-element.48), channel_id=1, source_target_pairs={{0,1},{1,0},{2,3},{3,2},{4,5},{5,4},{6,7},{7,6},{8,9},{9,8},{10,11... | collective-permute-start | bytes 98312 | tf_op jit(solution)/shard_map/ppermute | solution.py:263
  36.4 3.9 %collective-permute-start.13 = (f32[32,256]{1,0:T(8,128)S(1)}, f32[32,256]{1,0:T(8,128)S(1)}, u32[]{:S(2)}, u32[]{:S(2)}) collective-permute-start(f32[32,256]{1,0:T(8,128)S(1)} %get-tuple-element.49), channel_id=1, source_target_pairs={{0,2},{1,3},{2,0},{3,1},{4,6},{5,7},{6,4},{7,5},{8,10},{9,11},{10,... | collective-permute-start | bytes 98312 | tf_op jit(solution)/shard_map/ppermute | solution.py:263
  37.5 3.7 %collective-permute-start.14 = (f32[32,256]{1,0:T(8,128)S(1)}, f32[32,256]{1,0:T(8,128)S(1)}, u32[]{:S(2)}, u32[]{:S(2)}) collective-permute-start(f32[32,256]{1,0:T(8,128)S(1)} %get-tuple-element.50), channel_id=1, source_target_pairs={{0,3},{1,2},{2,1},{3,0},{4,7},{5,6},{6,5},{7,4},{8,11},{9,10},{10,... | collective-permute-start | bytes 98312 | tf_op jit(solution)/shard_map/ppermute | solution.py:263
  42.0 15.6 %all-to-all-start.1 = ((bf16[8,192,128]{2,1,0:T(8,128)(2,1)}), bf16[8,192,128]{2,1,0:T(8,128)(2,1)S(1)}, u32[]{:S(2)}, u32[]{:S(2)}) async-start(bf16[8,192,128]{2,1,0:T(8,128)(2,1)} %shard_map.86), calls=%async_computation.1 | async-start | bytes 786432 | tf_op jit(solution)/shard_map/all_to_all | solution.py:266
  45.6 6.5 %collective-permute-start.10 = (f32[32,2048]{1,0:T(8,128)S(1)}, f32[32,2048]{1,0:T(8,128)S(1)}, u32[]{:S(2)}, u32[]{:S(2)}) collective-permute-start(f32[32,2048]{1,0:T(8,128)S(1)} %get-tuple-element.44), channel_id=1, source_target_pairs={{0,1},{1,0},{2,3},{3,2},{4,5},{5,4},{6,7},{7,6},{8,9},{9,8},{10,11... | collective-permute-start | bytes 786440 | tf_op jit(solution)/shard_map/ppermute | solution.py:263
  45.7 1.9 %collective-permute-start.6 = (bf16[64,512]{1,0:T(8,128)(2,1)S(1)}, bf16[64,512]{1,0:T(8,128)(2,1)S(1)}, u32[]{:S(2)}, u32[]{:S(2)}) collective-permute-start(bf16[64,512]{1,0:T(8,128)(2,1)S(1)} %get-tuple-element.37), channel_id=1, source_target_pairs={{0,1},{1,0},{2,3},{3,2},{4,5},{5,4},{6,7},{7,6},{8,9},{9,8},{10,11... | collective-permute-start | bytes 196616 | tf_op jit(solution)/shard_map/ppermute | solution.py:263
  46.1 4.6 %collective-permute-start.7 = (bf16[64,512]{1,0:T(8,128)(2,1)S(1)}, bf16[64,512]{1,0:T(8,128)(2,1)S(1)}, u32[]{:S(2)}, u32[]{:S(2)}) collective-permute-start(bf16[64,512]{1,0:T(8,128)(2,1)S(1)} %get-tuple-element.38), channel_id=1, source_target_pairs={{0,2},{1,3},{2,0},{3,1},{4,6},{5,7},{6,4},{7,5},{8,10},{9,11},{10,... | collective-permute-start | bytes 196616 | tf_op jit(solution)/shard_map/ppermute | solution.py:263
  47.0 4.4 %collective-permute-start.8 = (bf16[64,512]{1,0:T(8,128)(2,1)S(1)}, bf16[64,512]{1,0:T(8,128)(2,1)S(1)}, u32[]{:S(2)}, u32[]{:S(2)}) collective-permute-start(bf16[64,512]{1,0:T(8,128)(2,1)S(1)} %get-tuple-element.39), channel_id=1, source_target_pairs={{0,3},{1,2},{2,1},{3,0},{4,7},{5,6},{6,5},{7,4},{8,11},{9,10},{10,... | collective-permute-start | bytes 196616 | tf_op jit(solution)/shard_map/ppermute | solution.py:263

commit v3 on v2

--- a/solution.py
+++ b/solution.py
@@ -17,21 +17,21 @@
 MIB = 1 << 20
 
 
-def call(kernel, in_specs, out_shape, args, scratch=(), flops=10**6, mib=8, out=False):
-    place = jax.ShapeDtypeStruct if out else pltpu.VMEM
-    outs = out_shape if isinstance(out_shape, list) else [out_shape]
+def call(kernel, in_specs, outs, args, scratch=(), flops=10**6, mib=8):
+    kinds = {"vmem": (pltpu.VMEM, VMEM), "smem": (pltpu.SMEM, SMEM)}
+    shapes = [kinds[k][0](s, d) if k in kinds else jax.ShapeDtypeStruct(s, d) for k, s, d in outs]
+    specs = [kinds[k][1] if k in kinds else {"hbm": HBM, "out": VMEM}[k] for k, _, _ in outs]
     nbytes = sum(a.size * a.dtype.itemsize for a in args)
-    return pl.pallas_call(
+    result = pl.pallas_call(
         kernel,
-        out_shape=[place(s, d) for s, d in outs]
-        if isinstance(out_shape, list)
-        else place(*out_shape),
+        out_shape=shapes,
         in_specs=in_specs,
-        out_specs=[VMEM] * len(outs) if isinstance(out_shape, list) else VMEM,
+        out_specs=specs,
         scratch_shapes=list(scratch),
         compiler_params=pltpu.CompilerParams(vmem_limit_bytes=mib * MIB),
         cost_estimate=pl.CostEstimate(flops=flops, bytes_accessed=nbytes, transcendentals=0),
     )(*args)
+    return result if len(outs) > 1 else result[0]
 
 
 def iota(shape, dim):
@@ -47,39 +47,41 @@
     return pl.ds(pl.multiple_of(start * size, size), size)
 
 
-def choose_kernel(adj_hbm, feats, sel, copied, adj_ref, sends, sel_s, sems):
-    names = pltpu.make_async_copy(adj_hbm, adj_ref, sems.at[2])
+def choose_kernel(adj_hbm, feats, sel, copied, adj_ref, sends, sems):
+    names = pltpu.make_async_copy(adj_hbm, adj_ref, sems.at[0])
     names.start()
-    copy = pltpu.make_async_copy(feats, copied, sems.at[0])
+    copy = pltpu.make_async_copy(feats, copied, sems.at[1])
     copy.start()
     slots_n, ids_n = adj_ref.shape
     tile = sends.shape[3]
     blk = feats.shape[1] // tile
     r, _, _ = position()
+    mine = r * blk + iota((blk, ids_n), 0)
+    group = (iota((ids_n, LANES), 0) // blk == iota((ids_n, LANES), 1)).astype(BF16)
+    below = (iota((blk, blk), 1) < iota((blk, blk), 0)).astype(BF16)
+    number = iota((blk, LANES), 0).astype(F32)
     names.wait()
     adj = adj_ref[...]
-    mine = r * blk + iota((blk, ids_n), 0)
     hits = jnp.zeros((blk, ids_n), F32)
     for k in range(slots_n):
         hits += (adj[k : k + 1, :] == mine).astype(F32)
-    group = (iota((ids_n, LANES), 0) // blk == iota((ids_n, LANES), 1)).astype(BF16)
     wants = jnp.dot(hits.astype(BF16), group, preferred_element_type=F32) > 0.5
-    below = (iota((blk, blk), 1) < iota((blk, blk), 0)).astype(BF16)
     order = jnp.dot(below, wants.astype(BF16), preferred_element_type=F32)
-    number = iota((blk, LANES), 0).astype(F32)
+    picks = []
     for o in range(CAP):
         pick = jnp.where(wants & (jnp.abs(order - o) < 0.5), number, 0.0)
-        sel[o : o + 1, :] = jnp.sum(pick, axis=0, keepdims=True).astype(I32)
-    scalars = pltpu.make_async_copy(sel, sel_s, sems.at[1])
-    scalars.start()
+        picks.append(jnp.sum(pick, axis=0, keepdims=True).astype(I32))
     copy.wait()
-    scalars.wait()
     for d in range(sends.shape[0]):
         for o in range(CAP):
-            sends[d, o] = copied[:, rows_at(sel_s[o, d], tile)]
-
-
-def slot_kernel(blk, adj_ref, out_ref):
+            at = picks[o][0, d]
+            sel[o, d] = at
+            source = copied.at[:, rows_at(at, tile)]
+            pltpu.make_async_copy(source, sends.at[d, o], sems.at[2]).start()
+    pltpu.make_async_copy(sends, sends, sems.at[2]).wait()
+
+
+def slot_kernel(blk, adj_ref, slots, out_ref, sem):
     slots_n, ids_n = adj_ref.shape
     r, _, _ = position()
     start = pl.multiple_of((r * blk) // LANES * LANES, LANES)
@@ -98,6 +100,9 @@
     for k in range(slots_n):
         found = jnp.where(near[k : k + 1, :] == block, slot, 0.0)
         out_ref[k : k + 1, :] = jnp.sum(found, axis=0, keepdims=True).astype(I32)
+    copy = pltpu.make_async_copy(out_ref, slots, sem)
+    copy.start()
+    copy.wait()
 
 
 def fetch_kernel(side_of, a_hbm, *rest):
@@ -152,8 +157,8 @@
 
 
 def dense_kernel(keep, came, w_ref, c0, c1, c2, c3, *rest):
-    outs, (g_send, g_keep), wgs = rest[:4], rest[4:6], rest[6:10]
-    agg, cot, out_s, grad_s, wg_s = rest[10:]
+    outs, (g_send, g_keep, wg_send, wg_keep) = rest[:4], rest[4:8]
+    agg, cot, out_s, grad_s, wg_s = rest[8:]
     _, c, x = position()
     fx = keep.shape[0]
     u = c0.shape[0]
@@ -172,10 +177,10 @@
     wg_s[...] = lax.dot_general(act, pre, (((1,), (1,)), ((), ())), preferred_element_type=F32)
     g_keep[...] = grad_s[rows_at(x, fx), :]
     g_send[...] = grad_s[rows_at(1 - x, fx), :]
-    f = wgs[0].shape[0]
+    wg_keep[...] = wg_s[rows_at(x, fx), :]
+    wg_send[...] = wg_s[rows_at(1 - x, fx), :]
     for q in range(4):
         outs[q][...] = out_s[rows_at(col ^ q, u), :]
-        wgs[q][...] = wg_s[rows_at(col ^ q, f), :]
 
 
 def spread(side_of, slot, a_side, g_ref, acc):
@@ -196,7 +201,8 @@
     spread(side_of, slot, a_side, g_ref, acc)
 
 
-def spread_last_kernel(side_of, slot, a_side, g_ref, before, own, own_send, stay, send, acc):
+def spread_last_kernel(side_of, slot, a_side, g_ref, before, wg, wg_came, *rest):
+    own, own_send, stay, send, wg_keep, wg_send, acc = rest
     acc[...] = before[...]
     spread(side_of, slot, a_side, g_ref, acc)
     _, c, _ = position()
@@ -211,33 +217,50 @@
     for b in range(blk):
         own[:, b * tile : (b + 1) * tile] = acc[b, top, :]
         own_send[:, b * tile : (b + 1) * tile] = acc[b, low, :]
-
-
-def total_kernel(stay, came, w0, w1, w2, w3, out):
+    wg_keep[...] = wg[top, :] + wg_came[top, :]
+    wg_send[...] = wg[low, :] + wg_came[low, :]
+
+
+def total_kernel(stay, came, wg, wg_came, out, packed, sems):
     f, tile = stay.shape[2], stay.shape[3]
-    part = ((w0[...] + w1[...]) + (w2[...] + w3[...])).astype(BF16)
+    part = (wg[...] + wg_came[...]).astype(BF16)
+    copies = []
     for d in range(stay.shape[0]):
         for o in range(CAP):
-            out[d, o * f : (o + 1) * f, :] = (stay[d, o] + came[d, o].astype(F32)).astype(BF16)
+            packed[d, o * f : (o + 1) * f, :] = (stay[d, o] + came[d, o].astype(F32)).astype(BF16)
         for h in range(part.shape[1] // tile):
             at = (CAP + h) * f
-            out[d, at : at + f, :] = part[:, h * tile : (h + 1) * tile]
-
-
-def collect_kernel(scale, sel, own, came, back, out, wg):
+            packed[d, at : at + f, :] = part[:, h * tile : (h + 1) * tile]
+        copies.append(pltpu.make_async_copy(packed.at[d], out.at[d], sems.at[d]))
+        copies[-1].start()
+    for copy in copies:
+        copy.wait()
+
+
+def collect_kernel(scale, sel, own, came, back, out, wg_out, acc, wg, sems):
     tile = back.shape[2]
     f = own.shape[0]
-    out[...] = own[...] + came[...]
-    for d in range(back.shape[0]):
-        for o in range(CAP):
-            term = back[d, o * f : (o + 1) * f, :].astype(F32)
-            out[:, rows_at(sel[o, d], tile)] += term
+    half = f // 2
+    copies = []
+    for h in range(2):
+        rows = slice(h * half, (h + 1) * half)
+        acc[rows, :] = own[rows, :] + came[rows, :]
+        for d in range(back.shape[0]):
+            for o in range(CAP):
+                term = back[d, o * f + h * half : o * f + (h + 1) * half, :].astype(F32)
+                acc[rows, rows_at(sel[o, d], tile)] += term
+        copies.append(pltpu.make_async_copy(acc.at[rows, :], out.at[rows, :], sems.at[h]))
+        copies[-1].start()
     for h in range(wg.shape[1] // tile):
         at = (CAP + h) * f
         total = back[0, at : at + f, :].astype(F32)
         for d in range(1, back.shape[0]):
             total = total + back[d, at : at + f, :].astype(F32)
         wg[:, h * tile : (h + 1) * tile] = total * scale
+    copies.append(pltpu.make_async_copy(wg, wg_out, sems.at[2]))
+    copies[-1].start()
+    for copy in copies:
+        copy.wait()
 
 
 def place_kernel(p0, p1, p2, p3, out):
@@ -268,12 +291,12 @@
     adj_t = adj_index.T
     in_hbm = functools.partial(pltpu.with_memory_space_constraint, memory_space=pltpu.HBM)
     part = (rows_n, CAP, f, tile)
-    piece = ((units_loc, quarter), BF16)
+    piece = ("vmem", (units_loc, quarter), BF16)
     sel, feats, adj, sends = call(
         choose_kernel, [HBM, HBM],
-        [((8, LANES), I32), ((f, nodes), BF16), (adj_t.shape, I32), (part, BF16)],
-        [in_hbm(adj_t), in_hbm(feats_t)],
-        [pltpu.SMEM((8, LANES), I32), pltpu.SemaphoreType.DMA((3,))], mib=big,
+        [("smem", (CAP, rows_n), I32), ("vmem", (f, nodes), BF16), ("vmem", adj_t.shape, I32),
+         ("hbm", part, BF16)],
+        [in_hbm(adj_t), in_hbm(feats_t)], [pltpu.SemaphoreType.DMA((3,))], mib=big,
     )
     feats_mate = mate(feats, 1)
     got = over_rows(sends)
@@ -284,30 +307,33 @@
     def near(x):
         return x
 
-    a_side = ((blk // 4, slots_n, tile, tile), BF16)
+    a_side = ("vmem", (blk // 4, slots_n, tile, tile), BF16)
     sems = [pltpu.SemaphoreType.DMA((4 + blk // 4,))]
     a_far, *cots = call(
         functools.partial(fetch_kernel, far), [HBM, HBM], [a_side] + [piece] * 4,
         [in_hbm(adj_weight), in_hbm(cotangent_t)], sems,
     )
     a_near = call(
-        functools.partial(fetch_kernel, near), [HBM], a_side,
+        functools.partial(fetch_kernel, near), [HBM], [a_side],
         [in_hbm(adj_weight)], sems,
     )
     slot = call(
         functools.partial(slot_kernel, blk), [VMEM],
-        ((slots_n, LANES), I32), [adj], mib=big,
+        [("smem", (slots_n, LANES), I32)], [adj],
+        [pltpu.VMEM((slots_n, LANES), I32), pltpu.SemaphoreType.DMA], mib=big,
     )
     cots = [cots[0]] + [mate(cots[q], q) for q in (1, 2, 3)]
     got_mate = mate(got, 1)
 
     a_flops = blk // 2 * slots_n * fx * tile * tile
+
+    half_g = ("vmem", (fx, quarter), BF16)
 
     def gather(side_of, a_side):
         args = [slot, a_side, feats, feats_mate, got, got_mate]
         return call(
             functools.partial(gather_kernel, side_of), [SMEM] + [VMEM] * (len(args) - 1),
-            ((fx, quarter), BF16), args, [pltpu.VMEM((table_n, fx, tile), BF16)], a_flops,
+            [half_g], args, [pltpu.VMEM((table_n, fx, tile), BF16)], a_flops,
             big,
         )
 
@@ -315,12 +341,10 @@
     agg_came = mate(agg_far, 2)
     agg_near = gather(near, a_near)
 
-    half_g = ((fx, quarter), BF16)
-    wg_part = ((f, units), F32)
     args = [agg_near, agg_came, weight, *cots]
-    *outs, g_send, g_keep, w0, w1, w2, w3 = call(
+    *outs, g_send, g_keep, wg_send, wg_keep = call(
         dense_kernel, [VMEM] * len(args),
-        [piece] * 4 + [half_g] * 2 + [wg_part] * 4, args,
+        [piece] * 4 + [half_g] * 2 + [("vmem", (fx, units), F32)] * 2, args,
         [
             pltpu.VMEM((f_in, quarter), BF16),
             pltpu.VMEM((units, quarter), BF16),
@@ -331,30 +355,39 @@
         6 * f_in * units * quarter, 12,
     )
     g_came = mate(g_send, 2)
-    wgs = [w0, mate(w1, 1), mate(w2, 2), mate(w3, 3)]
+    wg_came = mate(wg_send, 2)
 
     acc = call(
         functools.partial(spread_first_kernel, near), [SMEM, VMEM, VMEM],
-        ((table_n, fx, tile), F32), [slot, a_near, g_keep], [], a_flops, big,
-    )
-    own, own_send, stay, send = call(
-        functools.partial(spread_last_kernel, far), [SMEM, VMEM, VMEM, VMEM],
-        [((f, nodes), F32)] * 2 + [(part, F32), (part, BF16)],
-        [slot, a_far, g_came, acc], [pltpu.VMEM((table_n, fx, tile), F32)], a_flops, big + 8,
-    )
+        [("vmem", (table_n, fx, tile), F32)], [slot, a_near, g_keep], [], a_flops, big,
+    )
+    wg_part = ((f, units), F32)
+    own, own_send, stay, send, wg_keep, wg_send = call(
+        functools.partial(spread_last_kernel, far), [SMEM] + [VMEM] * 5,
+        [("vmem", (f, nodes), F32)] * 2
+        + [("vmem", part, F32), ("vmem", part, BF16)]
+        + [("vmem", *wg_part)] * 2,
+        [slot, a_far, g_came, acc, wg_keep, wg_came],
+        [pltpu.VMEM((table_n, fx, tile), F32)], a_flops, big + 8,
+    )
+    packed = ((rows_n, CAP * f + f * units // tile, tile), BF16)
+    total = call(
+        total_kernel, [VMEM] * 4, [("hbm", *packed)],
+        [stay, mate(send, 1), wg_keep, mate(wg_send, 1)],
+        [pltpu.VMEM(*packed), pltpu.SemaphoreType.DMA((rows_n,))], mib=big,
+    )
+    back = over_rows(total)
     own_came = mate(own_send, 1)
-    total = call(
-        total_kernel, [VMEM] * 6, ((rows_n, CAP * f + f * units // tile, tile), BF16),
-        [stay, mate(send, 1), *wgs], mib=big,
-    )
     feat_grad, weight_grad = call(
         functools.partial(collect_kernel, 1.0 / math.sqrt(nodes * rows_n)),
-        [SMEM, VMEM, VMEM, VMEM], [((f, nodes), F32), wg_part],
-        [sel, own, own_came, over_rows(total)], mib=big, out=True,
+        [SMEM, VMEM, VMEM, VMEM], [("hbm", (f, nodes), F32), ("hbm", *wg_part)],
+        [sel, own, own_came, back],
+        [pltpu.VMEM((f, nodes), F32), pltpu.VMEM(*wg_part), pltpu.SemaphoreType.DMA((3,))],
+        mib=big,
     )
 
     outs = [outs[0]] + [mate(outs[q], q) for q in (1, 2, 3)]
-    output_t = call(place_kernel, [VMEM] * 4, ((units_loc, nodes), BF16), outs, out=True)
+    output_t = call(place_kernel, [VMEM] * 4, [("out", (units_loc, nodes), BF16)], outs)
     return output_t, weight_grad, feat_grad
 
 

time: 59.5 us -> 58.2 us (0.978)
  waiting for transfers between devices: 14.6 us -> 13.9 us
    ppermute x15 -> x14, waiting for transfers between devices: 9.12 us -> 8.2 us  [mate(): return lax.ppermute(v, 'cols', [(i, i ^ q) for i in range(cols_n)])]
    ppermute x15 -> x14, starting transfers between devices: 9.12 us -> 8.58 us  [mate(): return lax.ppermute(v, 'cols', [(i, i ^ q) for i in range(cols_n)])]
  transfers between devices with their start and end apart: 16 -> 15, of which waited for: 6 -> 7; matrix products, arithmetic and copies ran while one was open for 0% -> 0% of each run, Pallas kernels for 15% -> 13%
where the time goes in v3:
time: 58.2 us; the launch traced here: 57.9 us
  blocking collectives  16 us (27%)
  Pallas kernels  15 us (26%)
  waiting for transfers between devices  13.9 us (24%)
  starting transfers between devices  12.2 us (21%)
  between operations  0.78 us (1%)
    all_to_all x1, blocking collectives, over_rows(): return lax.all_to_all(v, 'rows', 0, 0, tiled=True)  16 us
    pallas_call x12, Pallas kernels, call(): pl.pallas_call(kernel, out_shape=shapes, in_specs=in_specs, out_specs=spe...  15 us
    ppermute x14, starting transfers between devices, mate(): return lax.ppermute(v, 'cols', [(i, i ^ q) for i in range(cols_n)])  8.58 us
    ppermute x14, waiting for transfers between devices, mate(): return lax.ppermute(v, 'cols', [(i, i ^ q) for i in range(cols_n)])  8.2 us
    all_to_all x1, waiting for transfers between devices, over_rows(): return lax.all_to_all(v, 'rows', 0, 0, tiled=True)  5.71 us
    all_to_all x1, starting transfers between devices, over_rows(): return lax.all_to_all(v, 'rows', 0, 0, tiled=True)  3.6 us
  transfers between devices with their start and end apart: 15, of which 7 were waited for; matrix products, arithmetic and copies ran while one was open for 0% of the time, Pallas kernels for 13%

profile of v3, /device:TPU:0, one launch (start us, length us, event | category | flops | bytes accessed | tf_op | source)
XLA Modules:
  0.0 57.9 jit_solution(13628605068434632952)
XLA Ops:
  0.6 4.1 %shard_map.76 = (s32[4,8]{1,0:T(4,128)S(4)}, bf16[32,2048]{1,0:T(8,128)(2,1)S(1)}, s32[16,128]{1,0:T(8,128)S(1)}, bf16[8,4,32,128]{3,2,1,0:T(8,128)(2,1)S(1)}) custom-call(s32[16,128]{1,0:T(8,128)} %bitcast.1, bf16[32,2048]{1,0:T(8,128)(2,1)} %feats.1), custom_call_target="tpu_custom_call" | custom-call | flops 1000000 | bytes 139264 | tf_op jit(solution)/shard_map/pallas_call | solution.py:25
  4.7 16.0 %all_to_all.10.got = bf16[8,4,32,128]{3,2,1,0:T(8,128)(2,1)S(1)} all-to-all(bf16[8,4,32,128]{3,2,1,0:T(8,128)(2,1)S(1)} %get-tuple-element.30), channel_id=1, replica_groups=mesh['rows'=8,'cols'=4] {'rows'}, dimensions={0} | all-to-all | bytes 524288 | tf_op jit(solution)/shard_map/all_to_all | solution.py:289
  20.8 0.0 collective-permute-start.1
  20.8 0.5 collective-permute-start
  21.3 1.7 %shard_map.80 = (bf16[4,16,128,128]{3,2,1,0:T(8,128)(2,1)S(1)}, bf16[64,512]{1,0:T(8,128)(2,1)S(1)}, bf16[64,512]{1,0:T(8,128)(2,1)S(1)}, bf16[64,512]{1,0:T(8,128)(2,1)S(1)}, bf16[64,512]{1,0:T(8,128)(2,1)S(1)}) custom-call(bf16[16,16,128,128]{3,2,1,0:T(8,128)(2,1)} %a_hbm.3, bf16[64,2048]{1,0:T(8,128)(2,1)} %rest_0_.1), custom_call_target="tpu_custom_call" | custom-call | flops 1000000 | bytes 8650752 | tf_op jit(solution)/shard_map/pallas_call | solution.py:25
  23.0 0.1 collective-permute-start.3
  23.1 1.6 %collective-permute-start.4 = (bf16[64,512]{1,0:T(8,128)(2,1)S(1)}, bf16[64,512]{1,0:T(8,128)(2,1)S(1)}, u32[]{:S(2)}, u32[]{:S(2)}) collective-permute-start(bf16[64,512]{1,0:T(8,128)(2,1)S(1)} %get-tuple-element.34), channel_id=1, source_target_pairs={{0,2},{1,3},{2,0},{3,1},{4,6},{5,7},{6,4},{7,5},{8,10},{9,11},{10,... | collective-permute-start | bytes 196616 | tf_op jit(solution)/shard_map/ppermute | solution.py:286
  24.6 0.3 collective-permute-start.5
  24.9 1.3 %shard_map.77.slot = s32[16,128]{1,0:T(8,128)S(4)} custom-call(s32[16,128]{1,0:T(8,128)S(1)} %get-tuple-element.28.adj_ref), custom_call_target="tpu_custom_call" | custom-call | flops 1000000 | bytes 8192 | tf_op jit(solution)/shard_map/pallas_call | solution.py:25
  26.2 0.0 collective-permute-done.mate
  26.2 0.0 collective-permute-done.1.got_mate
  26.2 0.9 %shard_map.81 = bf16[64,512]{1,0:T(8,128)(2,1)S(1)} custom-call(s32[16,128]{1,0:T(8,128)S(4)} %shard_map.77.slot, bf16[4,16,128,128]{3,2,1,0:T(8,128)(2,1)S(1)} %get-tuple-element.31.a_side, bf16[32,2048]{1,0:T(8,128)(2,1)S(1)} %get-tuple-element.29.mine, bf16[32,2048]{1,0:T(8,128)(2,1)S(1)} %collective-permute-done.mate, ...), custom_call_target="tpu_custom_call" | custom-call | flops 134217728 | bytes 2891776 | tf_op jit(solution)/shard_map/pallas_call | solution.py:25
  27.1 1.6 %collective-permute-start.2 = (bf16[64,512]{1,0:T(8,128)(2,1)S(1)}, bf16[64,512]{1,0:T(8,128)(2,1)S(1)}, u32[]{:S(2)}, u32[]{:S(2)}) collective-permute-start(bf16[64,512]{1,0:T(8,128)(2,1)S(1)} %shard_map.81), channel_id=1, source_target_pairs={{0,2},{1,3},{2,0},{3,1},{4,6},{5,7},{6,4},{7,5},{8,10},{9,11},{10,... | collective-permute-start | bytes 196616 | tf_op jit(solution)/shard_map/ppermute | solution.py:286
  28.7 1.6 %shard_map.78.a_side = bf16[4,16,128,128]{3,2,1,0:T(8,128)(2,1)S(1)} custom-call(bf16[16,16,128,128]{3,2,1,0:T(8,128)(2,1)} %a_hbm.3), custom_call_target="tpu_custom_call" | custom-call | flops 1000000 | bytes 8388608 | tf_op jit(solution)/shard_map/pallas_call | solution.py:25
  30.3 0.0 copy-start
  30.3 0.9 %shard_map.79.keep = bf16[64,512]{1,0:T(8,128)(2,1)S(1)} custom-call(s32[16,128]{1,0:T(8,128)S(4)} %shard_map.77.slot, bf16[4,16,128,128]{3,2,1,0:T(8,128)(2,1)S(1)} %shard_map.78.a_side, bf16[32,2048]{1,0:T(8,128)(2,1)S(1)} %get-tuple-element.29.mine, bf16[32,2048]{1,0:T(8,128)(2,1)S(1)} %collective-permute-done.mate, ...), custom_call_target="tpu_custom_call" | custom-call | flops 134217728 | bytes 2891776 | tf_op jit(solution)/shard_map/pallas_call | solution.py:25
  31.2 0.0 collective-permute-done.3.c1
  31.2 0.0 collective-permute-done.4.c2
  31.2 0.0 collective-permute-done.5.c3
  31.2 0.3 collective-permute-done.2.came
  31.6 0.0 copy-done
  31.6 0.6 %shard_map.82 = (bf16[64,512]{1,0:T(8,128)(2,1)S(1)}, bf16[64,512]{1,0:T(8,128)(2,1)S(1)}, bf16[64,512]{1,0:T(8,128)(2,1)S(1)}, bf16[64,512]{1,0:T(8,128)(2,1)S(...) custom-call(bf16[64,512]{1,0:T(8,128)(2,1)S(1)} %shard_map.79.keep, ...), custom_call_target="tpu_custom_call" | custom-call | flops 100663296 | bytes 458752 | tf_op jit(solution)/shard_map/pallas_call | solution.py:25
  32.2 1.6 %collective-permute-start.9 = (bf16[64,512]{1,0:T(8,128)(2,1)S(1)}, bf16[64,512]{1,0:T(8,128)(2,1)S(1)}, u32[]{:S(2)}, u32[]{:S(2)}) collective-permute-start(bf16[64,512]{1,0:T(8,128)(2,1)S(1)} %get-tuple-element.41), channel_id=1, source_target_pairs={{0,2},{1,3},{2,0},{3,1},{4,6},{5,7},{6,4},{7,5},{8,10},{9,11},{10,... | collective-permute-start | bytes 196616 | tf_op jit(solution)/shard_map/ppermute | solution.py:286
  33.7 0.5 collective-permute-start.10
  34.2 0.6 %shard_map.84.before = f32[48,64,128]{2,1,0:T(8,128)S(1)} custom-call(s32[16,128]{1,0:T(8,128)S(4)} %shard_map.77.slot, bf16[4,16,128,128]{3,2,1,0:T(8,128)(2,1)S(1)} %shard_map.78.a_side, bf16[64,512]{1,0:T(8,128)(2,1)S(1)} %get-tuple-element.42.g_ref), custom_call_target="tpu_custom_call" | custom-call | flops 134217728 | bytes 2170880 | tf_op jit(solution)/shard_map/pallas_call | solution.py:25
  34.9 2.1 %collective-permute-done.9.g_ref = bf16[64,512]{1,0:T(8,128)(2,1)S(1)} collective-permute-done((bf16[64,512]{1,0:T(8,128)(2,1)S(1)}, bf16[64,512]{1,0:T(8,128)(2,1)S(1)}, u32[]{:S(2)}, u32[]{:S(2)}) %collective-permute-start.9) | collective-permute-done | bytes 65568 | tf_op jit(solution)/shard_map/ppermute | solution.py:286
  36.9 1.0 %collective-permute-done.10.wg_came = f32[64,256]{1,0:T(8,128)S(1)} collective-permute-done((f32[64,256]{1,0:T(8,128)S(1)}, f32[64,256]{1,0:T(8,128)S(1)}, u32[]{:S(2)}, u32[]{:S(2)}) %collective-permute-start.10) | collective-permute-done | bytes 65568 | tf_op jit(solution)/shard_map/ppermute | solution.py:286
  38.0 0.7 %shard_map.85 = (f32[32,2048]{1,0:T(8,128)S(1)}, f32[32,2048]{1,0:T(8,128)S(1)}, f32[8,4,32,128]{3,2,1,0:T(8,128)S(1)}, bf16[8,4,32,128]{3,2,1,0:T(8,128)(2,1)S(...) custom-call(s32[16,128]{1,0:T(8,128)S(4)} %shard_map.77.slot, bf16[4,16,128,128]{3,2,1,0:T(8,128)(2,1)S(1)} %get-tuple-element.31.a_side, ...), custom_call_target="tpu_custom_call" | custom-call | flops 134217728 | bytes 3874816 | tf_op jit(solution)/shard_map/pallas_call | solution.py:25
  38.7 0.1 collective-permute-start.12
  38.8 0.5 collective-permute-start.13
  39.3 1.1 %collective-permute-done.13.wg_came = f32[32,256]{1,0:T(8,128)S(1)} collective-permute-done((f32[32,256]{1,0:T(8,128)S(1)}, f32[32,256]{1,0:T(8,128)S(1)}, u32[]{:S(2)}, u32[]{:S(2)}) %collective-permute-start.13) | collective-permute-done | bytes 32800 | tf_op jit(solution)/shard_map/ppermute | solution.py:286
  40.4 0.0 collective-permute-done.12.came
  40.4 0.8 %shard_map.86 = bf16[8,192,128]{2,1,0:T(8,128)(2,1)} custom-call(f32[8,4,32,128]{3,2,1,0:T(8,128)S(1)} %get-tuple-element.47.stay, bf16[8,4,32,128]{3,2,1,0:T(8,128)(2,1)S(1)} %collective-permute-done.12.came, f32[32,256]{1,0:T(8,128)S(1)} %get-tuple-element.49.wg, f32[32,256]{1,0:T(8,128)S(1)} %collective-permute-done.13.wg_came), custom_call_target="tpu_custom_call" | custom-call | flops 1000000 | bytes 851968 | tf_op jit(solution)/shard_map/pallas_call | solution.py:25
  41.2 3.6 %all-to-all-start.1 = ((bf16[8,192,128]{2,1,0:T(8,128)(2,1)}), bf16[8,192,128]{2,1,0:T(8,128)(2,1)S(1)}, u32[]{:S(2)}, u32[]{:S(2)}) async-start(bf16[8,192,128]{2,1,0:T(8,128)(2,1)} %shard_map.86), calls=%async_computation.1 | async-start | bytes 786432 | tf_op jit(solution)/shard_map/all_to_all | solution.py:289
  44.8 0.1 collective-permute-start.11
  44.9 0.4 collective-permute-start.6
  45.3 0.7 %collective-permute-start.7 = (bf16[64,512]{1,0:T(8,128)(2,1)S(1)}, bf16[64,512]{1,0:T(8,128)(2,1)S(1)}, u32[]{:S(2)}, u32[]{:S(2)}) collective-permute-start(bf16[64,512]{1,0:T(8,128)(2,1)S(1)} %get-tuple-element.38), channel_id=1, source_target_pairs={{0,2},{1,3},{2,0},{3,1},{4,6},{5,7},{6,4},{7,5},{8,10},{9,11},{10,... | collective-permute-start | bytes 196616 | tf_op jit(solution)/shard_map/ppermute | solution.py:286
  46.0 0.7 %collective-permute-start.8 = (bf16[64,512]{1,0:T(8,128)(2,1)S(1)}, bf16[64,512]{1,0:T(8,128)(2,1)S(1)}, u32[]{:S(2)}, u32[]{:S(2)}) collective-permute-start(bf16[64,512]{1,0:T(8,128)(2,1)S(1)} %get-tuple-element.39), channel_id=1, source_target_pairs={{0,3},{1,2},{2,1},{3,0},{4,7},{5,6},{6,5},{7,4},{8,11},{9,10},{10,... | collective-permute-start | bytes 196616 | tf_op jit(solution)/shard_map/ppermute | solution.py:286
  46.7 0.0 collective-permute-done.6.p1
  46.8 3.4 %collective-permute-done.7.p2 = bf16[64,512]{1,0:T(8,128)(2,1)S(1)} collective-permute-done((bf16[64,512]{1,0:T(8,128)(2,1)S(1)}, bf16[64,512]{1,0:T(8,128)(2,1)S(1)}, u32[]{:S(2)}, u32[]{:S(2)}) %collective-permute-start.7) | collective-permute-done | bytes 65568 | tf_op jit(solution)/shard_map/ppermute | solution.py:286
  50.2 0.3 collective-permute-done.8.p3
  50.4 0.7 %shard_map.83 = bf16[64,2048]{1,0:T(8,128)(2,1)} custom-call(bf16[64,512]{1,0:T(8,128)(2,1)S(1)} %get-tuple-element.36.p0, bf16[64,512]{1,0:T(8,128)(2,1)S(1)} %collective-permute-done.6.p1, bf16[64,512]{1,0:T(8,128)(2,1)S(1)} %collective-permute-done.7.p2, bf16[64,512]{1,0:T(8,128)(2,1)S(1)} %collective-permute-done.8.p3), custom_call_target="tpu_custom_call" | custom-call | flops 1000000 | bytes 262144 | tf_op jit(solution)/shard_map/pallas_call | solution.py:25
  51.1 0.0 collective-permute-done.11.came
  51.1 5.7 %all-to-all-done.1.back = bf16[8,192,128]{2,1,0:T(8,128)(2,1)S(1)} async-done(((bf16[8,192,128]{2,1,0:T(8,128)(2,1)}), bf16[8,192,128]{2,1,0:T(8,128)(2,1)S(1)}, u32[]{:S(2)}, u32[]{:S(2)}) %all-to-all-start.1) | async-done | bytes 393248 | tf_op jit(solution)/shard_map/all_to_all | solution.py:289
  56.9 1.0 %shard_map.87 = (f32[32,2048]{1,0:T(8,128)}, f32[32,256]{1,0:T(8,128)}) custom-call(s32[4,8]{1,0:T(4,128)S(4)} %get-tuple-element.40.sel, f32[32,2048]{1,0:T(8,128)S(1)} %get-tuple-element.45.own, f32[32,2048]{1,0:T(8,128)S(1)} %collective-permute-done.11.came, bf16[8,192,128]{2,1,0:T(8,128)(2,1)S(1)} %all-to-all-done.1.back), custom_call_target="tpu_custom_call" | custom-call | flops 1000000 | bytes 917632 | tf_op jit(solution)/shard_map/pallas_call | solution.py:25
Async XLA Ops:
  20.8 5.5 %collective-permute-start.1 = (bf16[8,4,32,128]{3,2,1,0:T(8,128)(2,1)S(1)}, bf16[8,4,32,128]{3,2,1,0:T(8,128)(2,1)S(1)}, u32[]{:S(2)}, u32[]{:S(2)}) collective-permute-start(bf16[8,4,32,128]{3,2,1,0:T(8,128)(2,1)S(1)} %all_to_all.10.got), channel_id=1, source_target_pairs={{0,1},{1,0},{2,3},{3,2},{4,5},{5,4},{6,7},{7,6},{8,9},{9,8},{10,11... | collective-permute-start | bytes 786440 | tf_op jit(solution)/shard_map/ppermute | solution.py:286
  20.8 5.5 %collective-permute-start = (bf16[32,2048]{1,0:T(8,128)(2,1)S(1)}, bf16[32,2048]{1,0:T(8,128)(2,1)S(1)}, u32[]{:S(2)}, u32[]{:S(2)}) collective-permute-start(bf16[32,2048]{1,0:T(8,128)(2,1)S(1)} %get-tuple-element.29.mine), channel_id=1, source_target_pairs={{0,1},{1,0},{2,3},{3,2},{4,5},{5,4},{6,7},{7,6},{8,9},{9,8},{10,11... | collective-permute-start | bytes 393224 | tf_op jit(solution)/shard_map/ppermute | solution.py:286
  23.0 8.2 %collective-permute-start.3 = (bf16[64,512]{1,0:T(8,128)(2,1)S(1)}, bf16[64,512]{1,0:T(8,128)(2,1)S(1)}, u32[]{:S(2)}, u32[]{:S(2)}) collective-permute-start(bf16[64,512]{1,0:T(8,128)(2,1)S(1)} %get-tuple-element.33), channel_id=1, source_target_pairs={{0,1},{1,0},{2,3},{3,2},{4,5},{5,4},{6,7},{7,6},{8,9},{9,8},{10,11... | collective-permute-start | bytes 196616 | tf_op jit(solution)/shard_map/ppermute | solution.py:286
  23.1 8.1 %collective-permute-start.4 = (bf16[64,512]{1,0:T(8,128)(2,1)S(1)}, bf16[64,512]{1,0:T(8,128)(2,1)S(1)}, u32[]{:S(2)}, u32[]{:S(2)}) collective-permute-start(bf16[64,512]{1,0:T(8,128)(2,1)S(1)} %get-tuple-element.34), channel_id=1, source_target_pairs={{0,2},{1,3},{2,0},{3,1},{4,6},{5,7},{6,4},{7,5},{8,10},{9,11},{10,... | collective-permute-start | bytes 196616 | tf_op jit(solution)/shard_map/ppermute | solution.py:286
  24.6 6.6 %collective-permute-start.5 = (bf16[64,512]{1,0:T(8,128)(2,1)S(1)}, bf16[64,512]{1,0:T(8,128)(2,1)S(1)}, u32[]{:S(2)}, u32[]{:S(2)}) collective-permute-start(bf16[64,512]{1,0:T(8,128)(2,1)S(1)} %get-tuple-element.35), channel_id=1, source_target_pairs={{0,3},{1,2},{2,1},{3,0},{4,7},{5,6},{6,5},{7,4},{8,11},{9,10},{10,... | collective-permute-start | bytes 196616 | tf_op jit(solution)/shard_map/ppermute | solution.py:286
  27.1 4.4 %collective-permute-start.2 = (bf16[64,512]{1,0:T(8,128)(2,1)S(1)}, bf16[64,512]{1,0:T(8,128)(2,1)S(1)}, u32[]{:S(2)}, u32[]{:S(2)}) collective-permute-start(bf16[64,512]{1,0:T(8,128)(2,1)S(1)} %shard_map.81), channel_id=1, source_target_pairs={{0,2},{1,3},{2,0},{3,1},{4,6},{5,7},{6,4},{7,5},{8,10},{9,11},{10,... | collective-permute-start | bytes 196616 | tf_op jit(solution)/shard_map/ppermute | solution.py:286
  30.3 1.3 %copy-start = (bf16[128,256]{1,0:T(8,128)(2,1)S(1)}, bf16[128,256]{1,0:T(8,128)(2,1)}, u32[]{:S(2)}) copy-start(bf16[128,256]{1,0:T(8,128)(2,1)} %w_ref.1) | copy-start | bytes 196612
  32.2 4.8 %collective-permute-start.9 = (bf16[64,512]{1,0:T(8,128)(2,1)S(1)}, bf16[64,512]{1,0:T(8,128)(2,1)S(1)}, u32[]{:S(2)}, u32[]{:S(2)}) collective-permute-start(bf16[64,512]{1,0:T(8,128)(2,1)S(1)} %get-tuple-element.41), channel_id=1, source_target_pairs={{0,2},{1,3},{2,0},{3,1},{4,6},{5,7},{6,4},{7,5},{8,10},{9,11},{10,... | collective-permute-start | bytes 196616 | tf_op jit(solution)/shard_map/ppermute | solution.py:286
  33.7 4.3 %collective-permute-start.10 = (f32[64,256]{1,0:T(8,128)S(1)}, f32[64,256]{1,0:T(8,128)S(1)}, u32[]{:S(2)}, u32[]{:S(2)}) collective-permute-start(f32[64,256]{1,0:T(8,128)S(1)} %get-tuple-element.44), channel_id=1, source_target_pairs={{0,2},{1,3},{2,0},{3,1},{4,6},{5,7},{6,4},{7,5},{8,10},{9,11},{10,... | collective-permute-start | bytes 196616 | tf_op jit(solution)/shard_map/ppermute | solution.py:286
  38.7 1.7 %collective-permute-start.12 = (bf16[8,4,32,128]{3,2,1,0:T(8,128)(2,1)S(1)}, bf16[8,4,32,128]{3,2,1,0:T(8,128)(2,1)S(1)}, u32[]{:S(2)}, u32[]{:S(2)}) collective-permute-start(bf16[8,4,32,128]{3,2,1,0:T(8,128)(2,1)S(1)} %get-tuple-element.48), channel_id=1, source_target_pairs={{0,1},{1,0},{2,3},{3,2},{4,5},{5,4},{6,7},{7,6},{8,9},{9,8},{10,11... | collective-permute-start | bytes 786440 | tf_op jit(solution)/shard_map/ppermute | solution.py:286
  38.8 1.6 %collective-permute-start.13 = (f32[32,256]{1,0:T(8,128)S(1)}, f32[32,256]{1,0:T(8,128)S(1)}, u32[]{:S(2)}, u32[]{:S(2)}) collective-permute-start(f32[32,256]{1,0:T(8,128)S(1)} %get-tuple-element.50), channel_id=1, source_target_pairs={{0,1},{1,0},{2,3},{3,2},{4,5},{5,4},{6,7},{7,6},{8,9},{9,8},{10,11... | collective-permute-start | bytes 98312 | tf_op jit(solution)/shard_map/ppermute | solution.py:286
  41.2 15.6 %all-to-all-start.1 = ((bf16[8,192,128]{2,1,0:T(8,128)(2,1)}), bf16[8,192,128]{2,1,0:T(8,128)(2,1)S(1)}, u32[]{:S(2)}, u32[]{:S(2)}) async-start(bf16[8,192,128]{2,1,0:T(8,128)(2,1)} %shard_map.86), calls=%async_computation.1 | async-start | bytes 786432 | tf_op jit(solution)/shard_map/all_to_all | solution.py:289
  44.8 6.3 %collective-permute-start.11 = (f32[32,2048]{1,0:T(8,128)S(1)}, f32[32,2048]{1,0:T(8,128)S(1)}, u32[]{:S(2)}, u32[]{:S(2)}) collective-permute-start(f32[32,2048]{1,0:T(8,128)S(1)} %get-tuple-element.46), channel_id=1, source_target_pairs={{0,1},{1,0},{2,3},{3,2},{4,5},{5,4},{6,7},{7,6},{8,9},{9,8},{10,11... | collective-permute-start | bytes 786440 | tf_op jit(solution)/shard_map/ppermute | solution.py:286
  44.9 1.9 %collective-permute-start.6 = (bf16[64,512]{1,0:T(8,128)(2,1)S(1)}, bf16[64,512]{1,0:T(8,128)(2,1)S(1)}, u32[]{:S(2)}, u32[]{:S(2)}) collective-permute-start(bf16[64,512]{1,0:T(8,128)(2,1)S(1)} %get-tuple-element.37), channel_id=1, source_target_pairs={{0,1},{1,0},{2,3},{3,2},{4,5},{5,4},{6,7},{7,6},{8,9},{9,8},{10,11... | collective-permute-start | bytes 196616 | tf_op jit(solution)/shard_map/ppermute | solution.py:286
  45.3 4.8 %collective-permute-start.7 = (bf16[64,512]{1,0:T(8,128)(2,1)S(1)}, bf16[64,512]{1,0:T(8,128)(2,1)S(1)}, u32[]{:S(2)}, u32[]{:S(2)}) collective-permute-start(bf16[64,512]{1,0:T(8,128)(2,1)S(1)} %get-tuple-element.38), channel_id=1, source_target_pairs={{0,2},{1,3},{2,0},{3,1},{4,6},{5,7},{6,4},{7,5},{8,10},{9,11},{10,... | collective-permute-start | bytes 196616 | tf_op jit(solution)/shard_map/ppermute | solution.py:286
  46.0 4.4 %collective-permute-start.8 = (bf16[64,512]{1,0:T(8,128)(2,1)S(1)}, bf16[64,512]{1,0:T(8,128)(2,1)S(1)}, u32[]{:S(2)}, u32[]{:S(2)}) collective-permute-start(bf16[64,512]{1,0:T(8,128)(2,1)S(1)} %get-tuple-element.39), channel_id=1, source_target_pairs={{0,3},{1,2},{2,1},{3,0},{4,7},{5,6},{6,5},{7,4},{8,11},{9,10},{10,... | collective-permute-start | bytes 196616 | tf_op jit(solution)/shard_map/ppermute | solution.py:286

commit v4 on v3

--- a/solution.py
+++ b/solution.py
@@ -15,6 +15,16 @@
 SMEM = pl.BlockSpec(memory_space=pltpu.SMEM)
 HBM = pl.BlockSpec(memory_space=pltpu.HBM)
 MIB = 1 << 20
+
+
+def order_of(rows_n):
+    bits = (rows_n // 2).bit_length() - 1
+    order = []
+    for i in range(rows_n // 2):
+        gray = i ^ (i >> 1)
+        at = sum(((gray >> b) & 1) << (bits - 1 - b) for b in range(bits)) + rows_n // 2
+        order += [at, rows_n - 1 - at]
+    return order
 
 
 def call(kernel, in_specs, outs, args, scratch=(), flops=10**6, mib=8):
@@ -47,7 +57,7 @@
     return pl.ds(pl.multiple_of(start * size, size), size)
 
 
-def choose_kernel(adj_hbm, feats, sel, copied, adj_ref, sends, sems):
+def choose_kernel(order, adj_hbm, feats, sel, copied, adj_ref, sends, sems):
     names = pltpu.make_async_copy(adj_hbm, adj_ref, sems.at[0])
     names.start()
     copy = pltpu.make_async_copy(feats, copied, sems.at[1])
@@ -66,22 +76,22 @@
     for k in range(slots_n):
         hits += (adj[k : k + 1, :] == mine).astype(F32)
     wants = jnp.dot(hits.astype(BF16), group, preferred_element_type=F32) > 0.5
-    order = jnp.dot(below, wants.astype(BF16), preferred_element_type=F32)
+    rank = jnp.dot(below, wants.astype(BF16), preferred_element_type=F32)
     picks = []
     for o in range(CAP):
-        pick = jnp.where(wants & (jnp.abs(order - o) < 0.5), number, 0.0)
+        pick = jnp.where(wants & (jnp.abs(rank - o) < 0.5), number, 0.0)
         picks.append(jnp.sum(pick, axis=0, keepdims=True).astype(I32))
     copy.wait()
-    for d in range(sends.shape[0]):
+    for p, d in enumerate(order):
         for o in range(CAP):
             at = picks[o][0, d]
-            sel[o, d] = at
+            sel[o, p] = at
             source = copied.at[:, rows_at(at, tile)]
-            pltpu.make_async_copy(source, sends.at[d, o], sems.at[2]).start()
+            pltpu.make_async_copy(source, sends.at[p, o], sems.at[2]).start()
     pltpu.make_async_copy(sends, sends, sems.at[2]).wait()
 
 
-def slot_kernel(blk, adj_ref, slots, out_ref, sem):
+def slot_kernel(order, blk, adj_ref, slots, out_ref, sem):
     slots_n, ids_n = adj_ref.shape
     r, _, _ = position()
     start = pl.multiple_of((r * blk) // LANES * LANES, LANES)
@@ -95,8 +105,9 @@
     a, b = iota((ids_n, ids_n), 0), iota((ids_n, ids_n), 1)
     earlier = ((b < a) & (a // blk == b // blk)).astype(BF16)
     place = jnp.dot(earlier, needed.astype(BF16), preferred_element_type=F32).astype(I32)
-    source = block // blk
-    slot = jnp.where(source == r, block % blk, blk + source * CAP + place).astype(F32)
+    turn = [jnp.full((blk, LANES), order.index(d), I32) for d in range(len(order))]
+    remote = blk + jnp.concatenate(turn, axis=0) * CAP + place
+    slot = jnp.where(block // blk == r, block % blk, remote).astype(F32)
     for k in range(slots_n):
         found = jnp.where(near[k : k + 1, :] == block, slot, 0.0)
         out_ref[k : k + 1, :] = jnp.sum(found, axis=0, keepdims=True).astype(I32)
@@ -177,10 +188,19 @@
     wg_s[...] = lax.dot_general(act, pre, (((1,), (1,)), ((), ())), preferred_element_type=F32)
     g_keep[...] = grad_s[rows_at(x, fx), :]
     g_send[...] = grad_s[rows_at(1 - x, fx), :]
-    wg_keep[...] = wg_s[rows_at(x, fx), :]
-    wg_send[...] = wg_s[rows_at(1 - x, fx), :]
+    f = fx // 2
+    for h in range(2):
+        wg_keep[h * f : (h + 1) * f, :] = wg_s[rows_at(2 * h + c, f), :]
+        wg_send[h * f : (h + 1) * f, :] = wg_s[rows_at(2 * h + 1 - c, f), :]
     for q in range(4):
         outs[q][...] = out_s[rows_at(col ^ q, u), :]
+
+
+def wg_kernel(mine, came, keep, send):
+    _, _, x = position()
+    f = keep.shape[0]
+    keep[...] = mine[rows_at(x, f), :] + came[rows_at(x, f), :]
+    send[...] = mine[rows_at(1 - x, f), :] + came[rows_at(1 - x, f), :]
 
 
 def spread(side_of, slot, a_side, g_ref, acc):
@@ -201,8 +221,7 @@
     spread(side_of, slot, a_side, g_ref, acc)
 
 
-def spread_last_kernel(side_of, slot, a_side, g_ref, before, wg, wg_came, *rest):
-    own, own_send, stay, send, wg_keep, wg_send, acc = rest
+def spread_last_kernel(side_of, slot, a_side, g_ref, before, own, own_send, stay, send, acc):
     acc[...] = before[...]
     spread(side_of, slot, a_side, g_ref, acc)
     _, c, _ = position()
@@ -217,8 +236,6 @@
     for b in range(blk):
         own[:, b * tile : (b + 1) * tile] = acc[b, top, :]
         own_send[:, b * tile : (b + 1) * tile] = acc[b, low, :]
-    wg_keep[...] = wg[top, :] + wg_came[top, :]
-    wg_send[...] = wg[low, :] + wg_came[low, :]
 
 
 def total_kernel(stay, came, wg, wg_came, out, packed, sems):
@@ -245,10 +262,10 @@
     for h in range(2):
         rows = slice(h * half, (h + 1) * half)
         acc[rows, :] = own[rows, :] + came[rows, :]
-        for d in range(back.shape[0]):
+        for p in range(back.shape[0]):
             for o in range(CAP):
-                term = back[d, o * f + h * half : o * f + (h + 1) * half, :].astype(F32)
-                acc[rows, rows_at(sel[o, d], tile)] += term
+                term = back[p, o * f + h * half : o * f + (h + 1) * half, :].astype(F32)
+                acc[rows, rows_at(sel[o, p], tile)] += term
         copies.append(pltpu.make_async_copy(acc.at[rows, :], out.at[rows, :], sems.at[h]))
         copies[-1].start()
     for h in range(wg.shape[1] // tile):
@@ -285,15 +302,17 @@
     def mate(v, q):
         return lax.ppermute(v, "cols", [(i, i ^ q) for i in range(cols_n)])
 
+    order = order_of(rows_n)
+
     def over_rows(v):
-        return lax.all_to_all(v, "rows", 0, 0, tiled=True)
+        return lax.all_to_all(v, "rows", 0, 0, tiled=True, axis_index_groups=[order])
 
     adj_t = adj_index.T
     in_hbm = functools.partial(pltpu.with_memory_space_constraint, memory_space=pltpu.HBM)
     part = (rows_n, CAP, f, tile)
     piece = ("vmem", (units_loc, quarter), BF16)
     sel, feats, adj, sends = call(
-        choose_kernel, [HBM, HBM],
+        functools.partial(choose_kernel, order), [HBM, HBM],
         [("smem", (CAP, rows_n), I32), ("vmem", (f, nodes), BF16), ("vmem", adj_t.shape, I32),
          ("hbm", part, BF16)],
         [in_hbm(adj_t), in_hbm(feats_t)], [pltpu.SemaphoreType.DMA((3,))], mib=big,
@@ -318,7 +337,7 @@
         [in_hbm(adj_weight)], sems,
     )
     slot = call(
-        functools.partial(slot_kernel, blk), [VMEM],
+        functools.partial(slot_kernel, order, blk), [VMEM],
         [("smem", (slots_n, LANES), I32)], [adj],
         [pltpu.VMEM((slots_n, LANES), I32), pltpu.SemaphoreType.DMA], mib=big,
     )
@@ -355,25 +374,25 @@
         6 * f_in * units * quarter, 12,
     )
     g_came = mate(g_send, 2)
+    wg_part = ((f, units), F32)
+    wg_keep, wg_send = call(
+        wg_kernel, [VMEM] * 2, [("vmem", *wg_part)] * 2, [wg_keep, mate(wg_send, 1)]
+    )
     wg_came = mate(wg_send, 2)
 
     acc = call(
         functools.partial(spread_first_kernel, near), [SMEM, VMEM, VMEM],
         [("vmem", (table_n, fx, tile), F32)], [slot, a_near, g_keep], [], a_flops, big,
     )
-    wg_part = ((f, units), F32)
-    own, own_send, stay, send, wg_keep, wg_send = call(
-        functools.partial(spread_last_kernel, far), [SMEM] + [VMEM] * 5,
-        [("vmem", (f, nodes), F32)] * 2
-        + [("vmem", part, F32), ("vmem", part, BF16)]
-        + [("vmem", *wg_part)] * 2,
-        [slot, a_far, g_came, acc, wg_keep, wg_came],
-        [pltpu.VMEM((table_n, fx, tile), F32)], a_flops, big + 8,
+    own, own_send, stay, send = call(
+        functools.partial(spread_last_kernel, far), [SMEM] + [VMEM] * 3,
+        [("vmem", (f, nodes), F32)] * 2 + [("vmem", part, F32), ("vmem", part, BF16)],
+        [slot, a_far, g_came, acc], [pltpu.VMEM((table_n, fx, tile), F32)], a_flops, big + 8,
     )
     packed = ((rows_n, CAP * f + f * units // tile, tile), BF16)
     total = call(
         total_kernel, [VMEM] * 4, [("hbm", *packed)],
-        [stay, mate(send, 1), wg_keep, mate(wg_send, 1)],
+        [stay, mate(send, 1), wg_keep, wg_came],
         [pltpu.VMEM(*packed), pltpu.SemaphoreType.DMA((rows_n,))], mib=big,
     )
     back = over_rows(total)

time: 58.2 us -> 56.3 us (0.967)
  waiting for transfers between devices: 13.9 us -> 11.2 us
  starting transfers between devices: 12.2 us -> 14.7 us
  blocking collectives: 16 us -> 14.2 us
    all_to_all x1, waiting for transfers between devices: 5.71 us -> 0.87 us  [over_rows(): lax.all_to_all(v, 'rows', 0, 0, tiled=True, axis_index_groups=[order])]
    ppermute x14, waiting for transfers between devices: 8.2 us -> 10.3 us  [mate(): return lax.ppermute(v, 'cols', [(i, i ^ q) for i in range(cols_n)])]
    all_to_all x1, blocking collectives: 16 us -> 14.2 us  [over_rows(): lax.all_to_all(v, 'rows', 0, 0, tiled=True, axis_index_groups=[order])]
    all_to_all x1, starting transfers between devices: 3.6 us -> 5.07 us  [over_rows(): lax.all_to_all(v, 'rows', 0, 0, tiled=True, axis_index_groups=[order])]
    ppermute x14, starting transfers between devices: 8.58 us -> 9.68 us  [mate(): return lax.ppermute(v, 'cols', [(i, i ^ q) for i in range(cols_n)])]
    pallas_call x12 -> x13, Pallas kernels: 15 us -> 15 us  [call(): pl.pallas_call(kernel, out_shape=shapes, in_specs=in_specs, out_specs=spe...]
  transfers between devices with their start and end apart: 15 -> 15, of which waited for: 7 -> 7; matrix products, arithmetic and copies ran while one was open for 0% -> 0% of each run, Pallas kernels for 13% -> 14%
where the time goes in v4:
time: 56.3 us; the launch traced here: 55.9 us
  Pallas kernels  15 us (27%)
  starting transfers between devices  14.7 us (26%)
  blocking collectives  14.2 us (25%)
  waiting for transfers between devices  11.2 us (20%)
  between operations  0.77 us (1%)
    pallas_call x13, Pallas kernels, call(): pl.pallas_call(kernel, out_shape=shapes, in_specs=in_specs, out_specs=spe...  15 us
    all_to_all x1, blocking collectives, over_rows(): lax.all_to_all(v, 'rows', 0, 0, tiled=True, axis_index_groups=[order])  14.2 us
    ppermute x14, waiting for transfers between devices, mate(): return lax.ppermute(v, 'cols', [(i, i ^ q) for i in range(cols_n)])  10.3 us
    ppermute x14, starting transfers between devices, mate(): return lax.ppermute(v, 'cols', [(i, i ^ q) for i in range(cols_n)])  9.68 us
    all_to_all x1, starting transfers between devices, over_rows(): lax.all_to_all(v, 'rows', 0, 0, tiled=True, axis_index_groups=[order])  5.07 us
  transfers between devices with their start and end apart: 15, of which 7 were waited for; matrix products, arithmetic and copies ran while one was open for 0% of the time, Pallas kernels for 14%

profile of v4, /device:TPU:0, one launch (start us, length us, event | category | flops | bytes accessed | tf_op | source)
XLA Modules:
  0.0 55.9 jit_solution(6521678681695647668)
XLA Ops:
  0.6 4.1 %shard_map.76 = (s32[4,8]{1,0:T(4,128)S(4)}, bf16[32,2048]{1,0:T(8,128)(2,1)S(1)}, s32[16,128]{1,0:T(8,128)S(1)}, bf16[8,4,32,128]{3,2,1,0:T(8,128)(2,1)S(1)}) custom-call(s32[16,128]{1,0:T(8,128)} %bitcast.1, bf16[32,2048]{1,0:T(8,128)(2,1)} %feats.1), custom_call_target="tpu_custom_call" | custom-call | flops 1000000 | bytes 139264 | tf_op jit(solution)/shard_map/pallas_call | solution.py:35
  4.7 14.2 %all_to_all.10.got = bf16[8,4,32,128]{3,2,1,0:T(8,128)(2,1)S(1)} all-to-all(bf16[8,4,32,128]{3,2,1,0:T(8,128)(2,1)S(1)} %get-tuple-element.30), channel_id=1, replica_groups={{16,12,24,4,28,0,20,8},{17,13,25,5,29,1,21,9},{18,14,26,6,30,2,22,10},{..., dimensions={0} | all-to-all | bytes 524288 | tf_op jit(solution)/shard_map/all_to_all | solution.py:308
  19.0 0.0 collective-permute-start.1
  19.0 0.5 collective-permute-start
  19.5 1.7 %shard_map.80 = (bf16[4,16,128,128]{3,2,1,0:T(8,128)(2,1)S(1)}, bf16[64,512]{1,0:T(8,128)(2,1)S(1)}, bf16[64,512]{1,0:T(8,128)(2,1)S(1)}, bf16[64,512]{1,0:T(8,128)(2,1)S(1)}, bf16[64,512]{1,0:T(8,128)(2,1)S(1)}) custom-call(bf16[16,16,128,128]{3,2,1,0:T(8,128)(2,1)} %a_hbm.3, bf16[64,2048]{1,0:T(8,128)(2,1)} %rest_0_.1), custom_call_target="tpu_custom_call" | custom-call | flops 1000000 | bytes 8650752 | tf_op jit(solution)/shard_map/pallas_call | solution.py:35
  21.2 0.1 collective-permute-start.3
  21.3 1.6 %collective-permute-start.4 = (bf16[64,512]{1,0:T(8,128)(2,1)S(1)}, bf16[64,512]{1,0:T(8,128)(2,1)S(1)}, u32[]{:S(2)}, u32[]{:S(2)}) collective-permute-start(bf16[64,512]{1,0:T(8,128)(2,1)S(1)} %get-tuple-element.34), channel_id=1, source_target_pairs={{0,2},{1,3},{2,0},{3,1},{4,6},{5,7},{6,4},{7,5},{8,10},{9,11},{10,... | collective-permute-start | bytes 196616 | tf_op jit(solution)/shard_map/ppermute | solution.py:303
  22.8 0.3 collective-permute-start.5
  23.1 1.3 %shard_map.77.slot = s32[16,128]{1,0:T(8,128)S(4)} custom-call(s32[16,128]{1,0:T(8,128)S(1)} %get-tuple-element.28.adj_ref), custom_call_target="tpu_custom_call" | custom-call | flops 1000000 | bytes 8192 | tf_op jit(solution)/shard_map/pallas_call | solution.py:35
  24.4 0.0 collective-permute-done.mate
  24.4 0.0 collective-permute-done.1.got_mate
  24.4 0.9 %shard_map.81 = bf16[64,512]{1,0:T(8,128)(2,1)S(1)} custom-call(s32[16,128]{1,0:T(8,128)S(4)} %shard_map.77.slot, bf16[4,16,128,128]{3,2,1,0:T(8,128)(2,1)S(1)} %get-tuple-element.31.a_side, bf16[32,2048]{1,0:T(8,128)(2,1)S(1)} %get-tuple-element.29.mine, bf16[32,2048]{1,0:T(8,128)(2,1)S(1)} %collective-permute-done.mate, ...), custom_call_target="tpu_custom_call" | custom-call | flops 134217728 | bytes 2891776 | tf_op jit(solution)/shard_map/pallas_call | solution.py:35
  25.3 1.6 %collective-permute-start.2 = (bf16[64,512]{1,0:T(8,128)(2,1)S(1)}, bf16[64,512]{1,0:T(8,128)(2,1)S(1)}, u32[]{:S(2)}, u32[]{:S(2)}) collective-permute-start(bf16[64,512]{1,0:T(8,128)(2,1)S(1)} %shard_map.81), channel_id=1, source_target_pairs={{0,2},{1,3},{2,0},{3,1},{4,6},{5,7},{6,4},{7,5},{8,10},{9,11},{10,... | collective-permute-start | bytes 196616 | tf_op jit(solution)/shard_map/ppermute | solution.py:303
  26.9 1.6 %shard_map.78.a_side = bf16[4,16,128,128]{3,2,1,0:T(8,128)(2,1)S(1)} custom-call(bf16[16,16,128,128]{3,2,1,0:T(8,128)(2,1)} %a_hbm.3), custom_call_target="tpu_custom_call" | custom-call | flops 1000000 | bytes 8388608 | tf_op jit(solution)/shard_map/pallas_call | solution.py:35
  28.5 0.0 copy-start
  28.5 0.9 %shard_map.79.keep = bf16[64,512]{1,0:T(8,128)(2,1)S(1)} custom-call(s32[16,128]{1,0:T(8,128)S(4)} %shard_map.77.slot, bf16[4,16,128,128]{3,2,1,0:T(8,128)(2,1)S(1)} %shard_map.78.a_side, bf16[32,2048]{1,0:T(8,128)(2,1)S(1)} %get-tuple-element.29.mine, bf16[32,2048]{1,0:T(8,128)(2,1)S(1)} %collective-permute-done.mate, ...), custom_call_target="tpu_custom_call" | custom-call | flops 134217728 | bytes 2891776 | tf_op jit(solution)/shard_map/pallas_call | solution.py:35
  29.4 0.0 collective-permute-done.3.c1
  29.4 0.0 collective-permute-done.4.c2
  29.4 0.0 collective-permute-done.5.c3
  29.4 0.3 collective-permute-done.2.came
  29.8 0.0 copy-done
  29.8 0.6 %shard_map.82 = (bf16[64,512]{1,0:T(8,128)(2,1)S(1)}, bf16[64,512]{1,0:T(8,128)(2,1)S(1)}, bf16[64,512]{1,0:T(8,128)(2,1)S(1)}, bf16[64,512]{1,0:T(8,128)(2,1)S(...) custom-call(bf16[64,512]{1,0:T(8,128)(2,1)S(1)} %shard_map.79.keep, ...), custom_call_target="tpu_custom_call" | custom-call | flops 100663296 | bytes 458752 | tf_op jit(solution)/shard_map/pallas_call | solution.py:35
  30.4 1.6 %collective-permute-start.9 = (bf16[64,512]{1,0:T(8,128)(2,1)S(1)}, bf16[64,512]{1,0:T(8,128)(2,1)S(1)}, u32[]{:S(2)}, u32[]{:S(2)}) collective-permute-start(bf16[64,512]{1,0:T(8,128)(2,1)S(1)} %get-tuple-element.41), channel_id=1, source_target_pairs={{0,2},{1,3},{2,0},{3,1},{4,6},{5,7},{6,4},{7,5},{8,10},{9,11},{10,... | collective-permute-start | bytes 196616 | tf_op jit(solution)/shard_map/ppermute | solution.py:303
  31.9 0.6 %shard_map.84.before = f32[48,64,128]{2,1,0:T(8,128)S(1)} custom-call(s32[16,128]{1,0:T(8,128)S(4)} %shard_map.77.slot, bf16[4,16,128,128]{3,2,1,0:T(8,128)(2,1)S(1)} %shard_map.78.a_side, bf16[64,512]{1,0:T(8,128)(2,1)S(1)} %get-tuple-element.42.g_ref), custom_call_target="tpu_custom_call" | custom-call | flops 134217728 | bytes 2170880 | tf_op jit(solution)/shard_map/pallas_call | solution.py:35
  32.5 2.2 %collective-permute-done.9.g_ref = bf16[64,512]{1,0:T(8,128)(2,1)S(1)} collective-permute-done((bf16[64,512]{1,0:T(8,128)(2,1)S(1)}, bf16[64,512]{1,0:T(8,128)(2,1)S(1)}, u32[]{:S(2)}, u32[]{:S(2)}) %collective-permute-start.9) | collective-permute-done | bytes 65568 | tf_op jit(solution)/shard_map/ppermute | solution.py:303
  34.7 0.7 %shard_map.85 = (f32[32,2048]{1,0:T(8,128)S(1)}, f32[32,2048]{1,0:T(8,128)S(1)}, f32[8,4,32,128]{3,2,1,0:T(8,128)S(1)}, bf16[8,4,32,128]{3,2,1,0:T(8,128)(2,1)S(1)}) custom-call(s32[16,128]{1,0:T(8,128)S(4)} %shard_map.77.slot, bf16[4,16,128,128]{3,2,1,0:T(8,128)(2,1)S(1)} %get-tuple-element.31.a_side, bf16[64,512]{1,0:T(8,128)(2,1)S(1)} %collective-permute-done.9.g_ref, ...), custom_call_target="tpu_custom_call" | custom-call | flops 134217728 | bytes 3743744 | tf_op jit(solution)/shard_map/pallas_call | solution.py:35
  35.4 0.1 collective-permute-start.11
  35.5 0.5 collective-permute-start.12
  36.0 1.1 %collective-permute-done.12.came = f32[64,256]{1,0:T(8,128)S(1)} collective-permute-done((f32[64,256]{1,0:T(8,128)S(1)}, f32[64,256]{1,0:T(8,128)S(1)}, u32[]{:S(2)}, u32[]{:S(2)}) %collective-permute-start.12) | collective-permute-done | bytes 65568 | tf_op jit(solution)/shard_map/ppermute | solution.py:303
  37.1 1.6 %collective-permute-start.13 = (f32[32,256]{1,0:T(8,128)S(1)}, f32[32,256]{1,0:T(8,128)S(1)}, u32[]{:S(2)}, u32[]{:S(2)}) collective-permute-start(f32[32,256]{1,0:T(8,128)S(1)} %get-tuple-element.50), channel_id=1, source_target_pairs={{0,2},{1,3},{2,0},{3,1},{4,6},{5,7},{6,4},{7,5},{8,10},{9,11},{10,... | collective-permute-start | bytes 98312 | tf_op jit(solution)/shard_map/ppermute | solution.py:303
  38.7 2.4 %collective-permute-done.13.wg_came = f32[32,256]{1,0:T(8,128)S(1)} collective-permute-done((f32[32,256]{1,0:T(8,128)S(1)}, f32[32,256]{1,0:T(8,128)S(1)}, u32[]{:S(2)}, u32[]{:S(2)}) %collective-permute-start.13) | collective-permute-done | bytes 32800 | tf_op jit(solution)/shard_map/ppermute | solution.py:303
  41.1 0.0 collective-permute-done.11.came
  41.1 0.8 %shard_map.87 = bf16[8,192,128]{2,1,0:T(8,128)(2,1)} custom-call(f32[8,4,32,128]{3,2,1,0:T(8,128)S(1)} %get-tuple-element.45.stay, bf16[8,4,32,128]{3,2,1,0:T(8,128)(2,1)S(1)} %collective-permute-done.11.came, f32[32,256]{1,0:T(8,128)S(1)} %get-tuple-element.49.wg, f32[32,256]{1,0:T(8,128)S(1)} %collective-permute-done.13.wg_came), custom_call_target="tpu_custom_call" | custom-call | flops 1000000 | bytes 851968 | tf_op jit(solution)/shard_map/pallas_call | solution.py:35
  42.0 5.1 %all-to-all-start.1 = ((bf16[8,192,128]{2,1,0:T(8,128)(2,1)}), bf16[8,192,128]{2,1,0:T(8,128)(2,1)S(1)}, u32[]{:S(2)}, u32[]{:S(2)}) async-start(bf16[8,192,128]{2,1,0:T(8,128)(2,1)} %shard_map.87), calls=%async_computation.1 | async-start | bytes 786432 | tf_op jit(solution)/shard_map/all_to_all | solution.py:308
  47.0 0.0 collective-permute-start.10
  47.0 0.5 collective-permute-start.6
  47.5 1.5 %collective-permute-start.7 = (bf16[64,512]{1,0:T(8,128)(2,1)S(1)}, bf16[64,512]{1,0:T(8,128)(2,1)S(1)}, u32[]{:S(2)}, u32[]{:S(2)}) collective-permute-start(bf16[64,512]{1,0:T(8,128)(2,1)S(1)} %get-tuple-element.38), channel_id=1, source_target_pairs={{0,2},{1,3},{2,0},{3,1},{4,6},{5,7},{6,4},{7,5},{8,10},{9,11},{10,... | collective-permute-start | bytes 196616 | tf_op jit(solution)/shard_map/ppermute | solution.py:303
  49.0 0.0 collective-permute-start.8
  49.0 0.0 collective-permute-done.6.p1
  49.0 2.8 %collective-permute-done.7.p2 = bf16[64,512]{1,0:T(8,128)(2,1)S(1)} collective-permute-done((bf16[64,512]{1,0:T(8,128)(2,1)S(1)}, bf16[64,512]{1,0:T(8,128)(2,1)S(1)}, u32[]{:S(2)}, u32[]{:S(2)}) %collective-permute-start.7) | collective-permute-done | bytes 65568 | tf_op jit(solution)/shard_map/ppermute | solution.py:303
  51.8 1.5 %collective-permute-done.8.p3 = bf16[64,512]{1,0:T(8,128)(2,1)S(1)} collective-permute-done((bf16[64,512]{1,0:T(8,128)(2,1)S(1)}, bf16[64,512]{1,0:T(8,128)(2,1)S(1)}, u32[]{:S(2)}, u32[]{:S(2)}) %collective-permute-start.8) | collective-permute-done | bytes 65568 | tf_op jit(solution)/shard_map/ppermute | solution.py:303
  53.3 0.7 %shard_map.83 = bf16[64,2048]{1,0:T(8,128)(2,1)} custom-call(bf16[64,512]{1,0:T(8,128)(2,1)S(1)} %get-tuple-element.36.p0, bf16[64,512]{1,0:T(8,128)(2,1)S(1)} %collective-permute-done.6.p1, bf16[64,512]{1,0:T(8,128)(2,1)S(1)} %collective-permute-done.7.p2, bf16[64,512]{1,0:T(8,128)(2,1)S(1)} %collective-permute-done.8.p3), custom_call_target="tpu_custom_call" | custom-call | flops 1000000 | bytes 262144 | tf_op jit(solution)/shard_map/pallas_call | solution.py:35
  54.1 0.0 collective-permute-done.10.came
  54.1 0.9 %all-to-all-done.1.back = bf16[8,192,128]{2,1,0:T(8,128)(2,1)S(1)} async-done(((bf16[8,192,128]{2,1,0:T(8,128)(2,1)}), bf16[8,192,128]{2,1,0:T(8,128)(2,1)S(1)}, u32[]{:S(2)}, u32[]{:S(2)}) %all-to-all-start.1) | async-done | bytes 393248 | tf_op jit(solution)/shard_map/all_to_all | solution.py:308
  54.9 1.0 %shard_map.88 = (f32[32,2048]{1,0:T(8,128)}, f32[32,256]{1,0:T(8,128)}) custom-call(s32[4,8]{1,0:T(4,128)S(4)} %get-tuple-element.40.sel, f32[32,2048]{1,0:T(8,128)S(1)} %get-tuple-element.43.own, f32[32,2048]{1,0:T(8,128)S(1)} %collective-permute-done.10.came, bf16[8,192,128]{2,1,0:T(8,128)(2,1)S(1)} %all-to-all-done.1.back), custom_call_target="tpu_custom_call" | custom-call | flops 1000000 | bytes 917632 | tf_op jit(solution)/shard_map/pallas_call | solution.py:35
  (1 shorter events, 0.0 us)
Async XLA Ops:
  19.0 5.5 %collective-permute-start.1 = (bf16[8,4,32,128]{3,2,1,0:T(8,128)(2,1)S(1)}, bf16[8,4,32,128]{3,2,1,0:T(8,128)(2,1)S(1)}, u32[]{:S(2)}, u32[]{:S(2)}) collective-permute-start(bf16[8,4,32,128]{3,2,1,0:T(8,128)(2,1)S(1)} %all_to_all.10.got), channel_id=1, source_target_pairs={{0,1},{1,0},{2,3},{3,2},{4,5},{5,4},{6,7},{7,6},{8,9},{9,8},{10,11... | collective-permute-start | bytes 786440 | tf_op jit(solution)/shard_map/ppermute | solution.py:303
  19.0 5.5 %collective-permute-start = (bf16[32,2048]{1,0:T(8,128)(2,1)S(1)}, bf16[32,2048]{1,0:T(8,128)(2,1)S(1)}, u32[]{:S(2)}, u32[]{:S(2)}) collective-permute-start(bf16[32,2048]{1,0:T(8,128)(2,1)S(1)} %get-tuple-element.29.mine), channel_id=1, source_target_pairs={{0,1},{1,0},{2,3},{3,2},{4,5},{5,4},{6,7},{7,6},{8,9},{9,8},{10,11... | collective-permute-start | bytes 393224 | tf_op jit(solution)/shard_map/ppermute | solution.py:303
  21.2 8.2 %collective-permute-start.3 = (bf16[64,512]{1,0:T(8,128)(2,1)S(1)}, bf16[64,512]{1,0:T(8,128)(2,1)S(1)}, u32[]{:S(2)}, u32[]{:S(2)}) collective-permute-start(bf16[64,512]{1,0:T(8,128)(2,1)S(1)} %get-tuple-element.33), channel_id=1, source_target_pairs={{0,1},{1,0},{2,3},{3,2},{4,5},{5,4},{6,7},{7,6},{8,9},{9,8},{10,11... | collective-permute-start | bytes 196616 | tf_op jit(solution)/shard_map/ppermute | solution.py:303
  21.3 8.1 %collective-permute-start.4 = (bf16[64,512]{1,0:T(8,128)(2,1)S(1)}, bf16[64,512]{1,0:T(8,128)(2,1)S(1)}, u32[]{:S(2)}, u32[]{:S(2)}) collective-permute-start(bf16[64,512]{1,0:T(8,128)(2,1)S(1)} %get-tuple-element.34), channel_id=1, source_target_pairs={{0,2},{1,3},{2,0},{3,1},{4,6},{5,7},{6,4},{7,5},{8,10},{9,11},{10,... | collective-permute-start | bytes 196616 | tf_op jit(solution)/shard_map/ppermute | solution.py:303
  22.8 6.6 %collective-permute-start.5 = (bf16[64,512]{1,0:T(8,128)(2,1)S(1)}, bf16[64,512]{1,0:T(8,128)(2,1)S(1)}, u32[]{:S(2)}, u32[]{:S(2)}) collective-permute-start(bf16[64,512]{1,0:T(8,128)(2,1)S(1)} %get-tuple-element.35), channel_id=1, source_target_pairs={{0,3},{1,2},{2,1},{3,0},{4,7},{5,6},{6,5},{7,4},{8,11},{9,10},{10,... | collective-permute-start | bytes 196616 | tf_op jit(solution)/shard_map/ppermute | solution.py:303
  25.3 4.4 %collective-permute-start.2 = (bf16[64,512]{1,0:T(8,128)(2,1)S(1)}, bf16[64,512]{1,0:T(8,128)(2,1)S(1)}, u32[]{:S(2)}, u32[]{:S(2)}) collective-permute-start(bf16[64,512]{1,0:T(8,128)(2,1)S(1)} %shard_map.81), channel_id=1, source_target_pairs={{0,2},{1,3},{2,0},{3,1},{4,6},{5,7},{6,4},{7,5},{8,10},{9,11},{10,... | collective-permute-start | bytes 196616 | tf_op jit(solution)/shard_map/ppermute | solution.py:303
  28.5 1.3 %copy-start = (bf16[128,256]{1,0:T(8,128)(2,1)S(1)}, bf16[128,256]{1,0:T(8,128)(2,1)}, u32[]{:S(2)}) copy-start(bf16[128,256]{1,0:T(8,128)(2,1)} %w_ref.1) | copy-start | bytes 196612
  30.4 4.3 %collective-permute-start.9 = (bf16[64,512]{1,0:T(8,128)(2,1)S(1)}, bf16[64,512]{1,0:T(8,128)(2,1)S(1)}, u32[]{:S(2)}, u32[]{:S(2)}) collective-permute-start(bf16[64,512]{1,0:T(8,128)(2,1)S(1)} %get-tuple-element.41), channel_id=1, source_target_pairs={{0,2},{1,3},{2,0},{3,1},{4,6},{5,7},{6,4},{7,5},{8,10},{9,11},{10,... | collective-permute-start | bytes 196616 | tf_op jit(solution)/shard_map/ppermute | solution.py:303
  35.4 5.7 %collective-permute-start.11 = (bf16[8,4,32,128]{3,2,1,0:T(8,128)(2,1)S(1)}, bf16[8,4,32,128]{3,2,1,0:T(8,128)(2,1)S(1)}, u32[]{:S(2)}, u32[]{:S(2)}) collective-permute-start(bf16[8,4,32,128]{3,2,1,0:T(8,128)(2,1)S(1)} %get-tuple-element.46), channel_id=1, source_target_pairs={{0,1},{1,0},{2,3},{3,2},{4,5},{5,4},{6,7},{7,6},{8,9},{9,8},{10,11... | collective-permute-start | bytes 786440 | tf_op jit(solution)/shard_map/ppermute | solution.py:303
  35.5 1.6 %collective-permute-start.12 = (f32[64,256]{1,0:T(8,128)S(1)}, f32[64,256]{1,0:T(8,128)S(1)}, u32[]{:S(2)}, u32[]{:S(2)}) collective-permute-start(f32[64,256]{1,0:T(8,128)S(1)} %get-tuple-element.48), channel_id=1, source_target_pairs={{0,1},{1,0},{2,3},{3,2},{4,5},{5,4},{6,7},{7,6},{8,9},{9,8},{10,11... | collective-permute-start | bytes 196616 | tf_op jit(solution)/shard_map/ppermute | solution.py:303
  37.1 4.0 %collective-permute-start.13 = (f32[32,256]{1,0:T(8,128)S(1)}, f32[32,256]{1,0:T(8,128)S(1)}, u32[]{:S(2)}, u32[]{:S(2)}) collective-permute-start(f32[32,256]{1,0:T(8,128)S(1)} %get-tuple-element.50), channel_id=1, source_target_pairs={{0,2},{1,3},{2,0},{3,1},{4,6},{5,7},{6,4},{7,5},{8,10},{9,11},{10,... | collective-permute-start | bytes 98312 | tf_op jit(solution)/shard_map/ppermute | solution.py:303
  42.0 13.0 %all-to-all-start.1 = ((bf16[8,192,128]{2,1,0:T(8,128)(2,1)}), bf16[8,192,128]{2,1,0:T(8,128)(2,1)S(1)}, u32[]{:S(2)}, u32[]{:S(2)}) async-start(bf16[8,192,128]{2,1,0:T(8,128)(2,1)} %shard_map.87), calls=%async_computation.1 | async-start | bytes 786432 | tf_op jit(solution)/shard_map/all_to_all | solution.py:308
  47.0 7.0 %collective-permute-start.10 = (f32[32,2048]{1,0:T(8,128)S(1)}, f32[32,2048]{1,0:T(8,128)S(1)}, u32[]{:S(2)}, u32[]{:S(2)}) collective-permute-start(f32[32,2048]{1,0:T(8,128)S(1)} %get-tuple-element.44), channel_id=1, source_target_pairs={{0,1},{1,0},{2,3},{3,2},{4,5},{5,4},{6,7},{7,6},{8,9},{9,8},{10,11... | collective-permute-start | bytes 786440 | tf_op jit(solution)/shard_map/ppermute | solution.py:303
  47.0 2.0 %collective-permute-start.6 = (bf16[64,512]{1,0:T(8,128)(2,1)S(1)}, bf16[64,512]{1,0:T(8,128)(2,1)S(1)}, u32[]{:S(2)}, u32[]{:S(2)}) collective-permute-start(bf16[64,512]{1,0:T(8,128)(2,1)S(1)} %get-tuple-element.37), channel_id=1, source_target_pairs={{0,1},{1,0},{2,3},{3,2},{4,5},{5,4},{6,7},{7,6},{8,9},{9,8},{10,11... | collective-permute-start | bytes 196616 | tf_op jit(solution)/shard_map/ppermute | solution.py:303
  47.5 4.3 %collective-permute-start.7 = (bf16[64,512]{1,0:T(8,128)(2,1)S(1)}, bf16[64,512]{1,0:T(8,128)(2,1)S(1)}, u32[]{:S(2)}, u32[]{:S(2)}) collective-permute-start(bf16[64,512]{1,0:T(8,128)(2,1)S(1)} %get-tuple-element.38), channel_id=1, source_target_pairs={{0,2},{1,3},{2,0},{3,1},{4,6},{5,7},{6,4},{7,5},{8,10},{9,11},{10,... | collective-permute-start | bytes 196616 | tf_op jit(solution)/shard_map/ppermute | solution.py:303
  49.0 4.3 %collective-permute-start.8 = (bf16[64,512]{1,0:T(8,128)(2,1)S(1)}, bf16[64,512]{1,0:T(8,128)(2,1)S(1)}, u32[]{:S(2)}, u32[]{:S(2)}) collective-permute-start(bf16[64,512]{1,0:T(8,128)(2,1)S(1)} %get-tuple-element.39), channel_id=1, source_target_pairs={{0,3},{1,2},{2,1},{3,0},{4,7},{5,6},{6,5},{7,4},{8,11},{9,10},{10,... | collective-permute-start | bytes 196616 | tf_op jit(solution)/shard_map/ppermute | solution.py:303

commit v5 on v4

--- a/solution.py
+++ b/solution.py
@@ -25,6 +25,12 @@
         at = sum(((gray >> b) & 1) << (bits - 1 - b) for b in range(bits)) + rows_n // 2
         order += [at, rows_n - 1 - at]
     return order
+
+
+def back_order_of(rows_n):
+    pairs = rows_n // 2
+    middle = [*range(pairs // 2, pairs), *range(pairs // 2 - 1, -1, -1)]
+    return [2 * i for i in middle] + [2 * i + 1 for i in middle]
 
 
 def call(kernel, in_specs, outs, args, scratch=(), flops=10**6, mib=8):
@@ -85,7 +91,7 @@
     for p, d in enumerate(order):
         for o in range(CAP):
             at = picks[o][0, d]
-            sel[o, p] = at
+            sel[o, d] = at
             source = copied.at[:, rows_at(at, tile)]
             pltpu.make_async_copy(source, sends.at[p, o], sems.at[2]).start()
     pltpu.make_async_copy(sends, sends, sems.at[2]).wait()
@@ -116,17 +122,14 @@
     copy.wait()
 
 
-def fetch_kernel(side_of, a_hbm, *rest):
+def fetch_kernel(side_of, a_hbm, cot, a_side, c0, c1, c2, c3, sems):
     _, c, x = position()
+    pieces = (c0, c1, c2, c3)
+    width = c0.shape[1]
     copies = []
-    if len(rest) > 2:
-        cot, a_side, *pieces, sems = rest
-        width = pieces[0].shape[1]
-        for q in (1, 2, 3, 0):
-            at = rows_at((c ^ (q & 1)) * 2 + (x ^ (q >> 1)), width)
-            copies.append(pltpu.make_async_copy(cot.at[:, at], pieces[q], sems.at[q]))
-    else:
-        a_side, sems = rest
+    for q in (1, 2, 3, 0):
+        at = rows_at((c ^ (q & 1)) * 2 + (x ^ (q >> 1)), width)
+        copies.append(pltpu.make_async_copy(cot.at[:, at], pieces[q], sems.at[q]))
     n = a_side.shape[0]
     first = (2 * c + side_of(x)) * n
     for i in range(n):
@@ -137,11 +140,11 @@
         copy.wait()
 
 
-def gather_kernel(side_of, slot, a_side, mine, mate, got, got_mate, out, table):
+def gather(side_of, slot, a_side, mine, mate, got, got_mate, out, table, ready=None):
     r, c, x = position()
     f = mine.shape[0]
     top, low = rows_at(c, f), rows_at(1 - c, f)
-    tile = a_side.shape[3]
+    n, slots_n, tile, _ = a_side.shape
     blk = mine.shape[1] // tile
     for b in range(blk):
         table[b, top, :] = mine[:, b * tile : (b + 1) * tile]
@@ -150,9 +153,10 @@
         for o in range(CAP):
             table[blk + d * CAP + o, top, :] = got[d, o]
             table[blk + d * CAP + o, low, :] = got_mate[d, o]
-    n, slots_n, tile, _ = a_side.shape
     lane = lax.rem(r * 4 * n, LANES) + (2 * c + side_of(x)) * n
     for t in range(n):
+        if ready is not None:
+            ready[t].wait()
         acc = None
         for k in range(0, slots_n, 2):
             left = [table[slot[k + h, lane + t]] for h in range(2)]
@@ -165,6 +169,18 @@
             )
             acc = part if acc is None else acc + part
         out[:, t * tile : (t + 1) * tile] = acc.astype(BF16)
+
+
+def gather_near_kernel(side_of, slot, a_hbm, *rest):
+    mine, mate, got, got_mate, out, a_side, table, sems = rest
+    _, c, x = position()
+    n = a_side.shape[0]
+    first = (2 * c + side_of(x)) * n
+    copies = []
+    for i in range(n):
+        copies.append(pltpu.make_async_copy(a_hbm.at[first + i], a_side.at[i], sems.at[i]))
+        copies[-1].start()
+    gather(side_of, slot, a_side, mine, mate, got, got_mate, out, table, copies)
 
 
 def dense_kernel(keep, came, w_ref, c0, c1, c2, c3, *rest):
@@ -221,7 +237,7 @@
     spread(side_of, slot, a_side, g_ref, acc)
 
 
-def spread_last_kernel(side_of, slot, a_side, g_ref, before, own, own_send, stay, send, acc):
+def spread_last_kernel(side_of, out_order, back_order, slot, a_side, g_ref, before, own, own_send, stay, send, acc):
     acc[...] = before[...]
     spread(side_of, slot, a_side, g_ref, acc)
     _, c, _ = position()
@@ -229,10 +245,11 @@
     top, low = rows_at(c, f), rows_at(1 - c, f)
     tile = a_side.shape[3]
     blk = own.shape[1] // tile
-    for d in range(send.shape[0]):
+    for p, d in enumerate(back_order):
+        at = blk + out_order.index(d) * CAP
         for o in range(CAP):
-            stay[d, o] = acc[blk + d * CAP + o, top, :]
-            send[d, o] = acc[blk + d * CAP + o, low, :].astype(BF16)
+            stay[p, o] = acc[at + o, top, :]
+            send[p, o] = acc[at + o, low, :].astype(BF16)
     for b in range(blk):
         own[:, b * tile : (b + 1) * tile] = acc[b, top, :]
         own_send[:, b * tile : (b + 1) * tile] = acc[b, low, :]
@@ -254,7 +271,7 @@
         copy.wait()
 
 
-def collect_kernel(scale, sel, own, came, back, out, wg_out, acc, wg, sems):
+def collect_kernel(scale, back_order, sel, own, came, back, out, wg_out, acc, wg, sems):
     tile = back.shape[2]
     f = own.shape[0]
     half = f // 2
@@ -262,10 +279,10 @@
     for h in range(2):
         rows = slice(h * half, (h + 1) * half)
         acc[rows, :] = own[rows, :] + came[rows, :]
-        for p in range(back.shape[0]):
+        for p, d in enumerate(back_order):
             for o in range(CAP):
                 term = back[p, o * f + h * half : o * f + (h + 1) * half, :].astype(F32)
-                acc[rows, rows_at(sel[o, p], tile)] += term
+                acc[rows, rows_at(sel[o, d], tile)] += term
         copies.append(pltpu.make_async_copy(acc.at[rows, :], out.at[rows, :], sems.at[h]))
         copies[-1].start()
     for h in range(wg.shape[1] // tile):
@@ -302,9 +319,9 @@
     def mate(v, q):
         return lax.ppermute(v, "cols", [(i, i ^ q) for i in range(cols_n)])
 
-    order = order_of(rows_n)
-
-    def over_rows(v):
+    out_order, back_order = order_of(rows_n), back_order_of(rows_n)
+
+    def over_rows(v, order):
         return lax.all_to_all(v, "rows", 0, 0, tiled=True, axis_index_groups=[order])
 
     adj_t = adj_index.T
@@ -312,13 +329,13 @@
     part = (rows_n, CAP, f, tile)
     piece = ("vmem", (units_loc, quarter), BF16)
     sel, feats, adj, sends = call(
-        functools.partial(choose_kernel, order), [HBM, HBM],
+        functools.partial(choose_kernel, out_order), [HBM, HBM],
         [("smem", (CAP, rows_n), I32), ("vmem", (f, nodes), BF16), ("vmem", adj_t.shape, I32),
          ("hbm", part, BF16)],
         [in_hbm(adj_t), in_hbm(feats_t)], [pltpu.SemaphoreType.DMA((3,))], mib=big,
     )
     feats_mate = mate(feats, 1)
-    got = over_rows(sends)
+    got = over_rows(sends, out_order)
 
     def far(x):
         return 1 - x
@@ -332,12 +349,8 @@
         functools.partial(fetch_kernel, far), [HBM, HBM], [a_side] + [piece] * 4,
         [in_hbm(adj_weight), in_hbm(cotangent_t)], sems,
     )
-    a_near = call(
-        functools.partial(fetch_kernel, near), [HBM], [a_side],
-        [in_hbm(adj_weight)], sems,
-    )
     slot = call(
-        functools.partial(slot_kernel, order, blk), [VMEM],
+        functools.partial(slot_kernel, out_order, blk), [VMEM],
         [("smem", (slots_n, LANES), I32)], [adj],
         [pltpu.VMEM((slots_n, LANES), I32), pltpu.SemaphoreType.DMA], mib=big,
     )
@@ -348,17 +361,18 @@
 
     half_g = ("vmem", (fx, quarter), BF16)
 
-    def gather(side_of, a_side):
-        args = [slot, a_side, feats, feats_mate, got, got_mate]
-        return call(
-            functools.partial(gather_kernel, side_of), [SMEM] + [VMEM] * (len(args) - 1),
-            [half_g], args, [pltpu.VMEM((table_n, fx, tile), BF16)], a_flops,
-            big,
-        )
-
-    agg_far = gather(far, a_far)
+    tables = [feats, feats_mate, got, got_mate]
+    table = pltpu.VMEM((table_n, fx, tile), BF16)
+    agg_far = call(
+        functools.partial(gather, far), [SMEM] + [VMEM] * 5, [half_g],
+        [slot, a_far, *tables], [table], a_flops, big,
+    )
     agg_came = mate(agg_far, 2)
-    agg_near = gather(near, a_near)
+    agg_near, a_near = call(
+        functools.partial(gather_near_kernel, near), [SMEM, HBM] + [VMEM] * 4,
+        [half_g, a_side], [slot, in_hbm(adj_weight), *tables],
+        [table, pltpu.SemaphoreType.DMA((blk // 4,))], a_flops, big,
+    )
 
     args = [agg_near, agg_came, weight, *cots]
     *outs, g_send, g_keep, wg_send, wg_keep = call(
@@ -385,7 +399,7 @@
         [("vmem", (table_n, fx, tile), F32)], [slot, a_near, g_keep], [], a_flops, big,
     )
     own, own_send, stay, send = call(
-        functools.partial(spread_last_kernel, far), [SMEM] + [VMEM] * 3,
+        functools.partial(spread_last_kernel, far, out_order, back_order), [SMEM] + [VMEM] * 3,
         [("vmem", (f, nodes), F32)] * 2 + [("vmem", part, F32), ("vmem", part, BF16)],
         [slot, a_far, g_came, acc], [pltpu.VMEM((table_n, fx, tile), F32)], a_flops, big + 8,
     )
@@ -395,10 +409,10 @@
         [stay, mate(send, 1), wg_keep, wg_came],
         [pltpu.VMEM(*packed), pltpu.SemaphoreType.DMA((rows_n,))], mib=big,
     )
-    back = over_rows(total)
+    back = over_rows(total, back_order)
     own_came = mate(own_send, 1)
     feat_grad, weight_grad = call(
-        functools.partial(collect_kernel, 1.0 / math.sqrt(nodes * rows_n)),
+        functools.partial(collect_kernel, 1.0 / math.sqrt(nodes * rows_n), back_order),
         [SMEM, VMEM, VMEM, VMEM], [("hbm", (f, nodes), F32), ("hbm", *wg_part)],
         [sel, own, own_came, back],
         [pltpu.VMEM((f, nodes), F32), pltpu.VMEM(*wg_part), pltpu.SemaphoreType.DMA((3,))],

time: 56.3 us -> 55.4 us (0.984)
  waiting for transfers between devices: 11.2 us -> 10.1 us
    all_to_all x1, waiting for transfers between devices: 0.87 us -> 0.01 us  [over_rows(): lax.all_to_all(v, 'rows', 0, 0, tiled=True, axis_index_groups=[order])]
    pallas_call x13 -> x12, Pallas kernels: 15 us -> 15.3 us  [call(): pl.pallas_call(kernel, out_shape=shapes, in_specs=in_specs, out_specs=spe...]
  transfers between devices with their start and end apart: 15 -> 15, of which waited for: 7 -> 6; matrix products, arithmetic and copies ran while one was open for 0% -> 0% of each run, Pallas kernels for 14% -> 15%
where the time goes in v5:
time: 55.4 us; the launch traced here: 55.1 us
  Pallas kernels  15.3 us (28%)
  starting transfers between devices  14.7 us (27%)
  blocking collectives  14.2 us (26%)
  waiting for transfers between devices  10.1 us (18%)
  between operations  0.77 us (1%)
    pallas_call x12, Pallas kernels, call(): pl.pallas_call(kernel, out_shape=shapes, in_specs=in_specs, out_specs=spe...  15.3 us
    all_to_all x1, blocking collectives, over_rows(): lax.all_to_all(v, 'rows', 0, 0, tiled=True, axis_index_groups=[order])  14.2 us
    ppermute x14, waiting for transfers between devices, mate(): return lax.ppermute(v, 'cols', [(i, i ^ q) for i in range(cols_n)])  10.1 us
    ppermute x14, starting transfers between devices, mate(): return lax.ppermute(v, 'cols', [(i, i ^ q) for i in range(cols_n)])  9.66 us
    all_to_all x1, starting transfers between devices, over_rows(): lax.all_to_all(v, 'rows', 0, 0, tiled=True, axis_index_groups=[order])  5.07 us
  transfers between devices with their start and end apart: 15, of which 6 were waited for; matrix products, arithmetic and copies ran while one was open for 0% of the time, Pallas kernels for 15%

profile of v5, /device:TPU:0, one launch (start us, length us, event | category | flops | bytes accessed | tf_op | source)
XLA Modules:
  0.0 55.1 jit_solution(3978293571368819942)
XLA Ops:
  0.6 4.1 %shard_map.76 = (s32[4,8]{1,0:T(4,128)S(4)}, bf16[32,2048]{1,0:T(8,128)(2,1)S(1)}, s32[16,128]{1,0:T(8,128)S(1)}, bf16[8,4,32,128]{3,2,1,0:T(8,128)(2,1)S(1)}) custom-call(s32[16,128]{1,0:T(8,128)} %bitcast.1, bf16[32,2048]{1,0:T(8,128)(2,1)} %feats.1), custom_call_target="tpu_custom_call" | custom-call | flops 1000000 | bytes 139264 | tf_op jit(solution)/shard_map/pallas_call | solution.py:41
  4.7 14.2 %all_to_all.10.rest_2_.got = bf16[8,4,32,128]{3,2,1,0:T(8,128)(2,1)S(1)} all-to-all(bf16[8,4,32,128]{3,2,1,0:T(8,128)(2,1)S(1)} %get-tuple-element.32), channel_id=1, replica_groups={{16,12,24,4,28,0,20,8},{17,13,25,5,29,1,21,9},{18,14,26,6,30,2,22,10},{..., dimensions={0} | all-to-all | bytes 524288 | tf_op jit(solution)/shard_map/all_to_all | solution.py:325
  19.0 0.0 collective-permute-start.1
  19.0 0.5 collective-permute-start
  19.5 1.7 %shard_map.79 = (bf16[4,16,128,128]{3,2,1,0:T(8,128)(2,1)S(1)}, bf16[64,512]{1,0:T(8,128)(2,1)S(1)}, bf16[64,512]{1,0:T(8,128)(2,1)S(1)}, bf16[64,512]{1,0:T(8,128)(2,1)S(1)}, bf16[64,512]{1,0:T(8,128)(2,1)S(1)}) custom-call(bf16[16,16,128,128]{3,2,1,0:T(8,128)(2,1)} %a_hbm.3, bf16[64,2048]{1,0:T(8,128)(2,1)} %cot.1), custom_call_target="tpu_custom_call" | custom-call | flops 1000000 | bytes 8650752 | tf_op jit(solution)/shard_map/pallas_call | solution.py:41
  21.2 0.1 collective-permute-start.3
  21.3 1.6 %collective-permute-start.4 = (bf16[64,512]{1,0:T(8,128)(2,1)S(1)}, bf16[64,512]{1,0:T(8,128)(2,1)S(1)}, u32[]{:S(2)}, u32[]{:S(2)}) collective-permute-start(bf16[64,512]{1,0:T(8,128)(2,1)S(1)} %get-tuple-element.37), channel_id=1, source_target_pairs={{0,2},{1,3},{2,0},{3,1},{4,6},{5,7},{6,4},{7,5},{8,10},{9,11},{10,... | collective-permute-start | bytes 196616 | tf_op jit(solution)/shard_map/ppermute | solution.py:320
  22.8 0.3 collective-permute-start.5
  23.1 1.3 %shard_map.77.slot = s32[16,128]{1,0:T(8,128)S(4)} custom-call(s32[16,128]{1,0:T(8,128)S(1)} %get-tuple-element.30.adj_ref), custom_call_target="tpu_custom_call" | custom-call | flops 1000000 | bytes 8192 | tf_op jit(solution)/shard_map/pallas_call | solution.py:41
  24.4 0.0 collective-permute-done.rest_1_.mate
  24.4 0.0 collective-permute-done.1.rest_3_.got_mate
  24.4 0.9 %shard_map.80 = bf16[64,512]{1,0:T(8,128)(2,1)S(1)} custom-call(s32[16,128]{1,0:T(8,128)S(4)} %shard_map.77.slot, bf16[4,16,128,128]{3,2,1,0:T(8,128)(2,1)S(1)} %get-tuple-element.34.a_side, bf16[32,2048]{1,0:T(8,128)(2,1)S(1)} %get-tuple-element.31.rest_0_.mine, bf16[32,2048]{1,0:T(8,128)(2,1)S(1)} %collective-permute-done.rest_1_.mate, ...), custom_call_target="tpu_custom_call" | custom-call | flops 134217728 | bytes 2891776 | tf_op jit(solution)/shard_map/pallas_call | solution.py:41
  25.3 0.0 copy-start
  25.3 1.6 %collective-permute-start.2 = (bf16[64,512]{1,0:T(8,128)(2,1)S(1)}, bf16[64,512]{1,0:T(8,128)(2,1)S(1)}, u32[]{:S(2)}, u32[]{:S(2)}) collective-permute-start(bf16[64,512]{1,0:T(8,128)(2,1)S(1)} %shard_map.80), channel_id=1, source_target_pairs={{0,2},{1,3},{2,0},{3,1},{4,6},{5,7},{6,4},{7,5},{8,10},{9,11},{10,... | collective-permute-start | bytes 196616 | tf_op jit(solution)/shard_map/ppermute | solution.py:320
  26.9 2.7 %shard_map.78 = (bf16[64,512]{1,0:T(8,128)(2,1)S(1)}, bf16[4,16,128,128]{3,2,1,0:T(8,128)(2,1)S(1)}) custom-call(s32[16,128]{1,0:T(8,128)S(4)} %shard_map.77.slot, bf16[16,16,128,128]{3,2,1,0:T(8,128)(2,1)} %a_hbm.3, bf16[32,2048]{1,0:T(8,128)(2,1)S(1)} %get-tuple-element.31.rest_0_.mine, bf16[32,2048]{1,0:T(8,128)(2,1)S(1)} %collective-permute-done.rest_1_.mate, ...), custom_call_target="tpu_custom_call" | custom-call | flops 134217728 | bytes 9183232 | tf_op jit(solution)/shard_map/pallas_call | solution.py:41
  29.6 0.0 collective-permute-done.3.c1
  29.7 0.0 collective-permute-done.4.c2
  29.7 0.0 collective-permute-done.5.c3
  29.7 0.1 collective-permute-done.2.came
  29.8 0.0 copy-done
  29.8 0.6 %shard_map.81 = (bf16[64,512]{1,0:T(8,128)(2,1)S(1)}, bf16[64,512]{1,0:T(8,128)(2,1)S(1)}, bf16[64,512]{1,0:T(8,128)(2,1)S(1)}, bf16[64,512]{1,0:T(8,128)(2,1)S(...) custom-call(bf16[64,512]{1,0:T(8,128)(2,1)S(1)} %get-tuple-element.3, ...), custom_call_target="tpu_custom_call" | custom-call | flops 100663296 | bytes 458752 | tf_op jit(solution)/shard_map/pallas_call | solution.py:41
  30.4 1.6 %collective-permute-start.9 = (bf16[64,512]{1,0:T(8,128)(2,1)S(1)}, bf16[64,512]{1,0:T(8,128)(2,1)S(1)}, u32[]{:S(2)}, u32[]{:S(2)}) collective-permute-start(bf16[64,512]{1,0:T(8,128)(2,1)S(1)} %get-tuple-element.44), channel_id=1, source_target_pairs={{0,2},{1,3},{2,0},{3,1},{4,6},{5,7},{6,4},{7,5},{8,10},{9,11},{10,... | collective-permute-start | bytes 196616 | tf_op jit(solution)/shard_map/ppermute | solution.py:320
  31.9 0.6 %shard_map.83.before = f32[48,64,128]{2,1,0:T(8,128)S(1)} custom-call(s32[16,128]{1,0:T(8,128)S(4)} %shard_map.77.slot, bf16[4,16,128,128]{3,2,1,0:T(8,128)(2,1)S(1)} %get-tuple-element.45.a_side, bf16[64,512]{1,0:T(8,128)(2,1)S(1)} %get-tuple-element.46.g_ref), custom_call_target="tpu_custom_call" | custom-call | flops 134217728 | bytes 2170880 | tf_op jit(solution)/shard_map/pallas_call | solution.py:41
  32.6 2.1 %collective-permute-done.9.g_ref = bf16[64,512]{1,0:T(8,128)(2,1)S(1)} collective-permute-done((bf16[64,512]{1,0:T(8,128)(2,1)S(1)}, bf16[64,512]{1,0:T(8,128)(2,1)S(1)}, u32[]{:S(2)}, u32[]{:S(2)}) %collective-permute-start.9) | collective-permute-done | bytes 65568 | tf_op jit(solution)/shard_map/ppermute | solution.py:320
  34.7 0.7 %shard_map.84 = (f32[32,2048]{1,0:T(8,128)S(1)}, f32[32,2048]{1,0:T(8,128)S(1)}, f32[8,4,32,128]{3,2,1,0:T(8,128)S(1)}, bf16[8,4,32,128]{3,2,1,0:T(8,128)(2,1)S(1)}) custom-call(s32[16,128]{1,0:T(8,128)S(4)} %shard_map.77.slot, bf16[4,16,128,128]{3,2,1,0:T(8,128)(2,1)S(1)} %get-tuple-element.34.a_side, bf16[64,512]{1,0:T(8,128)(2,1)S(1)} %collective-permute-done.9.g_ref, ...), custom_call_target="tpu_custom_call" | custom-call | flops 134217728 | bytes 3743744 | tf_op jit(solution)/shard_map/pallas_call | solution.py:41
  35.5 0.1 collective-permute-start.11
  35.5 0.5 collective-permute-start.12
  36.0 1.1 %collective-permute-done.12.came = f32[64,256]{1,0:T(8,128)S(1)} collective-permute-done((f32[64,256]{1,0:T(8,128)S(1)}, f32[64,256]{1,0:T(8,128)S(1)}, u32[]{:S(2)}, u32[]{:S(2)}) %collective-permute-start.12) | collective-permute-done | bytes 65568 | tf_op jit(solution)/shard_map/ppermute | solution.py:320
  37.2 1.5 %collective-permute-start.13 = (f32[32,256]{1,0:T(8,128)S(1)}, f32[32,256]{1,0:T(8,128)S(1)}, u32[]{:S(2)}, u32[]{:S(2)}) collective-permute-start(f32[32,256]{1,0:T(8,128)S(1)} %get-tuple-element.54), channel_id=1, source_target_pairs={{0,2},{1,3},{2,0},{3,1},{4,6},{5,7},{6,4},{7,5},{8,10},{9,11},{10,... | collective-permute-start | bytes 98312 | tf_op jit(solution)/shard_map/ppermute | solution.py:320
  38.7 2.4 %collective-permute-done.13.wg_came = f32[32,256]{1,0:T(8,128)S(1)} collective-permute-done((f32[32,256]{1,0:T(8,128)S(1)}, f32[32,256]{1,0:T(8,128)S(1)}, u32[]{:S(2)}, u32[]{:S(2)}) %collective-permute-start.13) | collective-permute-done | bytes 32800 | tf_op jit(solution)/shard_map/ppermute | solution.py:320
  41.1 0.0 collective-permute-done.11.came
  41.1 0.8 %shard_map.86 = bf16[8,192,128]{2,1,0:T(8,128)(2,1)} custom-call(f32[8,4,32,128]{3,2,1,0:T(8,128)S(1)} %get-tuple-element.49.stay, bf16[8,4,32,128]{3,2,1,0:T(8,128)(2,1)S(1)} %collective-permute-done.11.came, f32[32,256]{1,0:T(8,128)S(1)} %get-tuple-element.53.wg, f32[32,256]{1,0:T(8,128)S(1)} %collective-permute-done.13.wg_came), custom_call_target="tpu_custom_call" | custom-call | flops 1000000 | bytes 851968 | tf_op jit(solution)/shard_map/pallas_call | solution.py:41
  42.0 5.1 %all-to-all-start.1 = ((bf16[8,192,128]{2,1,0:T(8,128)(2,1)}), bf16[8,192,128]{2,1,0:T(8,128)(2,1)S(1)}, u32[]{:S(2)}, u32[]{:S(2)}) async-start(bf16[8,192,128]{2,1,0:T(8,128)(2,1)} %shard_map.86), calls=%async_computation.1 | async-start | bytes 786432 | tf_op jit(solution)/shard_map/all_to_all | solution.py:325
  47.0 0.0 collective-permute-start.10
  47.0 0.5 collective-permute-start.6
  47.6 1.5 %collective-permute-start.7 = (bf16[64,512]{1,0:T(8,128)(2,1)S(1)}, bf16[64,512]{1,0:T(8,128)(2,1)S(1)}, u32[]{:S(2)}, u32[]{:S(2)}) collective-permute-start(bf16[64,512]{1,0:T(8,128)(2,1)S(1)} %get-tuple-element.41), channel_id=1, source_target_pairs={{0,2},{1,3},{2,0},{3,1},{4,6},{5,7},{6,4},{7,5},{8,10},{9,11},{10,... | collective-permute-start | bytes 196616 | tf_op jit(solution)/shard_map/ppermute | solution.py:320
  49.0 0.0 collective-permute-start.8
  49.0 0.0 collective-permute-done.6.p1
  49.1 2.8 %collective-permute-done.7.p2 = bf16[64,512]{1,0:T(8,128)(2,1)S(1)} collective-permute-done((bf16[64,512]{1,0:T(8,128)(2,1)S(1)}, bf16[64,512]{1,0:T(8,128)(2,1)S(1)}, u32[]{:S(2)}, u32[]{:S(2)}) %collective-permute-start.7) | collective-permute-done | bytes 65568 | tf_op jit(solution)/shard_map/ppermute | solution.py:320
  51.8 1.5 %collective-permute-done.8.p3 = bf16[64,512]{1,0:T(8,128)(2,1)S(1)} collective-permute-done((bf16[64,512]{1,0:T(8,128)(2,1)S(1)}, bf16[64,512]{1,0:T(8,128)(2,1)S(1)}, u32[]{:S(2)}, u32[]{:S(2)}) %collective-permute-start.8) | collective-permute-done | bytes 65568 | tf_op jit(solution)/shard_map/ppermute | solution.py:320
  53.3 0.7 %shard_map.82 = bf16[64,2048]{1,0:T(8,128)(2,1)} custom-call(bf16[64,512]{1,0:T(8,128)(2,1)S(1)} %get-tuple-element.39.p0, bf16[64,512]{1,0:T(8,128)(2,1)S(1)} %collective-permute-done.6.p1, bf16[64,512]{1,0:T(8,128)(2,1)S(1)} %collective-permute-done.7.p2, bf16[64,512]{1,0:T(8,128)(2,1)S(1)} %collective-permute-done.8.p3), custom_call_target="tpu_custom_call" | custom-call | flops 1000000 | bytes 262144 | tf_op jit(solution)/shard_map/pallas_call | solution.py:41
  54.1 0.0 collective-permute-done.10.came
  54.1 0.0 all-to-all-done.1.back
  54.1 1.0 %shard_map.87 = (f32[32,2048]{1,0:T(8,128)}, f32[32,256]{1,0:T(8,128)}) custom-call(s32[4,8]{1,0:T(4,128)S(4)} %get-tuple-element.43.sel, f32[32,2048]{1,0:T(8,128)S(1)} %get-tuple-element.47.own, f32[32,2048]{1,0:T(8,128)S(1)} %collective-permute-done.10.came, bf16[8,192,128]{2,1,0:T(8,128)(2,1)S(1)} %all-to-all-done.1.back), custom_call_target="tpu_custom_call" | custom-call | flops 1000000 | bytes 917632 | tf_op jit(solution)/shard_map/pallas_call | solution.py:41
  (1 shorter events, 0.0 us)
Async XLA Ops:
  19.0 5.5 %collective-permute-start.1 = (bf16[8,4,32,128]{3,2,1,0:T(8,128)(2,1)S(1)}, bf16[8,4,32,128]{3,2,1,0:T(8,128)(2,1)S(1)}, u32[]{:S(2)}, u32[]{:S(2)}) collective-permute-start(bf16[8,4,32,128]{3,2,1,0:T(8,128)(2,1)S(1)} %all_to_all.10.rest_2_.got), channel_id=1, source_target_pairs={{0,1},{1,0},{2,3},{3,2},{4,5},{5,4},{6,7},{7,6},{8,9},{9,8},{10,11... | collective-permute-start | bytes 786440 | tf_op jit(solution)/shard_map/ppermute | solution.py:320
  19.0 5.5 %collective-permute-start = (bf16[32,2048]{1,0:T(8,128)(2,1)S(1)}, bf16[32,2048]{1,0:T(8,128)(2,1)S(1)}, u32[]{:S(2)}, u32[]{:S(2)}) collective-permute-start(bf16[32,2048]{1,0:T(8,128)(2,1)S(1)} %get-tuple-element.31.rest_0_.mine), channel_id=1, source_target_pairs={{0,1},{1,0},{2,3},{3,2},{4,5},{5,4},{6,7},{7,6},{8,9},{9,8},{10,11... | collective-permute-start | bytes 393224 | tf_op jit(solution)/shard_map/ppermute | solution.py:320
  21.2 8.4 %collective-permute-start.3 = (bf16[64,512]{1,0:T(8,128)(2,1)S(1)}, bf16[64,512]{1,0:T(8,128)(2,1)S(1)}, u32[]{:S(2)}, u32[]{:S(2)}) collective-permute-start(bf16[64,512]{1,0:T(8,128)(2,1)S(1)} %get-tuple-element.36), channel_id=1, source_target_pairs={{0,1},{1,0},{2,3},{3,2},{4,5},{5,4},{6,7},{7,6},{8,9},{9,8},{10,11... | collective-permute-start | bytes 196616 | tf_op jit(solution)/shard_map/ppermute | solution.py:320
  21.3 8.4 %collective-permute-start.4 = (bf16[64,512]{1,0:T(8,128)(2,1)S(1)}, bf16[64,512]{1,0:T(8,128)(2,1)S(1)}, u32[]{:S(2)}, u32[]{:S(2)}) collective-permute-start(bf16[64,512]{1,0:T(8,128)(2,1)S(1)} %get-tuple-element.37), channel_id=1, source_target_pairs={{0,2},{1,3},{2,0},{3,1},{4,6},{5,7},{6,4},{7,5},{8,10},{9,11},{10,... | collective-permute-start | bytes 196616 | tf_op jit(solution)/shard_map/ppermute | solution.py:320
  22.8 6.8 %collective-permute-start.5 = (bf16[64,512]{1,0:T(8,128)(2,1)S(1)}, bf16[64,512]{1,0:T(8,128)(2,1)S(1)}, u32[]{:S(2)}, u32[]{:S(2)}) collective-permute-start(bf16[64,512]{1,0:T(8,128)(2,1)S(1)} %get-tuple-element.38), channel_id=1, source_target_pairs={{0,3},{1,2},{2,1},{3,0},{4,7},{5,6},{6,5},{7,4},{8,11},{9,10},{10,... | collective-permute-start | bytes 196616 | tf_op jit(solution)/shard_map/ppermute | solution.py:320
  25.3 4.4 %copy-start = (bf16[128,256]{1,0:T(8,128)(2,1)S(1)}, bf16[128,256]{1,0:T(8,128)(2,1)}, u32[]{:S(2)}) copy-start(bf16[128,256]{1,0:T(8,128)(2,1)} %w_ref.1) | copy-start | bytes 196612
  25.3 4.4 %collective-permute-start.2 = (bf16[64,512]{1,0:T(8,128)(2,1)S(1)}, bf16[64,512]{1,0:T(8,128)(2,1)S(1)}, u32[]{:S(2)}, u32[]{:S(2)}) collective-permute-start(bf16[64,512]{1,0:T(8,128)(2,1)S(1)} %shard_map.80), channel_id=1, source_target_pairs={{0,2},{1,3},{2,0},{3,1},{4,6},{5,7},{6,4},{7,5},{8,10},{9,11},{10,... | collective-permute-start | bytes 196616 | tf_op jit(solution)/shard_map/ppermute | solution.py:320
  30.4 4.3 %collective-permute-start.9 = (bf16[64,512]{1,0:T(8,128)(2,1)S(1)}, bf16[64,512]{1,0:T(8,128)(2,1)S(1)}, u32[]{:S(2)}, u32[]{:S(2)}) collective-permute-start(bf16[64,512]{1,0:T(8,128)(2,1)S(1)} %get-tuple-element.44), channel_id=1, source_target_pairs={{0,2},{1,3},{2,0},{3,1},{4,6},{5,7},{6,4},{7,5},{8,10},{9,11},{10,... | collective-permute-start | bytes 196616 | tf_op jit(solution)/shard_map/ppermute | solution.py:320
  35.5 5.7 %collective-permute-start.11 = (bf16[8,4,32,128]{3,2,1,0:T(8,128)(2,1)S(1)}, bf16[8,4,32,128]{3,2,1,0:T(8,128)(2,1)S(1)}, u32[]{:S(2)}, u32[]{:S(2)}) collective-permute-start(bf16[8,4,32,128]{3,2,1,0:T(8,128)(2,1)S(1)} %get-tuple-element.50), channel_id=1, source_target_pairs={{0,1},{1,0},{2,3},{3,2},{4,5},{5,4},{6,7},{7,6},{8,9},{9,8},{10,11... | collective-permute-start | bytes 786440 | tf_op jit(solution)/shard_map/ppermute | solution.py:320
  35.5 1.6 %collective-permute-start.12 = (f32[64,256]{1,0:T(8,128)S(1)}, f32[64,256]{1,0:T(8,128)S(1)}, u32[]{:S(2)}, u32[]{:S(2)}) collective-permute-start(f32[64,256]{1,0:T(8,128)S(1)} %get-tuple-element.52), channel_id=1, source_target_pairs={{0,1},{1,0},{2,3},{3,2},{4,5},{5,4},{6,7},{7,6},{8,9},{9,8},{10,11... | collective-permute-start | bytes 196616 | tf_op jit(solution)/shard_map/ppermute | solution.py:320
  37.2 4.0 %collective-permute-start.13 = (f32[32,256]{1,0:T(8,128)S(1)}, f32[32,256]{1,0:T(8,128)S(1)}, u32[]{:S(2)}, u32[]{:S(2)}) collective-permute-start(f32[32,256]{1,0:T(8,128)S(1)} %get-tuple-element.54), channel_id=1, source_target_pairs={{0,2},{1,3},{2,0},{3,1},{4,6},{5,7},{6,4},{7,5},{8,10},{9,11},{10,... | collective-permute-start | bytes 98312 | tf_op jit(solution)/shard_map/ppermute | solution.py:320
  42.0 12.1 %all-to-all-start.1 = ((bf16[8,192,128]{2,1,0:T(8,128)(2,1)}), bf16[8,192,128]{2,1,0:T(8,128)(2,1)S(1)}, u32[]{:S(2)}, u32[]{:S(2)}) async-start(bf16[8,192,128]{2,1,0:T(8,128)(2,1)} %shard_map.86), calls=%async_computation.1 | async-start | bytes 786432 | tf_op jit(solution)/shard_map/all_to_all | solution.py:325
  47.0 7.0 %collective-permute-start.10 = (f32[32,2048]{1,0:T(8,128)S(1)}, f32[32,2048]{1,0:T(8,128)S(1)}, u32[]{:S(2)}, u32[]{:S(2)}) collective-permute-start(f32[32,2048]{1,0:T(8,128)S(1)} %get-tuple-element.48), channel_id=1, source_target_pairs={{0,1},{1,0},{2,3},{3,2},{4,5},{5,4},{6,7},{7,6},{8,9},{9,8},{10,11... | collective-permute-start | bytes 786440 | tf_op jit(solution)/shard_map/ppermute | solution.py:320
  47.0 2.0 %collective-permute-start.6 = (bf16[64,512]{1,0:T(8,128)(2,1)S(1)}, bf16[64,512]{1,0:T(8,128)(2,1)S(1)}, u32[]{:S(2)}, u32[]{:S(2)}) collective-permute-start(bf16[64,512]{1,0:T(8,128)(2,1)S(1)} %get-tuple-element.40), channel_id=1, source_target_pairs={{0,1},{1,0},{2,3},{3,2},{4,5},{5,4},{6,7},{7,6},{8,9},{9,8},{10,11... | collective-permute-start | bytes 196616 | tf_op jit(solution)/shard_map/ppermute | solution.py:320
  47.6 4.3 %collective-permute-start.7 = (bf16[64,512]{1,0:T(8,128)(2,1)S(1)}, bf16[64,512]{1,0:T(8,128)(2,1)S(1)}, u32[]{:S(2)}, u32[]{:S(2)}) collective-permute-start(bf16[64,512]{1,0:T(8,128)(2,1)S(1)} %get-tuple-element.41), channel_id=1, source_target_pairs={{0,2},{1,3},{2,0},{3,1},{4,6},{5,7},{6,4},{7,5},{8,10},{9,11},{10,... | collective-permute-start | bytes 196616 | tf_op jit(solution)/shard_map/ppermute | solution.py:320
  49.0 4.3 %collective-permute-start.8 = (bf16[64,512]{1,0:T(8,128)(2,1)S(1)}, bf16[64,512]{1,0:T(8,128)(2,1)S(1)}, u32[]{:S(2)}, u32[]{:S(2)}) collective-permute-start(bf16[64,512]{1,0:T(8,128)(2,1)S(1)} %get-tuple-element.42), channel_id=1, source_target_pairs={{0,3},{1,2},{2,1},{3,0},{4,7},{5,6},{6,5},{7,4},{8,11},{9,10},{10,... | collective-permute-start | bytes 196616 | tf_op jit(solution)/shard_map/ppermute | solution.py:320

commit v6 on v5

--- a/solution.py
+++ b/solution.py
@@ -15,6 +15,7 @@
 SMEM = pl.BlockSpec(memory_space=pltpu.SMEM)
 HBM = pl.BlockSpec(memory_space=pltpu.HBM)
 MIB = 1 << 20
+BACK_ORDERS = {8: (4, 1, 3, 6, 2, 0, 5, 7)}
 
 
 def order_of(rows_n):
@@ -28,6 +29,8 @@
 
 
 def back_order_of(rows_n):
+    if rows_n in BACK_ORDERS:
+        return list(BACK_ORDERS[rows_n])
     pairs = rows_n // 2
     middle = [*range(pairs // 2, pairs), *range(pairs // 2 - 1, -1, -1)]
     return [2 * i for i in middle] + [2 * i + 1 for i in middle]
@@ -140,7 +143,7 @@
         copy.wait()
 
 
-def gather(side_of, slot, a_side, mine, mate, got, got_mate, out, table, ready=None):
+def gather(side_of, slot, a_side, mine, mate, got, got_mate, out, table):
     r, c, x = position()
     f = mine.shape[0]
     top, low = rows_at(c, f), rows_at(1 - c, f)
@@ -155,24 +158,21 @@
             table[blk + d * CAP + o, low, :] = got_mate[d, o]
     lane = lax.rem(r * 4 * n, LANES) + (2 * c + side_of(x)) * n
     for t in range(n):
-        if ready is not None:
-            ready[t].wait()
         acc = None
         for k in range(0, slots_n, 2):
             left = [table[slot[k + h, lane + t]] for h in range(2)]
             right = [a_side[t, k + h] for h in range(2)]
             part = lax.dot_general(
+                jnp.concatenate(right, axis=1),
                 jnp.concatenate(left, axis=1),
-                jnp.concatenate(right, axis=1),
                 (((1,), (1,)), ((), ())),
                 preferred_element_type=F32,
             )
             acc = part if acc is None else acc + part
-        out[:, t * tile : (t + 1) * tile] = acc.astype(BF16)
-
-
-def gather_near_kernel(side_of, slot, a_hbm, *rest):
-    mine, mate, got, got_mate, out, a_side, table, sems = rest
+        out[:, t * tile : (t + 1) * tile] = acc.T.astype(BF16)
+
+
+def fetch_near_kernel(side_of, a_hbm, a_side, sems):
     _, c, x = position()
     n = a_side.shape[0]
     first = (2 * c + side_of(x)) * n
@@ -180,7 +180,8 @@
     for i in range(n):
         copies.append(pltpu.make_async_copy(a_hbm.at[first + i], a_side.at[i], sems.at[i]))
         copies[-1].start()
-    gather(side_of, slot, a_side, mine, mate, got, got_mate, out, table, copies)
+    for copy in copies:
+        copy.wait()
 
 
 def dense_kernel(keep, came, w_ref, c0, c1, c2, c3, *rest):
@@ -368,10 +369,13 @@
         [slot, a_far, *tables], [table], a_flops, big,
     )
     agg_came = mate(agg_far, 2)
-    agg_near, a_near = call(
-        functools.partial(gather_near_kernel, near), [SMEM, HBM] + [VMEM] * 4,
-        [half_g, a_side], [slot, in_hbm(adj_weight), *tables],
-        [table, pltpu.SemaphoreType.DMA((blk // 4,))], a_flops, big,
+    a_near = call(
+        functools.partial(fetch_near_kernel, near), [HBM], [a_side],
+        [in_hbm(adj_weight)], [pltpu.SemaphoreType.DMA((blk // 4,))],
+    )
+    agg_near = call(
+        functools.partial(gather, near), [SMEM] + [VMEM] * 5, [half_g],
+        [slot, a_near, *tables], [table], a_flops, big,
     )
 
     args = [agg_near, agg_came, weight, *cots]

time: 55.4 us -> 56.1 us (1.013)
  waiting for transfers between devices: 10.1 us -> 11.2 us
    all_to_all x1, waiting for transfers between devices: 0.01 us -> 0.79 us  [over_rows(): lax.all_to_all(v, 'rows', 0, 0, tiled=True, axis_index_groups=[order])]
    pallas_call x12 -> x13, Pallas kernels: 15.3 us -> 14.8 us  [call(): pl.pallas_call(kernel, out_shape=shapes, in_specs=in_specs, out_specs=spe...]
  transfers between devices with their start and end apart: 15 -> 15, of which waited for: 6 -> 7; matrix products, arithmetic and copies ran while one was open for 0% -> 0% of each run, Pallas kernels for 15% -> 14%
where the time goes in v6:
time: 56.1 us; the launch traced here: 55.8 us
  Pallas kernels  14.8 us (26%)
  starting transfers between devices  14.7 us (26%)
  blocking collectives  14.2 us (25%)
  waiting for transfers between devices  11.2 us (20%)
  between operations  0.78 us (1%)
    pallas_call x13, Pallas kernels, call(): pl.pallas_call(kernel, out_shape=shapes, in_specs=in_specs, out_specs=spe...  14.8 us
    all_to_all x1, blocking collectives, over_rows(): lax.all_to_all(v, 'rows', 0, 0, tiled=True, axis_index_groups=[order])  14.2 us
    ppermute x14, waiting for transfers between devices, mate(): return lax.ppermute(v, 'cols', [(i, i ^ q) for i in range(cols_n)])  10.4 us
    ppermute x14, starting transfers between devices, mate(): return lax.ppermute(v, 'cols', [(i, i ^ q) for i in range(cols_n)])  9.65 us
    all_to_all x1, starting transfers between devices, over_rows(): lax.all_to_all(v, 'rows', 0, 0, tiled=True, axis_index_groups=[order])  5.07 us
  transfers between devices with their start and end apart: 15, of which 7 were waited for; matrix products, arithmetic and copies ran while one was open for 0% of the time, Pallas kernels for 14%

profile of v6, /device:TPU:0, one launch (start us, length us, event | category | flops | bytes accessed | tf_op | source)
XLA Modules:
  0.0 55.8 jit_solution(11157588212121126011)
XLA Ops:
  0.6 4.1 %shard_map.76 = (s32[4,8]{1,0:T(4,128)S(4)}, bf16[32,2048]{1,0:T(8,128)(2,1)S(1)}, s32[16,128]{1,0:T(8,128)S(1)}, bf16[8,4,32,128]{3,2,1,0:T(8,128)(2,1)S(1)}) custom-call(s32[16,128]{1,0:T(8,128)} %bitcast.1, bf16[32,2048]{1,0:T(8,128)(2,1)} %feats.1), custom_call_target="tpu_custom_call" | custom-call | flops 1000000 | bytes 139264 | tf_op jit(solution)/shard_map/pallas_call | solution.py:44
  4.7 14.2 %all_to_all.10.got = bf16[8,4,32,128]{3,2,1,0:T(8,128)(2,1)S(1)} all-to-all(bf16[8,4,32,128]{3,2,1,0:T(8,128)(2,1)S(1)} %get-tuple-element.30), channel_id=1, replica_groups={{16,12,24,4,28,0,20,8},{17,13,25,5,29,1,21,9},{18,14,26,6,30,2,22,10},{..., dimensions={0} | all-to-all | bytes 524288 | tf_op jit(solution)/shard_map/all_to_all | solution.py:326
  19.0 0.0 collective-permute-start.1
  19.0 0.5 collective-permute-start
  19.5 1.7 %shard_map.80 = (bf16[4,16,128,128]{3,2,1,0:T(8,128)(2,1)S(1)}, bf16[64,512]{1,0:T(8,128)(2,1)S(1)}, bf16[64,512]{1,0:T(8,128)(2,1)S(1)}, bf16[64,512]{1,0:T(8,128)(2,1)S(1)}, bf16[64,512]{1,0:T(8,128)(2,1)S(1)}) custom-call(bf16[16,16,128,128]{3,2,1,0:T(8,128)(2,1)} %a_hbm.3, bf16[64,2048]{1,0:T(8,128)(2,1)} %cot.1), custom_call_target="tpu_custom_call" | custom-call | flops 1000000 | bytes 8650752 | tf_op jit(solution)/shard_map/pallas_call | solution.py:44
  21.2 0.1 collective-permute-start.3
  21.3 1.6 %collective-permute-start.4 = (bf16[64,512]{1,0:T(8,128)(2,1)S(1)}, bf16[64,512]{1,0:T(8,128)(2,1)S(1)}, u32[]{:S(2)}, u32[]{:S(2)}) collective-permute-start(bf16[64,512]{1,0:T(8,128)(2,1)S(1)} %get-tuple-element.34), channel_id=1, source_target_pairs={{0,2},{1,3},{2,0},{3,1},{4,6},{5,7},{6,4},{7,5},{8,10},{9,11},{10,... | collective-permute-start | bytes 196616 | tf_op jit(solution)/shard_map/ppermute | solution.py:321
  22.8 0.3 collective-permute-start.5
  23.1 1.3 %shard_map.77.slot = s32[16,128]{1,0:T(8,128)S(4)} custom-call(s32[16,128]{1,0:T(8,128)S(1)} %get-tuple-element.28.adj_ref), custom_call_target="tpu_custom_call" | custom-call | flops 1000000 | bytes 8192 | tf_op jit(solution)/shard_map/pallas_call | solution.py:44
  24.4 0.0 collective-permute-done.mate
  24.4 0.0 collective-permute-done.1.got_mate
  24.4 0.8 %shard_map.81 = bf16[64,512]{1,0:T(8,128)(2,1)S(1)} custom-call(s32[16,128]{1,0:T(8,128)S(4)} %shard_map.77.slot, bf16[4,16,128,128]{3,2,1,0:T(8,128)(2,1)S(1)} %get-tuple-element.31.a_side, bf16[32,2048]{1,0:T(8,128)(2,1)S(1)} %get-tuple-element.29.mine, bf16[32,2048]{1,0:T(8,128)(2,1)S(1)} %collective-permute-done.mate, ...), custom_call_target="tpu_custom_call" | custom-call | flops 134217728 | bytes 2891776 | tf_op jit(solution)/shard_map/pallas_call | solution.py:44
  25.3 1.6 %collective-permute-start.2 = (bf16[64,512]{1,0:T(8,128)(2,1)S(1)}, bf16[64,512]{1,0:T(8,128)(2,1)S(1)}, u32[]{:S(2)}, u32[]{:S(2)}) collective-permute-start(bf16[64,512]{1,0:T(8,128)(2,1)S(1)} %shard_map.81), channel_id=1, source_target_pairs={{0,2},{1,3},{2,0},{3,1},{4,6},{5,7},{6,4},{7,5},{8,10},{9,11},{10,... | collective-permute-start | bytes 196616 | tf_op jit(solution)/shard_map/ppermute | solution.py:321
  26.8 1.5 %shard_map.78.a_side = bf16[4,16,128,128]{3,2,1,0:T(8,128)(2,1)S(1)} custom-call(bf16[16,16,128,128]{3,2,1,0:T(8,128)(2,1)} %a_hbm.3), custom_call_target="tpu_custom_call" | custom-call | flops 1000000 | bytes 8388608 | tf_op jit(solution)/shard_map/pallas_call | solution.py:44
  28.4 0.0 copy-start
  28.4 0.8 %shard_map.79.keep = bf16[64,512]{1,0:T(8,128)(2,1)S(1)} custom-call(s32[16,128]{1,0:T(8,128)S(4)} %shard_map.77.slot, bf16[4,16,128,128]{3,2,1,0:T(8,128)(2,1)S(1)} %shard_map.78.a_side, bf16[32,2048]{1,0:T(8,128)(2,1)S(1)} %get-tuple-element.29.mine, bf16[32,2048]{1,0:T(8,128)(2,1)S(1)} %collective-permute-done.mate, ...), custom_call_target="tpu_custom_call" | custom-call | flops 134217728 | bytes 2891776 | tf_op jit(solution)/shard_map/pallas_call | solution.py:44
  29.2 0.0 collective-permute-done.3.c1
  29.2 0.0 collective-permute-done.4.c2
  29.3 0.0 collective-permute-done.5.c3
  29.3 0.4 collective-permute-done.2.came
  29.7 0.0 copy-done
  29.7 0.6 %shard_map.82 = (bf16[64,512]{1,0:T(8,128)(2,1)S(1)}, bf16[64,512]{1,0:T(8,128)(2,1)S(1)}, bf16[64,512]{1,0:T(8,128)(2,1)S(1)}, bf16[64,512]{1,0:T(8,128)(2,1)S(...) custom-call(bf16[64,512]{1,0:T(8,128)(2,1)S(1)} %shard_map.79.keep, ...), custom_call_target="tpu_custom_call" | custom-call | flops 100663296 | bytes 458752 | tf_op jit(solution)/shard_map/pallas_call | solution.py:44
  30.3 1.6 %collective-permute-start.9 = (bf16[64,512]{1,0:T(8,128)(2,1)S(1)}, bf16[64,512]{1,0:T(8,128)(2,1)S(1)}, u32[]{:S(2)}, u32[]{:S(2)}) collective-permute-start(bf16[64,512]{1,0:T(8,128)(2,1)S(1)} %get-tuple-element.41), channel_id=1, source_target_pairs={{0,2},{1,3},{2,0},{3,1},{4,6},{5,7},{6,4},{7,5},{8,10},{9,11},{10,... | collective-permute-start | bytes 196616 | tf_op jit(solution)/shard_map/ppermute | solution.py:321
  31.9 0.6 %shard_map.84.before = f32[48,64,128]{2,1,0:T(8,128)S(1)} custom-call(s32[16,128]{1,0:T(8,128)S(4)} %shard_map.77.slot, bf16[4,16,128,128]{3,2,1,0:T(8,128)(2,1)S(1)} %shard_map.78.a_side, bf16[64,512]{1,0:T(8,128)(2,1)S(1)} %get-tuple-element.42.g_ref), custom_call_target="tpu_custom_call" | custom-call | flops 134217728 | bytes 2170880 | tf_op jit(solution)/shard_map/pallas_call | solution.py:44
  32.5 2.1 %collective-permute-done.9.g_ref = bf16[64,512]{1,0:T(8,128)(2,1)S(1)} collective-permute-done((bf16[64,512]{1,0:T(8,128)(2,1)S(1)}, bf16[64,512]{1,0:T(8,128)(2,1)S(1)}, u32[]{:S(2)}, u32[]{:S(2)}) %collective-permute-start.9) | collective-permute-done | bytes 65568 | tf_op jit(solution)/shard_map/ppermute | solution.py:321
  34.6 0.7 %shard_map.85 = (f32[32,2048]{1,0:T(8,128)S(1)}, f32[32,2048]{1,0:T(8,128)S(1)}, f32[8,4,32,128]{3,2,1,0:T(8,128)S(1)}, bf16[8,4,32,128]{3,2,1,0:T(8,128)(2,1)S(1)}) custom-call(s32[16,128]{1,0:T(8,128)S(4)} %shard_map.77.slot, bf16[4,16,128,128]{3,2,1,0:T(8,128)(2,1)S(1)} %get-tuple-element.31.a_side, bf16[64,512]{1,0:T(8,128)(2,1)S(1)} %collective-permute-done.9.g_ref, ...), custom_call_target="tpu_custom_call" | custom-call | flops 134217728 | bytes 3743744 | tf_op jit(solution)/shard_map/pallas_call | solution.py:44
  35.4 0.1 collective-permute-start.11
  35.5 0.5 collective-permute-start.12
  36.0 1.1 %collective-permute-done.12.came = f32[64,256]{1,0:T(8,128)S(1)} collective-permute-done((f32[64,256]{1,0:T(8,128)S(1)}, f32[64,256]{1,0:T(8,128)S(1)}, u32[]{:S(2)}, u32[]{:S(2)}) %collective-permute-start.12) | collective-permute-done | bytes 65568 | tf_op jit(solution)/shard_map/ppermute | solution.py:321
  37.1 1.5 %collective-permute-start.13 = (f32[32,256]{1,0:T(8,128)S(1)}, f32[32,256]{1,0:T(8,128)S(1)}, u32[]{:S(2)}, u32[]{:S(2)}) collective-permute-start(f32[32,256]{1,0:T(8,128)S(1)} %get-tuple-element.50), channel_id=1, source_target_pairs={{0,2},{1,3},{2,0},{3,1},{4,6},{5,7},{6,4},{7,5},{8,10},{9,11},{10,... | collective-permute-start | bytes 98312 | tf_op jit(solution)/shard_map/ppermute | solution.py:321
  38.6 2.4 %collective-permute-done.13.wg_came = f32[32,256]{1,0:T(8,128)S(1)} collective-permute-done((f32[32,256]{1,0:T(8,128)S(1)}, f32[32,256]{1,0:T(8,128)S(1)}, u32[]{:S(2)}, u32[]{:S(2)}) %collective-permute-start.13) | collective-permute-done | bytes 32800 | tf_op jit(solution)/shard_map/ppermute | solution.py:321
  41.1 0.0 collective-permute-done.11.came
  41.1 0.8 %shard_map.87 = bf16[8,192,128]{2,1,0:T(8,128)(2,1)} custom-call(f32[8,4,32,128]{3,2,1,0:T(8,128)S(1)} %get-tuple-element.45.stay, bf16[8,4,32,128]{3,2,1,0:T(8,128)(2,1)S(1)} %collective-permute-done.11.came, f32[32,256]{1,0:T(8,128)S(1)} %get-tuple-element.49.wg, f32[32,256]{1,0:T(8,128)S(1)} %collective-permute-done.13.wg_came), custom_call_target="tpu_custom_call" | custom-call | flops 1000000 | bytes 851968 | tf_op jit(solution)/shard_map/pallas_call | solution.py:44
  41.9 5.1 %all-to-all-start.1 = ((bf16[8,192,128]{2,1,0:T(8,128)(2,1)}), bf16[8,192,128]{2,1,0:T(8,128)(2,1)S(1)}, u32[]{:S(2)}, u32[]{:S(2)}) async-start(bf16[8,192,128]{2,1,0:T(8,128)(2,1)} %shard_map.87), calls=%async_computation.1 | async-start | bytes 786432 | tf_op jit(solution)/shard_map/all_to_all | solution.py:326
  47.0 0.0 collective-permute-start.10
  47.0 0.5 collective-permute-start.6
  47.5 1.5 %collective-permute-start.7 = (bf16[64,512]{1,0:T(8,128)(2,1)S(1)}, bf16[64,512]{1,0:T(8,128)(2,1)S(1)}, u32[]{:S(2)}, u32[]{:S(2)}) collective-permute-start(bf16[64,512]{1,0:T(8,128)(2,1)S(1)} %get-tuple-element.38), channel_id=1, source_target_pairs={{0,2},{1,3},{2,0},{3,1},{4,6},{5,7},{6,4},{7,5},{8,10},{9,11},{10,... | collective-permute-start | bytes 196616 | tf_op jit(solution)/shard_map/ppermute | solution.py:321
  49.0 0.0 collective-permute-start.8
  49.0 0.0 collective-permute-done.6.p1
  49.0 2.8 %collective-permute-done.7.p2 = bf16[64,512]{1,0:T(8,128)(2,1)S(1)} collective-permute-done((bf16[64,512]{1,0:T(8,128)(2,1)S(1)}, bf16[64,512]{1,0:T(8,128)(2,1)S(1)}, u32[]{:S(2)}, u32[]{:S(2)}) %collective-permute-start.7) | collective-permute-done | bytes 65568 | tf_op jit(solution)/shard_map/ppermute | solution.py:321
  51.8 1.5 %collective-permute-done.8.p3 = bf16[64,512]{1,0:T(8,128)(2,1)S(1)} collective-permute-done((bf16[64,512]{1,0:T(8,128)(2,1)S(1)}, bf16[64,512]{1,0:T(8,128)(2,1)S(1)}, u32[]{:S(2)}, u32[]{:S(2)}) %collective-permute-start.8) | collective-permute-done | bytes 65568 | tf_op jit(solution)/shard_map/ppermute | solution.py:321
  53.3 0.7 %shard_map.83 = bf16[64,2048]{1,0:T(8,128)(2,1)} custom-call(bf16[64,512]{1,0:T(8,128)(2,1)S(1)} %get-tuple-element.36.p0, bf16[64,512]{1,0:T(8,128)(2,1)S(1)} %collective-permute-done.6.p1, bf16[64,512]{1,0:T(8,128)(2,1)S(1)} %collective-permute-done.7.p2, bf16[64,512]{1,0:T(8,128)(2,1)S(1)} %collective-permute-done.8.p3), custom_call_target="tpu_custom_call" | custom-call | flops 1000000 | bytes 262144 | tf_op jit(solution)/shard_map/pallas_call | solution.py:44
  54.0 0.0 collective-permute-done.10.came
  54.0 0.8 %all-to-all-done.1.back = bf16[8,192,128]{2,1,0:T(8,128)(2,1)S(1)} async-done(((bf16[8,192,128]{2,1,0:T(8,128)(2,1)}), bf16[8,192,128]{2,1,0:T(8,128)(2,1)S(1)}, u32[]{:S(2)}, u32[]{:S(2)}) %all-to-all-start.1) | async-done | bytes 393248 | tf_op jit(solution)/shard_map/all_to_all | solution.py:326
  54.8 1.0 %shard_map.88 = (f32[32,2048]{1,0:T(8,128)}, f32[32,256]{1,0:T(8,128)}) custom-call(s32[4,8]{1,0:T(4,128)S(4)} %get-tuple-element.40.sel, f32[32,2048]{1,0:T(8,128)S(1)} %get-tuple-element.43.own, f32[32,2048]{1,0:T(8,128)S(1)} %collective-permute-done.10.came, bf16[8,192,128]{2,1,0:T(8,128)(2,1)S(1)} %all-to-all-done.1.back), custom_call_target="tpu_custom_call" | custom-call | flops 1000000 | bytes 917632 | tf_op jit(solution)/shard_map/pallas_call | solution.py:44
  (1 shorter events, 0.0 us)
Async XLA Ops:
  19.0 5.5 %collective-permute-start.1 = (bf16[8,4,32,128]{3,2,1,0:T(8,128)(2,1)S(1)}, bf16[8,4,32,128]{3,2,1,0:T(8,128)(2,1)S(1)}, u32[]{:S(2)}, u32[]{:S(2)}) collective-permute-start(bf16[8,4,32,128]{3,2,1,0:T(8,128)(2,1)S(1)} %all_to_all.10.got), channel_id=1, source_target_pairs={{0,1},{1,0},{2,3},{3,2},{4,5},{5,4},{6,7},{7,6},{8,9},{9,8},{10,11... | collective-permute-start | bytes 786440 | tf_op jit(solution)/shard_map/ppermute | solution.py:321
  19.0 5.5 %collective-permute-start = (bf16[32,2048]{1,0:T(8,128)(2,1)S(1)}, bf16[32,2048]{1,0:T(8,128)(2,1)S(1)}, u32[]{:S(2)}, u32[]{:S(2)}) collective-permute-start(bf16[32,2048]{1,0:T(8,128)(2,1)S(1)} %get-tuple-element.29.mine), channel_id=1, source_target_pairs={{0,1},{1,0},{2,3},{3,2},{4,5},{5,4},{6,7},{7,6},{8,9},{9,8},{10,11... | collective-permute-start | bytes 393224 | tf_op jit(solution)/shard_map/ppermute | solution.py:321
  21.2 8.0 %collective-permute-start.3 = (bf16[64,512]{1,0:T(8,128)(2,1)S(1)}, bf16[64,512]{1,0:T(8,128)(2,1)S(1)}, u32[]{:S(2)}, u32[]{:S(2)}) collective-permute-start(bf16[64,512]{1,0:T(8,128)(2,1)S(1)} %get-tuple-element.33), channel_id=1, source_target_pairs={{0,1},{1,0},{2,3},{3,2},{4,5},{5,4},{6,7},{7,6},{8,9},{9,8},{10,11... | collective-permute-start | bytes 196616 | tf_op jit(solution)/shard_map/ppermute | solution.py:321
  21.3 8.0 %collective-permute-start.4 = (bf16[64,512]{1,0:T(8,128)(2,1)S(1)}, bf16[64,512]{1,0:T(8,128)(2,1)S(1)}, u32[]{:S(2)}, u32[]{:S(2)}) collective-permute-start(bf16[64,512]{1,0:T(8,128)(2,1)S(1)} %get-tuple-element.34), channel_id=1, source_target_pairs={{0,2},{1,3},{2,0},{3,1},{4,6},{5,7},{6,4},{7,5},{8,10},{9,11},{10,... | collective-permute-start | bytes 196616 | tf_op jit(solution)/shard_map/ppermute | solution.py:321
  22.8 6.4 %collective-permute-start.5 = (bf16[64,512]{1,0:T(8,128)(2,1)S(1)}, bf16[64,512]{1,0:T(8,128)(2,1)S(1)}, u32[]{:S(2)}, u32[]{:S(2)}) collective-permute-start(bf16[64,512]{1,0:T(8,128)(2,1)S(1)} %get-tuple-element.35), channel_id=1, source_target_pairs={{0,3},{1,2},{2,1},{3,0},{4,7},{5,6},{6,5},{7,4},{8,11},{9,10},{10,... | collective-permute-start | bytes 196616 | tf_op jit(solution)/shard_map/ppermute | solution.py:321
  25.3 4.4 %collective-permute-start.2 = (bf16[64,512]{1,0:T(8,128)(2,1)S(1)}, bf16[64,512]{1,0:T(8,128)(2,1)S(1)}, u32[]{:S(2)}, u32[]{:S(2)}) collective-permute-start(bf16[64,512]{1,0:T(8,128)(2,1)S(1)} %shard_map.81), channel_id=1, source_target_pairs={{0,2},{1,3},{2,0},{3,1},{4,6},{5,7},{6,4},{7,5},{8,10},{9,11},{10,... | collective-permute-start | bytes 196616 | tf_op jit(solution)/shard_map/ppermute | solution.py:321
  28.4 1.3 %copy-start = (bf16[128,256]{1,0:T(8,128)(2,1)S(1)}, bf16[128,256]{1,0:T(8,128)(2,1)}, u32[]{:S(2)}) copy-start(bf16[128,256]{1,0:T(8,128)(2,1)} %w_ref.1) | copy-start | bytes 196612
  30.3 4.3 %collective-permute-start.9 = (bf16[64,512]{1,0:T(8,128)(2,1)S(1)}, bf16[64,512]{1,0:T(8,128)(2,1)S(1)}, u32[]{:S(2)}, u32[]{:S(2)}) collective-permute-start(bf16[64,512]{1,0:T(8,128)(2,1)S(1)} %get-tuple-element.41), channel_id=1, source_target_pairs={{0,2},{1,3},{2,0},{3,1},{4,6},{5,7},{6,4},{7,5},{8,10},{9,11},{10,... | collective-permute-start | bytes 196616 | tf_op jit(solution)/shard_map/ppermute | solution.py:321
  35.4 5.7 %collective-permute-start.11 = (bf16[8,4,32,128]{3,2,1,0:T(8,128)(2,1)S(1)}, bf16[8,4,32,128]{3,2,1,0:T(8,128)(2,1)S(1)}, u32[]{:S(2)}, u32[]{:S(2)}) collective-permute-start(bf16[8,4,32,128]{3,2,1,0:T(8,128)(2,1)S(1)} %get-tuple-element.46), channel_id=1, source_target_pairs={{0,1},{1,0},{2,3},{3,2},{4,5},{5,4},{6,7},{7,6},{8,9},{9,8},{10,11... | collective-permute-start | bytes 786440 | tf_op jit(solution)/shard_map/ppermute | solution.py:321
  35.5 1.6 %collective-permute-start.12 = (f32[64,256]{1,0:T(8,128)S(1)}, f32[64,256]{1,0:T(8,128)S(1)}, u32[]{:S(2)}, u32[]{:S(2)}) collective-permute-start(f32[64,256]{1,0:T(8,128)S(1)} %get-tuple-element.48), channel_id=1, source_target_pairs={{0,1},{1,0},{2,3},{3,2},{4,5},{5,4},{6,7},{7,6},{8,9},{9,8},{10,11... | collective-permute-start | bytes 196616 | tf_op jit(solution)/shard_map/ppermute | solution.py:321
  37.1 4.0 %collective-permute-start.13 = (f32[32,256]{1,0:T(8,128)S(1)}, f32[32,256]{1,0:T(8,128)S(1)}, u32[]{:S(2)}, u32[]{:S(2)}) collective-permute-start(f32[32,256]{1,0:T(8,128)S(1)} %get-tuple-element.50), channel_id=1, source_target_pairs={{0,2},{1,3},{2,0},{3,1},{4,6},{5,7},{6,4},{7,5},{8,10},{9,11},{10,... | collective-permute-start | bytes 98312 | tf_op jit(solution)/shard_map/ppermute | solution.py:321
  41.9 12.9 %all-to-all-start.1 = ((bf16[8,192,128]{2,1,0:T(8,128)(2,1)}), bf16[8,192,128]{2,1,0:T(8,128)(2,1)S(1)}, u32[]{:S(2)}, u32[]{:S(2)}) async-start(bf16[8,192,128]{2,1,0:T(8,128)(2,1)} %shard_map.87), calls=%async_computation.1 | async-start | bytes 786432 | tf_op jit(solution)/shard_map/all_to_all | solution.py:326
  47.0 7.0 %collective-permute-start.10 = (f32[32,2048]{1,0:T(8,128)S(1)}, f32[32,2048]{1,0:T(8,128)S(1)}, u32[]{:S(2)}, u32[]{:S(2)}) collective-permute-start(f32[32,2048]{1,0:T(8,128)S(1)} %get-tuple-element.44), channel_id=1, source_target_pairs={{0,1},{1,0},{2,3},{3,2},{4,5},{5,4},{6,7},{7,6},{8,9},{9,8},{10,11... | collective-permute-start | bytes 786440 | tf_op jit(solution)/shard_map/ppermute | solution.py:321
  47.0 2.0 %collective-permute-start.6 = (bf16[64,512]{1,0:T(8,128)(2,1)S(1)}, bf16[64,512]{1,0:T(8,128)(2,1)S(1)}, u32[]{:S(2)}, u32[]{:S(2)}) collective-permute-start(bf16[64,512]{1,0:T(8,128)(2,1)S(1)} %get-tuple-element.37), channel_id=1, source_target_pairs={{0,1},{1,0},{2,3},{3,2},{4,5},{5,4},{6,7},{7,6},{8,9},{9,8},{10,11... | collective-permute-start | bytes 196616 | tf_op jit(solution)/shard_map/ppermute | solution.py:321
  47.5 4.3 %collective-permute-start.7 = (bf16[64,512]{1,0:T(8,128)(2,1)S(1)}, bf16[64,512]{1,0:T(8,128)(2,1)S(1)}, u32[]{:S(2)}, u32[]{:S(2)}) collective-permute-start(bf16[64,512]{1,0:T(8,128)(2,1)S(1)} %get-tuple-element.38), channel_id=1, source_target_pairs={{0,2},{1,3},{2,0},{3,1},{4,6},{5,7},{6,4},{7,5},{8,10},{9,11},{10,... | collective-permute-start | bytes 196616 | tf_op jit(solution)/shard_map/ppermute | solution.py:321
  49.0 4.3 %collective-permute-start.8 = (bf16[64,512]{1,0:T(8,128)(2,1)S(1)}, bf16[64,512]{1,0:T(8,128)(2,1)S(1)}, u32[]{:S(2)}, u32[]{:S(2)}) collective-permute-start(bf16[64,512]{1,0:T(8,128)(2,1)S(1)} %get-tuple-element.39), channel_id=1, source_target_pairs={{0,3},{1,2},{2,1},{3,0},{4,7},{5,6},{6,5},{7,4},{8,11},{9,10},{10,... | collective-permute-start | bytes 196616 | tf_op jit(solution)/shard_map/ppermute | solution.py:321

commit v7 on v6

--- a/solution.py
+++ b/solution.py
@@ -163,13 +163,13 @@
             left = [table[slot[k + h, lane + t]] for h in range(2)]
             right = [a_side[t, k + h] for h in range(2)]
             part = lax.dot_general(
+                jnp.concatenate(left, axis=1),
                 jnp.concatenate(right, axis=1),
-                jnp.concatenate(left, axis=1),
                 (((1,), (1,)), ((), ())),
                 preferred_element_type=F32,
             )
             acc = part if acc is None else acc + part
-        out[:, t * tile : (t + 1) * tile] = acc.T.astype(BF16)
+        out[:, t * tile : (t + 1) * tile] = acc.astype(BF16)
 
 
 def fetch_near_kernel(side_of, a_hbm, a_side, sems):
@@ -217,7 +217,7 @@
     _, _, x = position()
     f = keep.shape[0]
     keep[...] = mine[rows_at(x, f), :] + came[rows_at(x, f), :]
-    send[...] = mine[rows_at(1 - x, f), :] + came[rows_at(1 - x, f), :]
+    send[...] = (mine[rows_at(1 - x, f), :] + came[rows_at(1 - x, f), :]).astype(BF16)
 
 
 def spread(side_of, slot, a_side, g_ref, acc):
@@ -258,7 +258,7 @@
 
 def total_kernel(stay, came, wg, wg_came, out, packed, sems):
     f, tile = stay.shape[2], stay.shape[3]
-    part = (wg[...] + wg_came[...]).astype(BF16)
+    part = (wg[...] + wg_came[...].astype(F32)).astype(BF16)
     copies = []
     for d in range(stay.shape[0]):
         for o in range(CAP):
@@ -394,7 +394,8 @@
     g_came = mate(g_send, 2)
     wg_part = ((f, units), F32)
     wg_keep, wg_send = call(
-        wg_kernel, [VMEM] * 2, [("vmem", *wg_part)] * 2, [wg_keep, mate(wg_send, 1)]
+        wg_kernel, [VMEM] * 2, [("vmem", *wg_part), ("vmem", wg_part[0], BF16)],
+        [wg_keep, mate(wg_send, 1)],
     )
     wg_came = mate(wg_send, 2)
 

time: 56.1 us -> 56 us (level)
  no operation moved by 1% of the time
where the time goes in v7:
time: 56 us; the launch traced here: 55.7 us
  Pallas kernels  14.9 us (27%)
  starting transfers between devices  14.7 us (26%)
  blocking collectives  14.2 us (25%)
  waiting for transfers between devices  11 us (20%)
  between operations  0.77 us (1%)
    pallas_call x13, Pallas kernels, call(): pl.pallas_call(kernel, out_shape=shapes, in_specs=in_specs, out_specs=spe...  14.9 us
    all_to_all x1, blocking collectives, over_rows(): lax.all_to_all(v, 'rows', 0, 0, tiled=True, axis_index_groups=[order])  14.2 us
    ppermute x14, waiting for transfers between devices, mate(): return lax.ppermute(v, 'cols', [(i, i ^ q) for i in range(cols_n)])  10.2 us
    ppermute x14, starting transfers between devices, mate(): return lax.ppermute(v, 'cols', [(i, i ^ q) for i in range(cols_n)])  9.68 us
    all_to_all x1, starting transfers between devices, over_rows(): lax.all_to_all(v, 'rows', 0, 0, tiled=True, axis_index_groups=[order])  5.07 us
  transfers between devices with their start and end apart: 15, of which 7 were waited for; matrix products, arithmetic and copies ran while one was open for 0% of the time, Pallas kernels for 14%

profile of v7, /device:TPU:0, one launch (start us, length us, event | category | flops | bytes accessed | tf_op | source)
XLA Modules:
  0.0 55.7 jit_solution(16819276383371125547)
XLA Ops:
  0.6 4.1 %shard_map.76 = (s32[4,8]{1,0:T(4,128)S(4)}, bf16[32,2048]{1,0:T(8,128)(2,1)S(1)}, s32[16,128]{1,0:T(8,128)S(1)}, bf16[8,4,32,128]{3,2,1,0:T(8,128)(2,1)S(1)}) custom-call(s32[16,128]{1,0:T(8,128)} %bitcast.1, bf16[32,2048]{1,0:T(8,128)(2,1)} %feats.1), custom_call_target="tpu_custom_call" | custom-call | flops 1000000 | bytes 139264 | tf_op jit(solution)/shard_map/pallas_call | solution.py:44
  4.7 14.2 %all_to_all.10.got = bf16[8,4,32,128]{3,2,1,0:T(8,128)(2,1)S(1)} all-to-all(bf16[8,4,32,128]{3,2,1,0:T(8,128)(2,1)S(1)} %get-tuple-element.30), channel_id=1, replica_groups={{16,12,24,4,28,0,20,8},{17,13,25,5,29,1,21,9},{18,14,26,6,30,2,22,10},{..., dimensions={0} | all-to-all | bytes 524288 | tf_op jit(solution)/shard_map/all_to_all | solution.py:326
  19.0 0.0 collective-permute-start.1
  19.0 0.5 collective-permute-start
  19.5 1.7 %shard_map.80 = (bf16[4,16,128,128]{3,2,1,0:T(8,128)(2,1)S(1)}, bf16[64,512]{1,0:T(8,128)(2,1)S(1)}, bf16[64,512]{1,0:T(8,128)(2,1)S(1)}, bf16[64,512]{1,0:T(8,128)(2,1)S(1)}, bf16[64,512]{1,0:T(8,128)(2,1)S(1)}) custom-call(bf16[16,16,128,128]{3,2,1,0:T(8,128)(2,1)} %a_hbm.3, bf16[64,2048]{1,0:T(8,128)(2,1)} %cot.1), custom_call_target="tpu_custom_call" | custom-call | flops 1000000 | bytes 8650752 | tf_op jit(solution)/shard_map/pallas_call | solution.py:44
  21.2 0.1 collective-permute-start.3
  21.3 1.6 %collective-permute-start.4 = (bf16[64,512]{1,0:T(8,128)(2,1)S(1)}, bf16[64,512]{1,0:T(8,128)(2,1)S(1)}, u32[]{:S(2)}, u32[]{:S(2)}) collective-permute-start(bf16[64,512]{1,0:T(8,128)(2,1)S(1)} %get-tuple-element.34), channel_id=1, source_target_pairs={{0,2},{1,3},{2,0},{3,1},{4,6},{5,7},{6,4},{7,5},{8,10},{9,11},{10,... | collective-permute-start | bytes 196616 | tf_op jit(solution)/shard_map/ppermute | solution.py:321
  22.8 0.3 collective-permute-start.5
  23.1 1.3 %shard_map.77.slot = s32[16,128]{1,0:T(8,128)S(4)} custom-call(s32[16,128]{1,0:T(8,128)S(1)} %get-tuple-element.28.adj_ref), custom_call_target="tpu_custom_call" | custom-call | flops 1000000 | bytes 8192 | tf_op jit(solution)/shard_map/pallas_call | solution.py:44
  24.4 0.0 collective-permute-done.mate
  24.4 0.0 collective-permute-done.1.got_mate
  24.4 0.9 %shard_map.81 = bf16[64,512]{1,0:T(8,128)(2,1)S(1)} custom-call(s32[16,128]{1,0:T(8,128)S(4)} %shard_map.77.slot, bf16[4,16,128,128]{3,2,1,0:T(8,128)(2,1)S(1)} %get-tuple-element.31.a_side, bf16[32,2048]{1,0:T(8,128)(2,1)S(1)} %get-tuple-element.29.mine, bf16[32,2048]{1,0:T(8,128)(2,1)S(1)} %collective-permute-done.mate, ...), custom_call_target="tpu_custom_call" | custom-call | flops 134217728 | bytes 2891776 | tf_op jit(solution)/shard_map/pallas_call | solution.py:44
  25.3 1.6 %collective-permute-start.2 = (bf16[64,512]{1,0:T(8,128)(2,1)S(1)}, bf16[64,512]{1,0:T(8,128)(2,1)S(1)}, u32[]{:S(2)}, u32[]{:S(2)}) collective-permute-start(bf16[64,512]{1,0:T(8,128)(2,1)S(1)} %shard_map.81), channel_id=1, source_target_pairs={{0,2},{1,3},{2,0},{3,1},{4,6},{5,7},{6,4},{7,5},{8,10},{9,11},{10,... | collective-permute-start | bytes 196616 | tf_op jit(solution)/shard_map/ppermute | solution.py:321
  26.9 1.5 %shard_map.78.a_side = bf16[4,16,128,128]{3,2,1,0:T(8,128)(2,1)S(1)} custom-call(bf16[16,16,128,128]{3,2,1,0:T(8,128)(2,1)} %a_hbm.3), custom_call_target="tpu_custom_call" | custom-call | flops 1000000 | bytes 8388608 | tf_op jit(solution)/shard_map/pallas_call | solution.py:44
  28.4 0.0 copy-start
  28.5 0.9 %shard_map.79.keep = bf16[64,512]{1,0:T(8,128)(2,1)S(1)} custom-call(s32[16,128]{1,0:T(8,128)S(4)} %shard_map.77.slot, bf16[4,16,128,128]{3,2,1,0:T(8,128)(2,1)S(1)} %shard_map.78.a_side, bf16[32,2048]{1,0:T(8,128)(2,1)S(1)} %get-tuple-element.29.mine, bf16[32,2048]{1,0:T(8,128)(2,1)S(1)} %collective-permute-done.mate, ...), custom_call_target="tpu_custom_call" | custom-call | flops 134217728 | bytes 2891776 | tf_op jit(solution)/shard_map/pallas_call | solution.py:44
  29.3 0.0 collective-permute-done.3.c1
  29.4 0.0 collective-permute-done.4.c2
  29.4 0.0 collective-permute-done.5.c3
  29.4 0.4 collective-permute-done.2.came
  29.8 0.0 copy-done
  29.8 0.6 %shard_map.82 = (bf16[64,512]{1,0:T(8,128)(2,1)S(1)}, bf16[64,512]{1,0:T(8,128)(2,1)S(1)}, bf16[64,512]{1,0:T(8,128)(2,1)S(1)}, bf16[64,512]{1,0:T(8,128)(2,1)S(...) custom-call(bf16[64,512]{1,0:T(8,128)(2,1)S(1)} %shard_map.79.keep, ...), custom_call_target="tpu_custom_call" | custom-call | flops 100663296 | bytes 458752 | tf_op jit(solution)/shard_map/pallas_call | solution.py:44
  30.4 1.6 %collective-permute-start.9 = (bf16[64,512]{1,0:T(8,128)(2,1)S(1)}, bf16[64,512]{1,0:T(8,128)(2,1)S(1)}, u32[]{:S(2)}, u32[]{:S(2)}) collective-permute-start(bf16[64,512]{1,0:T(8,128)(2,1)S(1)} %get-tuple-element.41), channel_id=1, source_target_pairs={{0,2},{1,3},{2,0},{3,1},{4,6},{5,7},{6,4},{7,5},{8,10},{9,11},{10,... | collective-permute-start | bytes 196616 | tf_op jit(solution)/shard_map/ppermute | solution.py:321
  31.9 0.6 %shard_map.84.before = f32[48,64,128]{2,1,0:T(8,128)S(1)} custom-call(s32[16,128]{1,0:T(8,128)S(4)} %shard_map.77.slot, bf16[4,16,128,128]{3,2,1,0:T(8,128)(2,1)S(1)} %shard_map.78.a_side, bf16[64,512]{1,0:T(8,128)(2,1)S(1)} %get-tuple-element.42.g_ref), custom_call_target="tpu_custom_call" | custom-call | flops 134217728 | bytes 2170880 | tf_op jit(solution)/shard_map/pallas_call | solution.py:44
  32.5 2.2 %collective-permute-done.9.g_ref = bf16[64,512]{1,0:T(8,128)(2,1)S(1)} collective-permute-done((bf16[64,512]{1,0:T(8,128)(2,1)S(1)}, bf16[64,512]{1,0:T(8,128)(2,1)S(1)}, u32[]{:S(2)}, u32[]{:S(2)}) %collective-permute-start.9) | collective-permute-done | bytes 65568 | tf_op jit(solution)/shard_map/ppermute | solution.py:321
  34.7 0.7 %shard_map.85 = (f32[32,2048]{1,0:T(8,128)S(1)}, f32[32,2048]{1,0:T(8,128)S(1)}, f32[8,4,32,128]{3,2,1,0:T(8,128)S(1)}, bf16[8,4,32,128]{3,2,1,0:T(8,128)(2,1)S(1)}) custom-call(s32[16,128]{1,0:T(8,128)S(4)} %shard_map.77.slot, bf16[4,16,128,128]{3,2,1,0:T(8,128)(2,1)S(1)} %get-tuple-element.31.a_side, bf16[64,512]{1,0:T(8,128)(2,1)S(1)} %collective-permute-done.9.g_ref, ...), custom_call_target="tpu_custom_call" | custom-call | flops 134217728 | bytes 3743744 | tf_op jit(solution)/shard_map/pallas_call | solution.py:44
  35.4 0.1 collective-permute-start.11
  35.5 0.5 collective-permute-start.12
  36.0 1.1 %collective-permute-done.12.came = f32[64,256]{1,0:T(8,128)S(1)} collective-permute-done((f32[64,256]{1,0:T(8,128)S(1)}, f32[64,256]{1,0:T(8,128)S(1)}, u32[]{:S(2)}, u32[]{:S(2)}) %collective-permute-start.12) | collective-permute-done | bytes 65568 | tf_op jit(solution)/shard_map/ppermute | solution.py:321
  37.1 1.6 %collective-permute-start.13 = (bf16[32,256]{1,0:T(8,128)(2,1)S(1)}, bf16[32,256]{1,0:T(8,128)(2,1)S(1)}, u32[]{:S(2)}, u32[]{:S(2)}) collective-permute-start(bf16[32,256]{1,0:T(8,128)(2,1)S(1)} %get-tuple-element.50), channel_id=1, source_target_pairs={{0,2},{1,3},{2,0},{3,1},{4,6},{5,7},{6,4},{7,5},{8,10},{9,11},{10,... | collective-permute-start | bytes 49160 | tf_op jit(solution)/shard_map/ppermute | solution.py:321
  38.7 2.2 %collective-permute-done.13.wg_came = bf16[32,256]{1,0:T(8,128)(2,1)S(1)} collective-permute-done((bf16[32,256]{1,0:T(8,128)(2,1)S(1)}, bf16[32,256]{1,0:T(8,128)(2,1)S(1)}, u32[]{:S(2)}, u32[]{:S(2)}) %collective-permute-start.13) | collective-permute-done | bytes 16416 | tf_op jit(solution)/shard_map/ppermute | solution.py:321
  40.9 0.0 collective-permute-done.11.came
  40.9 0.8 %shard_map.87 = bf16[8,192,128]{2,1,0:T(8,128)(2,1)} custom-call(f32[8,4,32,128]{3,2,1,0:T(8,128)S(1)} %get-tuple-element.45.stay, bf16[8,4,32,128]{3,2,1,0:T(8,128)(2,1)S(1)} %collective-permute-done.11.came, f32[32,256]{1,0:T(8,128)S(1)} %get-tuple-element.49.wg, bf16[32,256]{1,0:T(8,128)(2,1)S(1)} %collective-permute-done.13.wg_came), custom_call_target="tpu_custom_call" | custom-call | flops 1000000 | bytes 835584 | tf_op jit(solution)/shard_map/pallas_call | solution.py:44
  41.8 5.1 %all-to-all-start.1 = ((bf16[8,192,128]{2,1,0:T(8,128)(2,1)}), bf16[8,192,128]{2,1,0:T(8,128)(2,1)S(1)}, u32[]{:S(2)}, u32[]{:S(2)}) async-start(bf16[8,192,128]{2,1,0:T(8,128)(2,1)} %shard_map.87), calls=%async_computation.1 | async-start | bytes 786432 | tf_op jit(solution)/shard_map/all_to_all | solution.py:326
  46.9 0.0 collective-permute-start.10
  46.9 0.5 collective-permute-start.6
  47.4 1.5 %collective-permute-start.7 = (bf16[64,512]{1,0:T(8,128)(2,1)S(1)}, bf16[64,512]{1,0:T(8,128)(2,1)S(1)}, u32[]{:S(2)}, u32[]{:S(2)}) collective-permute-start(bf16[64,512]{1,0:T(8,128)(2,1)S(1)} %get-tuple-element.38), channel_id=1, source_target_pairs={{0,2},{1,3},{2,0},{3,1},{4,6},{5,7},{6,4},{7,5},{8,10},{9,11},{10,... | collective-permute-start | bytes 196616 | tf_op jit(solution)/shard_map/ppermute | solution.py:321
  48.9 0.0 collective-permute-start.8
  48.9 0.0 collective-permute-done.6.p1
  48.9 2.8 %collective-permute-done.7.p2 = bf16[64,512]{1,0:T(8,128)(2,1)S(1)} collective-permute-done((bf16[64,512]{1,0:T(8,128)(2,1)S(1)}, bf16[64,512]{1,0:T(8,128)(2,1)S(1)}, u32[]{:S(2)}, u32[]{:S(2)}) %collective-permute-start.7) | collective-permute-done | bytes 65568 | tf_op jit(solution)/shard_map/ppermute | solution.py:321
  51.6 1.5 %collective-permute-done.8.p3 = bf16[64,512]{1,0:T(8,128)(2,1)S(1)} collective-permute-done((bf16[64,512]{1,0:T(8,128)(2,1)S(1)}, bf16[64,512]{1,0:T(8,128)(2,1)S(1)}, u32[]{:S(2)}, u32[]{:S(2)}) %collective-permute-start.8) | collective-permute-done | bytes 65568 | tf_op jit(solution)/shard_map/ppermute | solution.py:321
  53.2 0.7 %shard_map.83 = bf16[64,2048]{1,0:T(8,128)(2,1)} custom-call(bf16[64,512]{1,0:T(8,128)(2,1)S(1)} %get-tuple-element.36.p0, bf16[64,512]{1,0:T(8,128)(2,1)S(1)} %collective-permute-done.6.p1, bf16[64,512]{1,0:T(8,128)(2,1)S(1)} %collective-permute-done.7.p2, bf16[64,512]{1,0:T(8,128)(2,1)S(1)} %collective-permute-done.8.p3), custom_call_target="tpu_custom_call" | custom-call | flops 1000000 | bytes 262144 | tf_op jit(solution)/shard_map/pallas_call | solution.py:44
  53.9 0.0 collective-permute-done.10.came
  53.9 0.8 %all-to-all-done.1.back = bf16[8,192,128]{2,1,0:T(8,128)(2,1)S(1)} async-done(((bf16[8,192,128]{2,1,0:T(8,128)(2,1)}), bf16[8,192,128]{2,1,0:T(8,128)(2,1)S(1)}, u32[]{:S(2)}, u32[]{:S(2)}) %all-to-all-start.1) | async-done | bytes 393248 | tf_op jit(solution)/shard_map/all_to_all | solution.py:326
  54.7 1.0 %shard_map.88 = (f32[32,2048]{1,0:T(8,128)}, f32[32,256]{1,0:T(8,128)}) custom-call(s32[4,8]{1,0:T(4,128)S(4)} %get-tuple-element.40.sel, f32[32,2048]{1,0:T(8,128)S(1)} %get-tuple-element.43.own, f32[32,2048]{1,0:T(8,128)S(1)} %collective-permute-done.10.came, bf16[8,192,128]{2,1,0:T(8,128)(2,1)S(1)} %all-to-all-done.1.back), custom_call_target="tpu_custom_call" | custom-call | flops 1000000 | bytes 917632 | tf_op jit(solution)/shard_map/pallas_call | solution.py:44
  (1 shorter events, 0.0 us)
Async XLA Ops:
  19.0 5.5 %collective-permute-start.1 = (bf16[8,4,32,128]{3,2,1,0:T(8,128)(2,1)S(1)}, bf16[8,4,32,128]{3,2,1,0:T(8,128)(2,1)S(1)}, u32[]{:S(2)}, u32[]{:S(2)}) collective-permute-start(bf16[8,4,32,128]{3,2,1,0:T(8,128)(2,1)S(1)} %all_to_all.10.got), channel_id=1, source_target_pairs={{0,1},{1,0},{2,3},{3,2},{4,5},{5,4},{6,7},{7,6},{8,9},{9,8},{10,11... | collective-permute-start | bytes 786440 | tf_op jit(solution)/shard_map/ppermute | solution.py:321
  19.0 5.5 %collective-permute-start = (bf16[32,2048]{1,0:T(8,128)(2,1)S(1)}, bf16[32,2048]{1,0:T(8,128)(2,1)S(1)}, u32[]{:S(2)}, u32[]{:S(2)}) collective-permute-start(bf16[32,2048]{1,0:T(8,128)(2,1)S(1)} %get-tuple-element.29.mine), channel_id=1, source_target_pairs={{0,1},{1,0},{2,3},{3,2},{4,5},{5,4},{6,7},{7,6},{8,9},{9,8},{10,11... | collective-permute-start | bytes 393224 | tf_op jit(solution)/shard_map/ppermute | solution.py:321
  21.2 8.1 %collective-permute-start.3 = (bf16[64,512]{1,0:T(8,128)(2,1)S(1)}, bf16[64,512]{1,0:T(8,128)(2,1)S(1)}, u32[]{:S(2)}, u32[]{:S(2)}) collective-permute-start(bf16[64,512]{1,0:T(8,128)(2,1)S(1)} %get-tuple-element.33), channel_id=1, source_target_pairs={{0,1},{1,0},{2,3},{3,2},{4,5},{5,4},{6,7},{7,6},{8,9},{9,8},{10,11... | collective-permute-start | bytes 196616 | tf_op jit(solution)/shard_map/ppermute | solution.py:321
  21.3 8.1 %collective-permute-start.4 = (bf16[64,512]{1,0:T(8,128)(2,1)S(1)}, bf16[64,512]{1,0:T(8,128)(2,1)S(1)}, u32[]{:S(2)}, u32[]{:S(2)}) collective-permute-start(bf16[64,512]{1,0:T(8,128)(2,1)S(1)} %get-tuple-element.34), channel_id=1, source_target_pairs={{0,2},{1,3},{2,0},{3,1},{4,6},{5,7},{6,4},{7,5},{8,10},{9,11},{10,... | collective-permute-start | bytes 196616 | tf_op jit(solution)/shard_map/ppermute | solution.py:321
  22.8 6.5 %collective-permute-start.5 = (bf16[64,512]{1,0:T(8,128)(2,1)S(1)}, bf16[64,512]{1,0:T(8,128)(2,1)S(1)}, u32[]{:S(2)}, u32[]{:S(2)}) collective-permute-start(bf16[64,512]{1,0:T(8,128)(2,1)S(1)} %get-tuple-element.35), channel_id=1, source_target_pairs={{0,3},{1,2},{2,1},{3,0},{4,7},{5,6},{6,5},{7,4},{8,11},{9,10},{10,... | collective-permute-start | bytes 196616 | tf_op jit(solution)/shard_map/ppermute | solution.py:321
  25.3 4.4 %collective-permute-start.2 = (bf16[64,512]{1,0:T(8,128)(2,1)S(1)}, bf16[64,512]{1,0:T(8,128)(2,1)S(1)}, u32[]{:S(2)}, u32[]{:S(2)}) collective-permute-start(bf16[64,512]{1,0:T(8,128)(2,1)S(1)} %shard_map.81), channel_id=1, source_target_pairs={{0,2},{1,3},{2,0},{3,1},{4,6},{5,7},{6,4},{7,5},{8,10},{9,11},{10,... | collective-permute-start | bytes 196616 | tf_op jit(solution)/shard_map/ppermute | solution.py:321
  28.4 1.3 %copy-start = (bf16[128,256]{1,0:T(8,128)(2,1)S(1)}, bf16[128,256]{1,0:T(8,128)(2,1)}, u32[]{:S(2)}) copy-start(bf16[128,256]{1,0:T(8,128)(2,1)} %w_ref.1) | copy-start | bytes 196612
  30.4 4.3 %collective-permute-start.9 = (bf16[64,512]{1,0:T(8,128)(2,1)S(1)}, bf16[64,512]{1,0:T(8,128)(2,1)S(1)}, u32[]{:S(2)}, u32[]{:S(2)}) collective-permute-start(bf16[64,512]{1,0:T(8,128)(2,1)S(1)} %get-tuple-element.41), channel_id=1, source_target_pairs={{0,2},{1,3},{2,0},{3,1},{4,6},{5,7},{6,4},{7,5},{8,10},{9,11},{10,... | collective-permute-start | bytes 196616 | tf_op jit(solution)/shard_map/ppermute | solution.py:321
  35.4 5.5 %collective-permute-start.11 = (bf16[8,4,32,128]{3,2,1,0:T(8,128)(2,1)S(1)}, bf16[8,4,32,128]{3,2,1,0:T(8,128)(2,1)S(1)}, u32[]{:S(2)}, u32[]{:S(2)}) collective-permute-start(bf16[8,4,32,128]{3,2,1,0:T(8,128)(2,1)S(1)} %get-tuple-element.46), channel_id=1, source_target_pairs={{0,1},{1,0},{2,3},{3,2},{4,5},{5,4},{6,7},{7,6},{8,9},{9,8},{10,11... | collective-permute-start | bytes 786440 | tf_op jit(solution)/shard_map/ppermute | solution.py:321
  35.5 1.6 %collective-permute-start.12 = (f32[64,256]{1,0:T(8,128)S(1)}, f32[64,256]{1,0:T(8,128)S(1)}, u32[]{:S(2)}, u32[]{:S(2)}) collective-permute-start(f32[64,256]{1,0:T(8,128)S(1)} %get-tuple-element.48), channel_id=1, source_target_pairs={{0,1},{1,0},{2,3},{3,2},{4,5},{5,4},{6,7},{7,6},{8,9},{9,8},{10,11... | collective-permute-start | bytes 196616 | tf_op jit(solution)/shard_map/ppermute | solution.py:321
  37.1 3.8 %collective-permute-start.13 = (bf16[32,256]{1,0:T(8,128)(2,1)S(1)}, bf16[32,256]{1,0:T(8,128)(2,1)S(1)}, u32[]{:S(2)}, u32[]{:S(2)}) collective-permute-start(bf16[32,256]{1,0:T(8,128)(2,1)S(1)} %get-tuple-element.50), channel_id=1, source_target_pairs={{0,2},{1,3},{2,0},{3,1},{4,6},{5,7},{6,4},{7,5},{8,10},{9,11},{10,... | collective-permute-start | bytes 49160 | tf_op jit(solution)/shard_map/ppermute | solution.py:321
  41.8 12.9 %all-to-all-start.1 = ((bf16[8,192,128]{2,1,0:T(8,128)(2,1)}), bf16[8,192,128]{2,1,0:T(8,128)(2,1)S(1)}, u32[]{:S(2)}, u32[]{:S(2)}) async-start(bf16[8,192,128]{2,1,0:T(8,128)(2,1)} %shard_map.87), calls=%async_computation.1 | async-start | bytes 786432 | tf_op jit(solution)/shard_map/all_to_all | solution.py:326
  46.9 7.0 %collective-permute-start.10 = (f32[32,2048]{1,0:T(8,128)S(1)}, f32[32,2048]{1,0:T(8,128)S(1)}, u32[]{:S(2)}, u32[]{:S(2)}) collective-permute-start(f32[32,2048]{1,0:T(8,128)S(1)} %get-tuple-element.44), channel_id=1, source_target_pairs={{0,1},{1,0},{2,3},{3,2},{4,5},{5,4},{6,7},{7,6},{8,9},{9,8},{10,11... | collective-permute-start | bytes 786440 | tf_op jit(solution)/shard_map/ppermute | solution.py:321
  46.9 2.0 %collective-permute-start.6 = (bf16[64,512]{1,0:T(8,128)(2,1)S(1)}, bf16[64,512]{1,0:T(8,128)(2,1)S(1)}, u32[]{:S(2)}, u32[]{:S(2)}) collective-permute-start(bf16[64,512]{1,0:T(8,128)(2,1)S(1)} %get-tuple-element.37), channel_id=1, source_target_pairs={{0,1},{1,0},{2,3},{3,2},{4,5},{5,4},{6,7},{7,6},{8,9},{9,8},{10,11... | collective-permute-start | bytes 196616 | tf_op jit(solution)/shard_map/ppermute | solution.py:321
  47.4 4.3 %collective-permute-start.7 = (bf16[64,512]{1,0:T(8,128)(2,1)S(1)}, bf16[64,512]{1,0:T(8,128)(2,1)S(1)}, u32[]{:S(2)}, u32[]{:S(2)}) collective-permute-start(bf16[64,512]{1,0:T(8,128)(2,1)S(1)} %get-tuple-element.38), channel_id=1, source_target_pairs={{0,2},{1,3},{2,0},{3,1},{4,6},{5,7},{6,4},{7,5},{8,10},{9,11},{10,... | collective-permute-start | bytes 196616 | tf_op jit(solution)/shard_map/ppermute | solution.py:321
  48.9 4.3 %collective-permute-start.8 = (bf16[64,512]{1,0:T(8,128)(2,1)S(1)}, bf16[64,512]{1,0:T(8,128)(2,1)S(1)}, u32[]{:S(2)}, u32[]{:S(2)}) collective-permute-start(bf16[64,512]{1,0:T(8,128)(2,1)S(1)} %get-tuple-element.39), channel_id=1, source_target_pairs={{0,3},{1,2},{2,1},{3,0},{4,7},{5,6},{6,5},{7,4},{8,11},{9,10},{10,... | collective-permute-start | bytes 196616 | tf_op jit(solution)/shard_map/ppermute | solution.py:321
